TPU v7x, 32 devices: a whole 2x2x4 slice. The times are simulated.
32 devices in a mesh: wide: 8 (over z, x), narrow: 4 (over y, core).
Axes of the slice: x: 2, y: 2, z: 4, core: 2. Of those that a mesh axis runs over, the one named last changes fastest.
Arguments:
- hidden_in: bfloat16 [16384, 768], P(('wide', 'narrow')), may hold values from -6 to 6
- out_grad: bfloat16 [16384, 768], P(('wide', 'narrow')), may hold values from -6 to 6
- pair_lengths: int32 [32, 4], P(('wide', 'narrow')), may hold values from 1 to 256, 512 in all within a row
- params: float32 [4, 1772544], P('narrow', 'wide'), may hold values from -4 to 4, as said below
- momentum: float32 [4, 1772544], P('narrow', 'wide'), may hold values from -2 to 2, as said below
- average: float32 [4, 1772544], P('narrow', 'wide'), may hold values from -4 to 4, as said below
Outputs:
- block_out: bfloat16 [16384, 768], P(('wide', 'narrow'))
- in_grad: float32 [16384, 768], P(('wide', 'narrow'))
- grads: float32 [4, 1772544], P('narrow', 'wide')
- new_params: float32 [4, 1772544], P('narrow', 'wide')
- new_momentum: float32 [4, 1772544], P('narrow', 'wide')
- new_average: float32 [4, 1772544], P('narrow', 'wide')
- params_bf16: bfloat16 [4, 1772544], P('narrow', 'wide')
Inputs may be any that keep to these rules, and one draw needn't show every extreme that they name: `pair_lengths`: each row's 4 lengths sum to 512, and some pair of each row has exactly 256 tokens. `params`: independent entries. `momentum`: independent entries. `average`: independent entries.
All inputs are finite; a program needn't handle non-finite values.
Results may differ from a plain program's by a relative error of at most 0.015.
Values may be sent and summed in bfloat16 or wider, within the bound.
No kernel may reach another device: no remote copies, remote signals or barrier semaphores. Data moves between devices by JAX's collectives and lax.ppermute only.
A program may use at most 128 MiB of HBM per device.

v0:
```python
import math

import jax
import jax.numpy as jnp
from jax import lax
from jax.sharding import PartitionSpec as P

D = 768
HEADS = 12
FF = 3072
HD = 64
BUCKETS = 256
L = 512


HIGHEST = lax.Precision.HIGHEST


def unpack_rank(flat_rank, ranks):
    width_part = D // ranks
    extents = [
        (D, 3, width_part),
        (width_part, D),
        (D, FF // ranks),
        (FF // ranks, D),
        (2, width_part),
        (FF // ranks,),
        (BUCKETS, HEADS // ranks),
        (6 * D // ranks,),
    ]
    pieces = []
    offset = 0
    for extent in extents:
        amount = math.prod(extent)
        pieces.append(lax.slice_in_dim(flat_rank, offset, offset + amount).reshape(extent))
        offset += amount
    return pieces


def packing(row_lengths):
    pair_ends = jnp.cumsum(row_lengths)
    position = jnp.arange(L, dtype=jnp.int32)
    segment = jnp.sum((position[:, None] >= pair_ends[None, :]).astype(jnp.int32), axis=1)
    return segment[:, None] == segment[None, :]


def offset_onehot():
    offsets = jnp.arange(2 * L + 1, dtype=jnp.int32) - L
    bucket = jnp.clip(offsets + BUCKETS // 2, 0, BUCKETS - 1)
    return (bucket[:, None] == jnp.arange(BUCKETS, dtype=jnp.int32)[None, :]).astype(jnp.float32)


def expand_bias(bias_table, onehot_table):
    head_count = bias_table.shape[1]
    by_offset = jnp.dot(onehot_table, bias_table.astype(jnp.float32), precision=HIGHEST)
    rolled = jnp.roll(by_offset, -L, axis=0).T
    tiled_rows = jnp.tile(rolled, (1, L))[:, : 2 * L * L]
    return tiled_rows.reshape(head_count, L, 2 * L)[:, :, :L]


def diag_sums(score_grid):
    head_count = score_grid.shape[0]
    padded = jnp.concatenate([jnp.zeros_like(score_grid), score_grid], axis=2).reshape(
        head_count, 2 * L * L
    )
    padded = jnp.concatenate([padded, jnp.zeros((head_count, L), jnp.float32)], axis=1)
    return jnp.sum(padded.reshape(head_count, L, 2 * L + 1), axis=1)


def split_heads(qkv_row):
    width_part = qkv_row.shape[1] // 3
    head_count = width_part // HD
    query_heads = qkv_row[:, :width_part].reshape(L, head_count, HD)
    key_heads = qkv_row[:, width_part : 2 * width_part].reshape(L, head_count, HD)
    value_heads = qkv_row[:, 2 * width_part :].reshape(L, head_count, HD)
    return (query_heads, key_heads, value_heads)


def masked_logits(query_heads, key_heads, row_lengths, bias_grid):
    head_scale = 1.0 / math.sqrt(HD)
    logits = (
        jnp.einsum("ihd,jhd->hij", query_heads, key_heads, preferred_element_type=jnp.float32)
        * head_scale
        + bias_grid
    )
    return jnp.where(packing(row_lengths)[None], logits, -1000000000.0)


def attend_forward(qkv_row, row_lengths, bias_grid):
    query_heads, key_heads, value_heads = split_heads(qkv_row)
    logits = masked_logits(query_heads, key_heads, row_lengths, bias_grid)
    row_max = jnp.max(logits, axis=-1)
    exponent = jnp.exp(logits - row_max[..., None])
    row_total = jnp.sum(exponent, axis=-1)
    attn_probs = exponent / row_total[..., None]
    mixed_heads = jnp.einsum(
        "hij,jhd->ihd",
        attn_probs.astype(jnp.bfloat16),
        value_heads,
        preferred_element_type=jnp.float32,
    )
    return (mixed_heads.reshape(L, -1), row_max + jnp.log(row_total))


def attend_backward(qkv_row, row_lengths, log_total, grad_row, bias_grid):
    head_scale = 1.0 / math.sqrt(HD)
    query_heads, key_heads, value_heads = split_heads(qkv_row)
    logits = masked_logits(query_heads, key_heads, row_lengths, bias_grid)
    attn_probs = jnp.exp(logits - log_total[..., None])
    grad_heads = grad_row.reshape(L, -1, HD)
    grad_probs = jnp.einsum(
        "ihd,jhd->hij", grad_heads, value_heads, preferred_element_type=jnp.float32
    )
    grad_values = jnp.einsum(
        "hij,ihd->jhd",
        attn_probs.astype(jnp.bfloat16),
        grad_heads,
        preferred_element_type=jnp.float32,
    )
    row_dot = jnp.sum(attn_probs * grad_probs, axis=-1, keepdims=True)
    grad_logits = (attn_probs * (grad_probs - row_dot)).astype(jnp.bfloat16)
    grad_query = (
        jnp.einsum("hij,jhd->ihd", grad_logits, key_heads, preferred_element_type=jnp.float32)
        * head_scale
    )
    grad_keys = (
        jnp.einsum("hij,ihd->jhd", grad_logits, query_heads, preferred_element_type=jnp.float32)
        * head_scale
    )
    grad_qkv = jnp.concatenate(
        [grad_query.reshape(L, -1), grad_keys.reshape(L, -1), grad_values.reshape(L, -1)], axis=1
    )
    return (grad_qkv, diag_sums(grad_logits.astype(jnp.float32)))


def normalize(values):
    centred = values - jnp.mean(values, axis=-1, keepdims=True)
    inv_scale = lax.rsqrt(jnp.mean(centred * centred, axis=-1, keepdims=True) + 1e-05)
    return (centred * inv_scale, inv_scale)


def norm_backward(grad_normed, normed, inv_scale):
    return inv_scale * (
        grad_normed
        - jnp.mean(grad_normed, axis=-1, keepdims=True)
        - normed * jnp.mean(grad_normed * normed, axis=-1, keepdims=True)
    )


def gelu_exact(values):
    return 0.5 * values * (1.0 + lax.erf(values * (1.0 / math.sqrt(2.0))))


def gelu_slope(values):
    return 0.5 * (1.0 + lax.erf(values * (1.0 / math.sqrt(2.0)))) + values * jnp.exp(
        -0.5 * values * values
    ) * (1.0 / math.sqrt(2.0 * math.pi))


def body(hidden_in, out_grad, pair_lengths, params, momentum, average):
    ranks = lax.axis_size("narrow")
    width_part = D // ranks
    tok_rows = hidden_in.shape[0]
    gathered = lax.all_gather(params.astype(jnp.bfloat16), "wide", axis=1, tiled=True)
    w_qkv, w_out, w_up, w_down, qv_bias, up_bias, bias_table, vec_piece = unpack_rank(
        gathered[0], ranks
    )
    group_in, vec_all = (
        lax.all_gather(hidden_in, "narrow", axis=0, tiled=True),
        lax.all_gather(vec_piece.reshape(1, -1), "narrow", axis=0, tiled=True),
    )
    group_lengths = lax.all_gather(pair_lengths, "narrow", axis=0, tiled=True)
    vector_rows = vec_all.reshape(6, D).astype(jnp.float32)
    onehot_table = offset_onehot()
    bias_grid = expand_bias(bias_table, onehot_table)
    qv_rows = qv_bias.astype(jnp.float32)
    qkv_bias = jnp.concatenate([qv_rows[0], jnp.zeros((width_part,), jnp.float32), qv_rows[1]])
    w_qkv_flat = w_qkv.reshape(D, 3 * width_part)
    qkv_loc = (jnp.dot(group_in, w_qkv_flat, preferred_element_type=jnp.float32) + qkv_bias).astype(
        jnp.bfloat16
    )
    row_blocks = qkv_loc.reshape(-1, L, 3 * width_part)
    mixed_rows, log_totals = lax.map(
        lambda element: attend_forward(element[0], element[1], bias_grid),
        (row_blocks, group_lengths),
    )
    mixed_loc = mixed_rows.reshape(-1, width_part).astype(jnp.bfloat16)
    attn_out = (
        lax.psum_scatter(
            jnp.dot(mixed_loc, w_out, preferred_element_type=jnp.float32),
            "narrow",
            scatter_dimension=0,
            tiled=True,
        )
        + vector_rows[0]
    )
    first_normed, first_scale = normalize(hidden_in.astype(jnp.float32) + attn_out)
    first_norm = first_normed * vector_rows[2] + vector_rows[3]
    first_low = first_norm.astype(jnp.bfloat16)
    first_group = lax.all_gather(first_low, "narrow", axis=0, tiled=True)
    up_proj = jnp.dot(first_group, w_up, preferred_element_type=jnp.float32) + up_bias.astype(
        jnp.float32
    )
    activated = gelu_exact(up_proj).astype(jnp.bfloat16)
    down_proj = (
        lax.psum_scatter(
            jnp.dot(activated, w_down, preferred_element_type=jnp.float32).astype(jnp.bfloat16),
            "narrow",
            scatter_dimension=0,
            tiled=True,
        ).astype(jnp.float32)
        + vector_rows[1]
    )
    second_normed, second_scale = normalize(first_norm + down_proj)
    block_out = (second_normed * vector_rows[4] + vector_rows[5]).astype(jnp.bfloat16)
    back_weights = lax.all_gather(params.astype(jnp.bfloat16), "wide", axis=1, tiled=True)
    w_qkv, w_out, w_up, w_down, qv_bias, up_bias, bias_table, vec_piece = unpack_rank(
        back_weights[0], ranks
    )
    w_qkv_flat = w_qkv.reshape(D, 3 * width_part)
    back_grid = expand_bias(bias_table, onehot_table)
    grad_float = out_grad.astype(jnp.float32)
    gain_two = jnp.sum(grad_float * second_normed, axis=0)
    shift_two = jnp.sum(grad_float, axis=0)
    grad_two = norm_backward(grad_float * vector_rows[4], second_normed, second_scale)
    grad_down = grad_two.astype(jnp.bfloat16)
    bias_down = jnp.sum(grad_down.astype(jnp.float32), axis=0)
    down_group = lax.all_gather(grad_down, "narrow", axis=0, tiled=True)
    weight_down = jnp.einsum("nf,nd->fd", activated, down_group, preferred_element_type=jnp.float32)
    grad_act = jnp.einsum("nd,fd->nf", down_group, w_down, preferred_element_type=jnp.float32)
    grad_up = (grad_act * gelu_slope(up_proj)).astype(jnp.bfloat16)
    bias_up = jnp.sum(grad_up.astype(jnp.float32), axis=0)
    weight_up = jnp.einsum("nd,nf->df", first_group, grad_up, preferred_element_type=jnp.float32)
    grad_first = (
        lax.psum_scatter(
            jnp.einsum("nf,df->nd", grad_up, w_up, preferred_element_type=jnp.float32).astype(
                jnp.bfloat16
            ),
            "narrow",
            scatter_dimension=0,
            tiled=True,
        ).astype(jnp.float32)
        + grad_two
    )
    gain_one = jnp.sum(grad_first * first_normed, axis=0)
    shift_one = jnp.sum(grad_first, axis=0)
    grad_one = norm_backward(grad_first * vector_rows[2], first_normed, first_scale)
    grad_attn = grad_one.astype(jnp.bfloat16)
    bias_out = jnp.sum(grad_attn.astype(jnp.float32), axis=0)
    attn_group = lax.all_gather(grad_attn, "narrow", axis=0, tiled=True)
    weight_out = jnp.einsum("nd,ne->de", mixed_loc, attn_group, preferred_element_type=jnp.float32)
    grad_mixed = jnp.einsum(
        "ne,de->nd", attn_group, w_out, preferred_element_type=jnp.float32
    ).astype(jnp.bfloat16)
    grad_rows, table_rows = lax.map(
        lambda element: attend_backward(element[0], element[1], element[2], element[3], back_grid),
        (row_blocks, group_lengths, log_totals, grad_mixed.reshape(-1, L, width_part)),
    )
    grad_qkv = grad_rows.reshape(-1, 3 * width_part).astype(jnp.bfloat16)
    grad_table = jnp.dot(jnp.sum(table_rows, axis=0), onehot_table, precision=HIGHEST).T
    qkv_sums = jnp.sum(grad_qkv.astype(jnp.float32), axis=0)
    weight_qkv = jnp.einsum("nd,ne->de", group_in, grad_qkv, preferred_element_type=jnp.float32)
    input_grad = grad_one + lax.psum_scatter(
        jnp.einsum("ne,de->nd", grad_qkv, w_qkv_flat, preferred_element_type=jnp.float32).astype(
            jnp.bfloat16
        ),
        "narrow",
        scatter_dimension=0,
        tiled=True,
    ).astype(jnp.float32)
    vec_grads = jnp.stack([bias_out, bias_down, gain_one, shift_one, gain_two, shift_two]).reshape(
        ranks, -1
    )
    vec_share = lax.psum_scatter(vec_grads, "narrow", scatter_dimension=0, tiled=True)
    local_grads = jnp.concatenate(
        [
            weight_qkv.reshape(-1),
            weight_out.reshape(-1),
            weight_up.reshape(-1),
            weight_down.reshape(-1),
            qkv_sums[:width_part],
            qkv_sums[2 * width_part :],
            bias_up,
            grad_table.reshape(-1),
            vec_share.reshape(-1),
        ]
    )
    grad_shard = lax.psum_scatter(local_grads, "wide", scatter_dimension=0, tiled=True).reshape(
        1, -1
    )
    device_count = lax.axis_size("wide") * ranks
    step_rate = 1.0 / (32.0 * math.sqrt(tok_rows * device_count))
    new_momentum = 0.5 * momentum + step_rate * grad_shard
    new_params = params - (step_rate * grad_shard + 0.5 * new_momentum)
    new_average = 0.5 * average + 0.5 * new_params
    return (
        block_out,
        input_grad,
        grad_shard,
        new_params,
        new_momentum,
        new_average,
        new_params.astype(jnp.bfloat16),
    )


def solution(mesh):
    placed = (
        P(("wide", "narrow"), None),
        P(("wide", "narrow"), None),
        P(("wide", "narrow"), None),
        P("narrow", "wide"),
        P("narrow", "wide"),
        P("narrow", "wide"),
    )
    return jax.shard_map(
        body,
        mesh=mesh,
        in_specs=placed,
        out_specs=(
            P(("wide", "narrow"), None),
            P(("wide", "narrow"), None),
            P("narrow", "wide"),
            P("narrow", "wide"),
            P("narrow", "wide"),
            P("narrow", "wide"),
            P("narrow", "wide"),
        ),
        check_vma=False,
    )
```

profile of v0, /device:TPU:0, one launch (start us, length us, event | category | flops | bytes accessed | tf_op | source)
XLA Modules:
  0.0 994.1 jit_solution(861757795889754027)
XLA Ops:
  10.5 6.0 all-gather
  16.5 105.4 %all-gather.10.cloned.1.call-done = bf16[1,1772544]{1,0:T(2,128)(2,1)} async-done(((bf16[1,221568]{1,0:T(2,128)(2,1)}), bf16[1,1772544]{1,0:T(2,128)(2,1)}) %all-gather.10.cloned.1.call-update) | async-done | bytes 3545104 | tf_op jit(solution)/shard_map/all_gather | solution.py:164
  123.3 5.9 slice_reduce_fusion.3
  129.4 16.1 %slice_reduce_fusion.2 = bf16[442368]{0:T(1024)(128)(2,1)S(1)} fusion(bf16[1,1772544]{1,0:T(2,128)(2,1)} %all-gather.10.cloned.1.call-done), kind=kLoop, calls=%fused_computation.59 | loop fusion | bytes 1769472 | tf_op jit(solution)/shard_map/slice | solution.py:35
  159.6 13.9 %tile.5 = f32[3,524800]{1,0:T(4,128)} reshape(f32[3,512,1025]{2,1,0:T(8,128)} %tile.4) | data formatting | bytes 12595200 | tf_op jit(solution)/shard_map/tile | solution.py:57
  185.5 17.5 %while.24 = (s32[]{:T(128)}, bf16[4,512,192]{1,2,0:T(8,128)(2,1)}, f32[4,3,512]{2,1,0:T(4,128)S(1)}, bf16[4,512,576]{1,2,0:T(8,128)(2,1)}, s32[4,4]{1,0:T(4,128)...) while((s32[]{:T(128)}, bf16[4,512,192]{1,2,0:T(8,128)(2,1)}, f32[4,3,512]{2,1,0:T(4,128)S(1)}, ...), condition=%wide.region_5.6_spmd, body=%wide.region_0.5_spmd.sunk | while | flops 208670736 | bytes 16705729 | solution.py:183
  214.9 52.9 %reduce-scatter.5.cloned.1.call-done = f32[512,768]{1,0:T(8,128)} async-done(((f32[2048,768]{1,0:T(8,128)}), f32[512,768]{1,0:T(8,128)}) %reduce-scatter.5.cloned.1.call-update) | async-done | bytes 1572880 | tf_op jit(solution)/shard_map/reduce_scatter | solution.py:189
  272.1 27.9 %slice_reduce_fusion = (bf16[589824]{0:T(1024)(128)(2,1)}, bf16[589824]{0:T(1024)(128)(2,1)}) fusion(bf16[1,1772544]{1,0:T(2,128)(2,1)} %all-gather.10.cloned.1.call-done), kind=kLoop, calls=%fused_computation.54 | loop fusion | bytes 4718592 | tf_op jit(solution)/shard_map/slice | solution.py:35
  307.4 6.6 multiply_convert_fusion.1
  319.7 38.0 %reduce-scatter.7.cloned.1.call-done = bf16[512,768]{1,0:T(8,128)(2,1)} async-done(((bf16[2048,768]{1,0:T(8,128)(2,1)}), bf16[512,768]{1,0:T(8,128)(2,1)}) %reduce-scatter.7.cloned.1.call-update) | async-done | bytes 786448 | tf_op jit(solution)/shard_map/reduce_scatter | solution.py:206
  363.6 28.6 %all-gather.14.cloned.1.call-done = bf16[2048,768]{1,0:T(8,128)(2,1)} async-done(((bf16[512,768]{1,0:T(8,128)(2,1)}), bf16[2048,768]{1,0:T(8,128)(2,1)}) %all-gather.14.cloned.1.call-update) | async-done | bytes 3145744 | tf_op jit(solution)/shard_map/all_gather | solution.py:228
  392.2 8.1 convert_reduce_fusion.2
  406.0 38.0 %reduce-scatter.9.cloned.1.call-done = bf16[512,768]{1,0:T(8,128)(2,1)} async-done(((bf16[2048,768]{1,0:T(8,128)(2,1)}), bf16[512,768]{1,0:T(8,128)(2,1)}) %reduce-scatter.9.cloned.1.call-update) | async-done | bytes 786448 | tf_op jit(solution)/shard_map/reduce_scatter | solution.py:235
  450.3 28.6 %all-gather.16.cloned.1.call-done = bf16[2048,768]{1,0:T(8,128)(2,1)} async-done(((bf16[512,768]{1,0:T(8,128)(2,1)}), bf16[2048,768]{1,0:T(8,128)(2,1)}) %all-gather.16.cloned.1.call-update) | async-done | bytes 3145744 | tf_op jit(solution)/shard_map/all_gather | solution.py:250
  482.9 145.1 %while.25 = (s32[]{:T(128)}, bf16[4,512,576]{1,2,0:T(8,128)(2,1)}, f32[4,3,1025]{2,1,0:T(4,128)}, bf16[4,512,576]{1,2,0:T(8,128)(2,1)}, s32[4,4]{1,0:T(4,128)S(1...) while((s32[]{:T(128)}, bf16[4,512,576]{1,2,0:T(8,128)(2,1)}, ...), condition=%wide.region_22.23_spmd, body=%wide.region_17.22_spmd.sunk | while | flops 516755456 | bytes 101880792 | solution.py:255
  500.6 14.7 %reshape.357 = f32[3,512,1025]{2,1,0:T(8,128)} reshape(f32[3,524800]{1,0:T(4,128)} %pad_convert_fusion.2) | data formatting | bytes 12595200 | tf_op jit(solution)/shard_map/while/body/eval_jaxpr/reshape | solution.py:67
  536.8 14.7 %reshape.357 = f32[3,512,1025]{2,1,0:T(8,128)} reshape(f32[3,524800]{1,0:T(4,128)} %pad_convert_fusion.2) | data formatting | bytes 12595200 | tf_op jit(solution)/shard_map/while/body/eval_jaxpr/reshape | solution.py:67
  572.9 14.7 %reshape.357 = f32[3,512,1025]{2,1,0:T(8,128)} reshape(f32[3,524800]{1,0:T(4,128)} %pad_convert_fusion.2) | data formatting | bytes 12595200 | tf_op jit(solution)/shard_map/while/body/eval_jaxpr/reshape | solution.py:67
  609.1 14.7 %reshape.357 = f32[3,512,1025]{2,1,0:T(8,128)} reshape(f32[3,524800]{1,0:T(4,128)} %pad_convert_fusion.2) | data formatting | bytes 12595200 | tf_op jit(solution)/shard_map/while/body/eval_jaxpr/reshape | solution.py:67
  636.3 6.0 fusion.41
  644.9 7.0 fusion.42
  655.5 12.3 %all-reduce.2 = f32[4,1152]{1,0:T(4,128)S(1)} all-reduce(f32[4,1152]{1,0:T(4,128)S(1)} %reshape.324), channel_id=6, replica_groups=mesh['wide'=8,'narrow'=4] {'narrow'}, use_global_device_ids=true, to_apply=%region_33.34.clone | all-reduce | flops 4608 | bytes 36864
  688.0 50.5 %concatenate.22 = f32[1772544]{0:T(1024)} concatenate(f32[442368]{0:T(1024)} %reshape.319, f32[147456]{0:T(1024)S(1)} %reshape.320, f32[589824]{0:T(1024)S(1)} %reshape.321, f32[589824]{0:T(1024)} %reshape.322, f32[192]{0:T(256)S(1)} %get-tuple-element.214, f32[192]{0:T(256)S(1)} %get-tuple-element.213, f32[768]{0:T(1024)S(1)} %copy-done.27, f32[768]{0:T(1024)S(1)} %reshape.323, ...), dimensions={0} | concatenate | bytes 14180352 | tf_op jit(solution)/shard_map/concatenate | solution.py:275
  742.9 230.8 %all-reduce.6.cloned.1.call-done = f32[1772544]{0:T(1024)} async-done(((f32[1772544]{0:T(1024)}), f32[1772544]{0:T(1024)}) %all-reduce.6.cloned.1.call-update) | async-done | bytes 7090192
  (353 shorter events, 236.1 us)
Async XLA Ops:
  7.2 114.8 %all-gather.10.cloned.1.call-start = ((), (), s32[]{:S(2)}) async-start(), calls=%async_computation.5 | async-start | bytes 7976448 | tf_op jit(solution)/shard_map/all_gather | solution.py:164
  9.7 140.6 %all-gather.8.cloned.1.call-start = ((), (), s32[]{:S(2)}) async-start(), calls=%async_computation.4 | async-start | bytes 3932160 | tf_op jit(solution)/shard_map/all_gather | solution.py:169
  10.4 257.4 %reduce-scatter.5.cloned.1.call-start = ((), (), s32[]{:S(2)}) async-start(), calls=%async_computation.6 | async-start | bytes 7864320 | tf_op jit(solution)/shard_map/reduce_scatter | solution.py:189
  16.5 129.0 %copy-start.25 = (s32[1025]{0:T(1024)}, s32[1025]{0:T(1024)S(1)}, u32[]{:S(2)}) copy-start(s32[1025]{0:T(1024)S(1)} %add_clamp_fusion) | copy-start | bytes 12304
  123.2 24.0 %copy-start.22 = (f32[1025,3]{0,1:T(4,128)}, f32[1025,3]{0,1:T(4,128)S(1)}, u32[]{:S(2)}) copy-start(f32[1025,3]{0,1:T(4,128)S(1)} %fusion.22) | copy-start | bytes 36904
  208.8 98.6 %all-gather.12.cloned.1.call-start = ((), (), s32[]{:S(2)}) async-start(), calls=%async_computation.7 | async-start | bytes 3932160 | tf_op jit(solution)/shard_map/all_gather | solution.py:200
  272.1 85.6 %reduce-scatter.7.cloned.1.call-start = ((), (), s32[]{:S(2)}) async-start(), calls=%async_computation.8 | async-start | bytes 3932160 | tf_op jit(solution)/shard_map/reduce_scatter | solution.py:206
  307.4 8.3 copy-start.15
  319.6 72.5 %all-gather.14.cloned.1.call-start = ((), (), s32[]{:S(2)}) async-start(), calls=%async_computation.9 | async-start | bytes 3932160 | tf_op jit(solution)/shard_map/all_gather | solution.py:228
  363.5 80.5 %reduce-scatter.9.cloned.1.call-start = ((), (), s32[]{:S(2)}) async-start(), calls=%async_computation.10 | async-start | bytes 3932160 | tf_op jit(solution)/shard_map/reduce_scatter | solution.py:235
  392.2 9.7 copy-start.14
  406.0 73.0 %all-gather.16.cloned.1.call-start = ((), (), s32[]{:S(2)}) async-start(), calls=%async_computation.11 | async-start | bytes 3932160 | tf_op jit(solution)/shard_map/all_gather | solution.py:250
  450.3 290.2 %reduce-scatter.11.cloned.1.call-start = ((), (), s32[]{:S(2)}) async-start(), calls=%async_computation.12 | async-start | bytes 3932160 | tf_op jit(solution)/shard_map/reduce_scatter | solution.py:263
  515.3 4.1 copy-start.29
  551.5 4.1 copy-start.29
  630.2 4.2 copy-start.13
  634.4 339.2 %all-reduce.6.cloned.1.call-start = ((), (), s32[]{:S(2)}) async-start(), calls=%async_computation.13 | async-start | bytes 14180352
  651.9 16.5 %copy-start.7 = (bf16[4,24,8,512]{3,2,0,1:T(8,128)(2,1)S(1)}, bf16[4,24,8,512]{3,2,0,1:T(8,128)(2,1)}, u32[]{:S(2)}) copy-start(bf16[4,24,8,512]{3,2,0,1:T(8,128)(2,1)} %copy-done.6) | copy-start | bytes 2359300
  668.4 4.7 copy-start.19
  668.4 4.7 copy-start.26
  683.0 5.1 copy-start.27
  742.9 237.2 %copy-start.10 = (f32[1,221568]{1,0:T(1,128)S(1)}, f32[1,221568]{1,0:T(1,128)}, u32[]{:S(2)}) copy-start(f32[1,221568]{1,0:T(1,128)} %param.13) | copy-start | bytes 2658820
  973.6 6.5 copy-start.17
  980.1 5.1 copy-start.18
  (46 other events, 139.1 us)
Sparse Core Ops, SparseCore 0:
  10.8 111.1 all-gather.9
  123.5 26.6 all-gather.7
  208.9 58.8 reduce-scatter.4
  272.2 28.4 all-gather.11
  319.8 37.8 reduce-scatter.6
  363.6 28.4 all-gather.13
  406.1 37.8 reduce-scatter.8
  450.4 28.4 all-gather.15
  634.5 38.4 reduce-scatter.10
  738.7 234.9 all-reduce.5
where the time goes:
time: 1000 us; the launch traced here: 994 us
  waiting for transfers between devices  525 us (52%)
  local copies, waits for them, and re-layouts  266 us (27%)
  matrix products  84.2 us (8%)
  other arithmetic  77.6 us (8%)
  blocking collectives  23.5 us (2%)
  between operations  15.4 us (2%)
    unnamed x11, waiting for transfers between devices  232 us
    all_gather x1, waiting for transfers between devices, body(): lax.all_gather(params.astype(jnp.bfloat16), 'wide', axis=1, tiled=True)  105 us
    reshape x4, local copies, waits for them, and re-layouts, diag_sums(): return jnp.sum(padded.reshape(head_count, L, 2 * L + 1), axis=1)  58.8 us
    reduce_scatter x1, waiting for transfers between devices, body(): lax.psum_scatter(jnp.dot(mixed_loc, w_out, preferred_element_type=jnp.flo...  52.9 us
    slice x4, local copies, waits for them, and re-layouts, unpack_rank(): lax.slice_in_dim(flat_rank, offset, offset + amount).reshape(extent)  50.5 us
    concatenate x1, local copies, waits for them, and re-layouts, body(): jnp.concatenate([weight_qkv.reshape(-1), weight_out.reshape(-1), weight_u...  50.5 us
    reduce_scatter x1, waiting for transfers between devices, body(): lax.psum_scatter(jnp.einsum('nf,df->nd', grad_up, w_up, preferred_element...  38 us
    reduce_scatter x1, waiting for transfers between devices, body(): lax.psum_scatter(jnp.dot(activated, w_down, preferred_element_type=jnp.fl...  38 us
  transfers between devices with their start and end apart: 10, of which 8 were waited for; matrix products, arithmetic and copies ran while one was open for 16% of the time, Pallas kernels for 0%

commit v1 on v0

v1 whole, which is shorter than its diff:
```python
import functools
import math

import jax
import jax.numpy as jnp
from jax import lax
from jax.experimental import pallas as pl
from jax.experimental.pallas import tpu as pltpu
from jax.sharding import PartitionSpec as P

D = 768
HEADS = 12
FF = 3072
HD = 64
BUCKETS = 256
L = 512
RANKS = 4
PART = D // RANKS
HPR = HEADS // RANKS
QKV_ROWS = 3 * PART
TILE_ROWS = 16
MAT_ROWS = 3 * D
PAD_ROWS = MAT_ROWS + TILE_ROWS
BLK = 128
NBLK = L // BLK
NEG = -1000000000.0
VMEM_LIMIT = 60 * 1024 * 1024
BF = jnp.bfloat16
F32 = jnp.float32


def mm(a, b):
    return jnp.dot(a, b, preferred_element_type=F32)


def mm_nt(a, b):
    return lax.dot_general(a, b, (((1,), (1,)), ((), ())), preferred_element_type=F32)


def mm_tn(a, b):
    return lax.dot_general(a, b, (((0,), (0,)), ((), ())), preferred_element_type=F32)


def qkv_pieces():
    for b in range(2):
        for j in range(4):
            for c in range(3):
                t, q = divmod(3 * j + c, 4)
                yield 288 * b + 96 * t, PART * q, PART * j + 96 * b, PART * c


def column_order():
    d = lax.broadcasted_iota(jnp.int32, (D, D), 0)
    n = lax.broadcasted_iota(jnp.int32, (D, D), 1)
    j = (n >= PART).astype(jnp.int32) + (n >= 2 * PART).astype(jnp.int32) + (n >= 3 * PART).astype(jnp.int32)
    return (d == 4 * (n - PART * j) + j).astype(F32).astype(BF)


def vector_rows(tail_ref):
    chunks = []
    for r in range(RANKS):
        chunks.append(tail_ref[r, 2:3, 384:768])
        chunks.append(tail_ref[r, 3:4, 0:384])
        chunks.append(tail_ref[r, 3:4, 384:768])
    return [
        jnp.concatenate([chunks[2 * v], chunks[2 * v + 1]], axis=1).astype(F32) for v in range(6)
    ]


def normalize(values):
    centred = values - jnp.mean(values, axis=-1, keepdims=True)
    inv = lax.rsqrt(jnp.mean(centred * centred, axis=-1, keepdims=True) + 1e-05)
    return centred * inv, inv


def norm_backward(e, normed, inv):
    return inv * (
        e - jnp.mean(e, axis=-1, keepdims=True) - normed * jnp.mean(e * normed, axis=-1, keepdims=True)
    )


def col_sum(values):
    return jnp.sum(values, axis=0, keepdims=True)


def merge_kernel(wide, rows, g_ref, out_ref):
    for w in range(wide):
        out_ref[0, rows * w : rows * (w + 1), :] = g_ref[0, w, 0:rows, :]
    for w in range(1, wide + 1):
        at = rows * w
        edge = g_ref[0, w - 1, rows : rows + TILE_ROWS, :]
        if w < wide:
            edge = g_ref[0, w, 0:TILE_ROWS, :] + edge
        out_ref[0, at : at + TILE_ROWS, :] = edge


def merge_blocks(g):
    _, wide, cap, _ = g.shape
    return pl.pallas_call(
        functools.partial(merge_kernel, wide, cap - TILE_ROWS),
        grid=(RANKS,),
        in_specs=[pl.BlockSpec((1, wide, cap, D), lambda r: (r, 0, 0, 0))],
        out_specs=pl.BlockSpec((1, PAD_ROWS, D), lambda r: (r, 0, 0)),
        out_shape=jax.ShapeDtypeStruct((RANKS, PAD_ROWS, D), BF),
        compiler_params=pltpu.CompilerParams(vmem_limit_bytes=VMEM_LIMIT),
        name="merge_weights",
    )(g)


def segment_of(pos, len_ref):
    end0 = len_ref[0]
    end1 = end0 + len_ref[1]
    end2 = end1 + len_ref[2]
    return (
        (pos >= end0).astype(jnp.int32)
        + (pos >= end1).astype(jnp.int32)
        + (pos >= end2).astype(jnp.int32)
    )


def att_fwd_kernel(
    len_ref, x_ref, mq_ref, wo_ref, tail_ref,
    qkv_ref, wq_ref, xp_ref, mixed_ref, probs_ref, n1_ref, r1_ref,
    table_s, acc_s,
):
    r = pl.program_id(0)

    @pl.when(r == 0)
    def _():
        xp_ref[...] = mm(x_ref[...], column_order()).astype(BF)
        acc_s[...] = jnp.zeros_like(acc_s)
        src = lax.broadcasted_iota(jnp.int32, (3 * BUCKETS, 3 * BUCKETS), 0)
        dst = lax.broadcasted_iota(jnp.int32, (3 * BUCKETS, 3 * BUCKETS), 1)
        hh = (dst >= BUCKETS).astype(jnp.int32) + (dst >= 2 * BUCKETS).astype(jnp.int32)
        pick = (src == 3 * (dst - BUCKETS * hh) + hh).astype(F32).astype(BF)
        flat = jnp.concatenate(
            [
                jnp.concatenate([tail_ref[k, 1:2, 384:768], tail_ref[k, 2:3, 0:384]], axis=1).astype(F32)
                for k in range(RANKS)
            ]
            + [jnp.zeros((4, D), F32)],
            axis=0,
        ).astype(BF)
        tables = mm(flat, pick)
        for k in range(RANKS):
            for h in range(HPR):
                row = tables[k : k + 1, BUCKETS * h : BUCKETS * (h + 1)]
                table_s[k, h : h + 1, :] = jnp.concatenate(
                    [
                        row,
                        jnp.broadcast_to(row[:, 255:256], (1, BLK)),
                        jnp.broadcast_to(row[:, 0:1], (1, BLK)),
                    ],
                    axis=1,
                )

    for src_row, src_col, dst_row, dst_col in qkv_pieces():
        wq_ref[0, dst_row : dst_row + 96, dst_col : dst_col + PART] = mq_ref[
            0, src_row : src_row + 96, src_col : src_col + PART
        ]
    first = tail_ref[r, 0:1, :]
    bias = jnp.concatenate(
        [first[:, 0:PART], jnp.zeros((1, PART), BF), first[:, PART : 2 * PART]], axis=1
    ).astype(F32)
    qkv = (mm(xp_ref[...], wq_ref[0]) + bias).astype(BF)
    qkv_ref[0] = qkv

    seg_j = segment_of(lax.broadcasted_iota(jnp.int32, (1, L), 1), len_ref)
    table = table_s[r]
    heads = []
    for h in range(HPR):
        q = qkv[:, HD * h : HD * (h + 1)]
        k = qkv[:, PART + HD * h : PART + HD * (h + 1)]
        v = qkv[:, 2 * PART + HD * h : 2 * PART + HD * (h + 1)]
        row = table[h : h + 1, :]
        near = pltpu.roll(jnp.broadcast_to(row, (BLK, 4 * BLK)), 0, 1, stride=1, stride_axis=0)
        far_right = jnp.broadcast_to(row[:, 255:256], (BLK, BLK))
        far_left = jnp.broadcast_to(row[:, 511:512], (BLK, BLK))
        for i in range(NBLK):
            seg_i = segment_of(
                lax.broadcasted_iota(jnp.int32, (BLK, 1), 0) + BLK * i, len_ref
            )
            parts = []
            for jb in range(NBLK):
                delta = jb - i
                if abs(delta) <= 1:
                    parts.append(near[:, BLK * (delta + 1) : BLK * (delta + 2)])
                else:
                    parts.append(far_right if delta > 0 else far_left)
            logits = mm_nt(q[BLK * i : BLK * (i + 1)], k) * 0.125 + jnp.concatenate(parts, axis=1)
            logits = jnp.where(seg_i == seg_j, logits, NEG)
            top = jnp.max(logits, axis=-1, keepdims=True)
            expo = jnp.exp(logits - top)
            total = jnp.sum(expo, axis=-1, keepdims=True)
            probs_ref[0, h, BLK * i : BLK * (i + 1), :] = (expo * (1.0 / total)).astype(BF)
        heads.append(mm(probs_ref[0, h], v))
    mixed = jnp.concatenate(heads, axis=1).astype(BF)
    mixed_ref[0] = mixed
    acc_s[...] += mm(mixed, wo_ref[0])

    @pl.when(r == RANKS - 1)
    def _():
        vec = vector_rows(tail_ref)
        normed, inv = normalize(x_ref[...].astype(F32) + acc_s[...] + vec[0])
        n1_ref[...] = normed
        r1_ref[...] = jnp.broadcast_to(inv, (L, BLK))


def attention_forward(lengths, x, mats):
    whole = lambda *shape: pl.BlockSpec(shape, lambda r, n: (0,) * len(shape))
    per = lambda *shape: pl.BlockSpec((1, *shape), lambda r, n: (r,) + (0,) * len(shape))
    return pl.pallas_call(
        att_fwd_kernel,
        grid_spec=pltpu.PrefetchScalarGridSpec(
            num_scalar_prefetch=1,
            grid=(RANKS,),
            in_specs=[
                whole(L, D),
                pl.BlockSpec((1, QKV_ROWS, D), lambda r, n: (r, 0, 0)),
                pl.BlockSpec((1, PART, D), lambda r, n: (r, 3, 0)),
                pl.BlockSpec((RANKS, TILE_ROWS, D), lambda r, n: (0, MAT_ROWS // TILE_ROWS, 0)),
            ],
            out_specs=[
                per(L, QKV_ROWS),
                per(D, QKV_ROWS),
                whole(L, D),
                per(L, PART),
                per(HPR, L, L),
                whole(L, D),
                whole(L, BLK),
            ],
            scratch_shapes=[pltpu.VMEM((RANKS, 8, 512), F32), pltpu.VMEM((L, D), F32)],
        ),
        out_shape=[
            jax.ShapeDtypeStruct((RANKS, L, QKV_ROWS), BF),
            jax.ShapeDtypeStruct((RANKS, D, QKV_ROWS), BF),
            jax.ShapeDtypeStruct((L, D), BF),
            jax.ShapeDtypeStruct((RANKS, L, PART), BF),
            jax.ShapeDtypeStruct((RANKS, HPR, L, L), BF),
            jax.ShapeDtypeStruct((L, D), F32),
            jax.ShapeDtypeStruct((L, BLK), F32),
        ],
        compiler_params=pltpu.CompilerParams(vmem_limit_bytes=VMEM_LIMIT),
        name="attention_forward",
    )(lengths, x, mats, mats, mats)


def ffn_kernel(
    n1_ref, r1_ref, og_ref, up_ref, down_ref, tail_ref,
    block_ref, du_ref, dd_ref, grad_one_ref, ga_ref, vec_ref, bup_ref,
    fn_s, fl_s, up_s, act_s, down_s, gd_s, gf_s,
):
    step = pl.program_id(0)
    r = lax.rem(step, RANKS)
    inv_root2 = 1.0 / math.sqrt(2.0)

    @pl.when(step == 0)
    def _():
        vec = vector_rows(tail_ref)
        first = n1_ref[...] * vec[2] + vec[3]
        fn_s[...] = first
        fl_s[...] = first.astype(BF)

    @pl.when(step < RANKS)
    def _():
        bias = jnp.concatenate([tail_ref[r, 0:1, 384:768], tail_ref[r, 1:2, 0:384]], axis=1)
        up = mm(fl_s[...], up_ref[0]) + bias.astype(F32)
        up_s[r] = up
        act = (0.5 * up * (1.0 + lax.erf(up * inv_root2))).astype(BF)
        act_s[r] = act
        down = mm(act, down_ref[0])

        @pl.when(step == 0)
        def _():
            down_s[...] = down

        @pl.when(step > 0)
        def _():
            down_s[...] += down

    @pl.when(step == RANKS)
    def _():
        vec = vector_rows(tail_ref)
        normed, inv = normalize(fn_s[...] + down_s[...] + vec[1])
        block_ref[...] = (normed * vec[4] + vec[5]).astype(BF)
        og = og_ref[...].astype(F32)
        vec_ref[4:5, :] = col_sum(og * normed)
        vec_ref[5:6, :] = col_sum(og)
        grad_two = norm_backward(og * vec[4], normed, inv)
        low = grad_two.astype(BF)
        gd_s[...] = low
        vec_ref[1:2, :] = col_sum(low.astype(F32))
        vec_ref[6:8, :] = jnp.zeros((2, D), F32)
        gf_s[...] = grad_two

    @pl.when(step >= RANKS)
    def _():
        gd = gd_s[...]
        dd_ref[0] = mm_tn(act_s[r], gd).astype(BF)
        up = up_s[r]
        slope = 0.5 * (1.0 + lax.erf(up * inv_root2)) + up * jnp.exp(-0.5 * up * up) * (
            1.0 / math.sqrt(2.0 * math.pi)
        )
        gu = (mm_nt(gd, down_ref[0]) * slope).astype(BF)
        bup_ref[0, 0:1, :] = col_sum(gu.astype(F32))
        bup_ref[0, 1:8, :] = jnp.zeros((7, D), F32)
        du_ref[0] = mm_tn(fl_s[...], gu).astype(BF)
        gf_s[...] += mm_nt(gu, up_ref[0])

    @pl.when(step == 2 * RANKS - 1)
    def _():
        vec = vector_rows(tail_ref)
        f = gf_s[...]
        normed = n1_ref[...]
        vec_ref[2:3, :] = col_sum(f * normed)
        vec_ref[3:4, :] = col_sum(f)
        grad_one = norm_backward(f * vec[2], normed, r1_ref[:, 0:1])
        grad_one_ref[...] = grad_one
        low = grad_one.astype(BF)
        ga_ref[...] = low
        vec_ref[0:1, :] = col_sum(low.astype(F32))


def feed_forward(n1, r1, out_grad, mats):
    whole = lambda *shape: pl.BlockSpec(shape, lambda s: (0,) * len(shape))
    late = lambda *shape: pl.BlockSpec(
        (1, *shape), lambda s: (jnp.maximum(s - RANKS, 0),) + (0,) * len(shape)
    )
    return pl.pallas_call(
        ffn_kernel,
        grid=(2 * RANKS,),
        in_specs=[
            whole(L, D),
            whole(L, BLK),
            whole(L, D),
            pl.BlockSpec((1, D, D), lambda s: (lax.rem(s, RANKS), 1, 0)),
            pl.BlockSpec((1, D, D), lambda s: (lax.rem(s, RANKS), 2, 0)),
            pl.BlockSpec((RANKS, TILE_ROWS, D), lambda s: (0, MAT_ROWS // TILE_ROWS, 0)),
        ],
        out_specs=[
            whole(L, D),
            late(D, D),
            late(D, D),
            whole(L, D),
            whole(L, D),
            whole(8, D),
            late(8, D),
        ],
        out_shape=[
            jax.ShapeDtypeStruct((L, D), BF),
            jax.ShapeDtypeStruct((RANKS, D, D), BF),
            jax.ShapeDtypeStruct((RANKS, D, D), BF),
            jax.ShapeDtypeStruct((L, D), F32),
            jax.ShapeDtypeStruct((L, D), BF),
            jax.ShapeDtypeStruct((8, D), F32),
            jax.ShapeDtypeStruct((RANKS, 8, D), F32),
        ],
        scratch_shapes=[
            pltpu.VMEM((L, D), F32),
            pltpu.VMEM((L, D), BF),
            pltpu.VMEM((RANKS, L, D), F32),
            pltpu.VMEM((RANKS, L, D), BF),
            pltpu.VMEM((L, D), F32),
            pltpu.VMEM((L, D), BF),
            pltpu.VMEM((L, D), F32),
        ],
        compiler_params=pltpu.CompilerParams(vmem_limit_bytes=VMEM_LIMIT),
        name="feed_forward",
    )(n1, r1, out_grad, mats, mats, mats)


def att_bwd_kernel(
    ga_ref, wo_ref, qkv_ref, probs_ref, mixed_ref, wq_ref, xp_ref, grad_one_ref,
    da_ref, in_grad_ref, table_ref, qv_ref,
    ds_s, near_s, dx_s,
):
    r = pl.program_id(0)
    ga = ga_ref[...]
    da_ref[0, QKV_ROWS:D, :] = mm_tn(mixed_ref[0], ga).astype(BF)
    dm_all = mm_nt(ga, wo_ref[0]).astype(BF)
    qkv = qkv_ref[0]
    dq, dk, dv = [], [], []
    for h in range(HPR):
        q = qkv[:, HD * h : HD * (h + 1)]
        k = qkv[:, PART + HD * h : PART + HD * (h + 1)]
        v = qkv[:, 2 * PART + HD * h : 2 * PART + HD * (h + 1)]
        dm = dm_all[:, HD * h : HD * (h + 1)]
        far_left = jnp.zeros((BLK, BLK), F32)
        far_right = jnp.zeros((BLK, BLK), F32)
        for i in range(NBLK):
            rows = slice(BLK * i, BLK * (i + 1))
            p = probs_ref[0, h, rows, :].astype(F32)
            dp = mm_nt(dm[rows], v)
            ds = (p * (dp - jnp.sum(p * dp, axis=-1, keepdims=True))).astype(BF)
            ds_s[rows, :] = ds
            ds = ds.astype(F32)
            for jb in range(NBLK):
                piece = ds[:, BLK * jb : BLK * (jb + 1)]
                delta = jb - i
                if abs(delta) <= 1:
                    cols = slice(BLK * (delta + 1), BLK * (delta + 2))
                    if i == max(0, -delta):
                        near_s[:, cols] = piece
                    else:
                        near_s[:, cols] += piece
                elif delta > 0:
                    far_right += piece
                else:
                    far_left += piece
        near_s[:, 3 * BLK :] = jnp.zeros((BLK, BLK), F32)
        table_ref[0, h : h + 1, 0 : 4 * BLK] = diagonal_sums(near_s[...])
        table_ref[0, h : h + 1, 4 * BLK : 5 * BLK] = col_sum(far_left)
        table_ref[0, h : h + 1, 5 * BLK : 6 * BLK] = col_sum(far_right)
        dscore = ds_s[...]
        dq.append(mm(dscore, k) * 0.125)
        dk.append(mm_tn(dscore, q) * 0.125)
        dv.append(mm_tn(probs_ref[0, h], dm))
    table_ref[0, HPR:8, :] = jnp.zeros((8 - HPR, 6 * BLK), F32)
    dqkv = jnp.concatenate(dq + dk + dv, axis=1).astype(BF)
    qv_ref[0, 0:1, :] = col_sum(dqkv.astype(F32))
    qv_ref[0, 1:8, :] = jnp.zeros((7, QKV_ROWS), F32)
    dw = mm_tn(xp_ref[...], dqkv).astype(BF)
    for src_row, src_col, dst_row, dst_col in qkv_pieces():
        da_ref[0, src_row : src_row + 96, src_col : src_col + PART] = dw[
            dst_row : dst_row + 96, dst_col : dst_col + PART
        ]
    dx = mm_nt(dqkv, wq_ref[0])

    @pl.when(r == 0)
    def _():
        dx_s[...] = dx

    @pl.when(r > 0)
    def _():
        dx_s[...] += dx

    @pl.when(r == RANKS - 1)
    def _():
        in_grad_ref[...] = grad_one_ref[...] + mm_nt(dx_s[...].astype(BF), column_order())


def diagonal_sums(block):
    half = block.shape[0] // 2
    while half >= 8:
        block = block[:half] + pltpu.roll(block[half:], 4 * BLK - half, 1)
        half //= 2
    row = lax.broadcasted_iota(jnp.int32, (8, 1), 0)
    for bit in (4, 2, 1):
        block = jnp.where((row & bit) > 0, pltpu.roll(block, 4 * BLK - bit, 1), block)
    return col_sum(block)


def attention_backward(ga, mats, qkv, probs, mixed, wq, xp, grad_one):
    whole = lambda *shape: pl.BlockSpec(shape, lambda r: (0,) * len(shape))
    per = lambda *shape: pl.BlockSpec((1, *shape), lambda r: (r,) + (0,) * len(shape))
    return pl.pallas_call(
        att_bwd_kernel,
        grid=(RANKS,),
        in_specs=[
            whole(L, D),
            pl.BlockSpec((1, PART, D), lambda r: (r, 3, 0)),
            per(L, QKV_ROWS),
            per(HPR, L, L),
            per(L, PART),
            per(D, QKV_ROWS),
            whole(L, D),
            whole(L, D),
        ],
        out_specs=[per(D, D), whole(L, D), per(8, 6 * BLK), per(8, QKV_ROWS)],
        out_shape=[
            jax.ShapeDtypeStruct((RANKS, D, D), BF),
            jax.ShapeDtypeStruct((L, D), F32),
            jax.ShapeDtypeStruct((RANKS, 8, 6 * BLK), F32),
            jax.ShapeDtypeStruct((RANKS, 8, QKV_ROWS), F32),
        ],
        scratch_shapes=[
            pltpu.VMEM((L, L), BF),
            pltpu.VMEM((BLK, 4 * BLK), F32),
            pltpu.VMEM((L, D), F32),
        ],
        compiler_params=pltpu.CompilerParams(vmem_limit_bytes=VMEM_LIMIT),
        name="attention_backward",
    )(ga, mats, qkv, probs, mixed, wq, xp, grad_one)


def aligned_plan(shard, wide, ranks):
    unit = TILE_ROWS * D
    tiles, spare = divmod(shard, unit)
    rows = tiles * TILE_ROWS
    fits = (
        ranks == RANKS
        and spare * wide <= unit
        and rows * wide == MAT_ROWS
        and rows == QKV_ROWS // 2
    )
    return rows, spare, fits


def split_thirds(rows_96x3):
    shape = rows_96x3.shape
    return jnp.swapaxes(rows_96x3.reshape(*shape[:-2], 96, 3, D), -3, -2).reshape(shape)


def join_thirds(rows_3x96):
    shape = rows_3x96.shape
    return jnp.swapaxes(rows_3x96.reshape(*shape[:-2], 3, 96, D), -3, -2).reshape(shape)


def gather_weights(params, wide, ranks):
    shard = params.shape[1]
    rows, spare, fits = aligned_plan(shard, wide, ranks)
    if fits:
        at = lax.axis_index("wide")
        flat = jnp.zeros(((rows + TILE_ROWS) * D,), F32)
        flat = lax.dynamic_update_slice(flat, params[0], (at * spare,))
        block = flat.reshape(rows + TILE_ROWS, D)
        head = jnp.where(at < 2, split_thirds(block[:rows]), block[:rows])
        block = jnp.concatenate([head, block[rows:]], axis=0).astype(BF)
        gathered = lax.all_gather(block, ("narrow", "wide"), axis=0, tiled=True)
        return merge_blocks(gathered.reshape(ranks, wide, rows + TILE_ROWS, D))
    flat = lax.all_gather(params.astype(BF)[0], "wide", axis=0, tiled=True)
    flat = jnp.pad(flat, (0, PAD_ROWS * D - flat.shape[0])).reshape(PAD_ROWS, D)
    head = split_thirds(flat[:QKV_ROWS].reshape(2, QKV_ROWS // 2, D)).reshape(QKV_ROWS, D)
    flat = jnp.concatenate([head, flat[QKV_ROWS:]], axis=0)
    return lax.all_gather(flat, "narrow", axis=0, tiled=True).reshape(ranks, PAD_ROWS, D)


def scatter_grads(grads, shard, wide, ranks):
    rows, spare, fits = aligned_plan(shard, wide, ranks)
    if fits:
        windows = jnp.stack(
            [grads[:, rows * w : rows * (w + 1) + TILE_ROWS] for w in range(wide)], axis=1
        )
        mine = lax.psum_scatter(
            windows.reshape(-1, D), ("narrow", "wide"), scatter_dimension=0, tiled=True
        ).astype(F32)
        at = lax.axis_index("wide")
        head = jnp.where(at < 2, join_thirds(mine[:rows]), mine[:rows])
        flat = jnp.concatenate([head, mine[rows:]], axis=0).reshape(-1)
        return lax.dynamic_slice(flat, (at * spare,), (shard,)).reshape(1, shard)
    mine = lax.psum_scatter(grads.reshape(-1, D), "narrow", scatter_dimension=0, tiled=True)
    head = join_thirds(mine[:QKV_ROWS].reshape(2, QKV_ROWS // 2, D)).reshape(QKV_ROWS, D)
    flat = jnp.concatenate([head, mine[QKV_ROWS:]], axis=0).reshape(-1)[: shard * wide]
    return lax.psum_scatter(flat.astype(F32), "wide", scatter_dimension=0, tiled=True).reshape(1, shard)


def body(hidden_in, out_grad, pair_lengths, params, momentum, average):
    wide, ranks = lax.axis_size("wide"), lax.axis_size("narrow")
    shard = params.shape[1]
    mats = gather_weights(params, wide, ranks)
    qkv, wq, xp, mixed, probs, n1, r1 = attention_forward(pair_lengths[0], hidden_in, mats)
    block_out, d_up, d_down, grad_one, ga, vec_g, up_g = feed_forward(n1, r1, out_grad, mats)
    d_att, in_grad, table_g, qv_g = attention_backward(
        ga, mats, qkv, probs, mixed, wq, xp, grad_one
    )
    near = table_g[:, :HPR, : 4 * BLK]
    left = near[:, :, 0] + jnp.sum(near[:, :, 3 * BLK :], axis=-1) + jnp.sum(
        table_g[:, :HPR, 4 * BLK : 5 * BLK], axis=-1
    )
    right = jnp.sum(near[:, :, 255 : 3 * BLK], axis=-1) + jnp.sum(
        table_g[:, :HPR, 5 * BLK :], axis=-1
    )
    table = jnp.concatenate([left[:, :, None], near[:, :, 1:255], right[:, :, None]], axis=2)
    tail = jnp.concatenate(
        [
            qv_g[:, 0, :PART],
            qv_g[:, 0, 2 * PART :],
            up_g[:, 0],
            jnp.swapaxes(table, 1, 2).reshape(RANKS, -1),
            vec_g[:6].reshape(RANKS, -1),
        ],
        axis=1,
    ).reshape(RANKS, 4, D)
    tail = jnp.pad(tail, ((0, 0), (0, TILE_ROWS - 4), (0, 0))).astype(BF)
    grads = jnp.concatenate([d_att, d_up, d_down, tail], axis=1)
    grad_shard = scatter_grads(grads, shard, wide, ranks)
    device_count = wide * ranks
    step_rate = 1.0 / (32.0 * math.sqrt(hidden_in.shape[0] * device_count))
    new_momentum = 0.5 * momentum + step_rate * grad_shard
    new_params = params - (step_rate * grad_shard + 0.5 * new_momentum)
    new_average = 0.5 * average + 0.5 * new_params
    return (
        block_out,
        in_grad,
        grad_shard,
        new_params,
        new_momentum,
        new_average,
        new_params.astype(BF),
    )


def solution(mesh):
    rows = P(("wide", "narrow"), None)
    flat = P("narrow", "wide")
    return jax.shard_map(
        body,
        mesh=mesh,
        in_specs=(rows, rows, rows, flat, flat, flat),
        out_specs=(rows, rows, flat, flat, flat, flat, flat),
        check_vma=False,
    )
```

time: 1000 us -> 419 us (0.42)
  waiting for transfers between devices: 525 us -> 275 us
  local copies, waits for them, and re-layouts: 266 us -> 25.9 us
  matrix products: 84.2 us -> 0 us
  Pallas kernels: 0 us -> 79.6 us
  other arithmetic: 77.6 us -> 23.8 us
  blocking collectives: 23.5 us -> 0 us
    unnamed x11 -> x2, waiting for transfers between devices: 232 us -> 0.03 us
    dot_general x42 -> x0, matrix products: 84.2 us -> none  [the longest x8 8.6 us: masked_logits(): jnp.einsum('ihd,jhd->hij', query_heads, key_heads, preferred_element_type...]
    pallas_call x0 -> x4, Pallas kernels: none -> 79.6 us  [the longest x1 26.7 us: feed_forward(): pl.pallas_call(ffn_kernel, grid=(2 * RANKS,), in_specs=[whole(L, D), whol...]
    reshape x18 -> x8, local copies, waits for them, and re-layouts: 84.6 us -> 6.59 us  [the longest x1 4.91 us: scatter_grads(): return lax.dynamic_slice(flat, (at * spare,), (shard,)).reshape(1, shard)]
    all_gather x5 -> x1, waiting for transfers between devices: 165 us -> 109 us  [gather_weights(): gathered = lax.all_gather(block, ('narrow', 'wide'), axis=0, tiled=True)]
    slice x22 -> x10, local copies, waits for them, and re-layouts: 56.6 us -> 3.41 us  [the longest x1 1.14 us: scatter_grads(): head = jnp.where(at < 2, join_thirds(mine[:rows]), mine[:rows])]
    concatenate x1, local copies, waits for them, and re-layouts: 50.5 us -> 0.1 us  [body(): jnp.concatenate([qv_g[:, 0, :PART], qv_g[:, 0, 2 * PART:], up_g[:, 0], jn...]
    reduce_scatter x4 -> x1, waiting for transfers between devices: 129 us -> 166 us  [scatter_grads(): lax.psum_scatter(windows.reshape(-1, D), ('narrow', 'wide'), scatter_dime...]
  transfers between devices with their start and end apart: 10 -> 2, of which waited for: 8 -> 2; matrix products, arithmetic and copies ran while one was open for 16% -> 0% of each run, Pallas kernels for 0% -> 0%
where the time goes in v1:
time: 419 us
  waiting for transfers between devices  275 us (66%)
  Pallas kernels  79.6 us (19%)
  local copies, waits for them, and re-layouts  25.9 us (6%)
  other arithmetic  23.8 us (6%)
  between operations  14.4 us (3%)
    reduce_scatter x1, waiting for transfers between devices, scatter_grads(): lax.psum_scatter(windows.reshape(-1, D), ('narrow', 'wide'), scatter_dime...  166 us
    all_gather x1, waiting for transfers between devices, gather_weights(): gathered = lax.all_gather(block, ('narrow', 'wide'), axis=0, tiled=True)  109 us
    pallas_call x1, Pallas kernels, feed_forward(): pl.pallas_call(ffn_kernel, grid=(2 * RANKS,), in_specs=[whole(L, D), whol...  26.7 us
    pallas_call x1, Pallas kernels, attention_backward(): pl.pallas_call(att_bwd_kernel, grid=(RANKS,), in_specs=[whole(L, D), pl.B...  24 us
    pallas_call x1, Pallas kernels, attention_forward(): pl.pallas_call(att_fwd_kernel, grid_spec=pltpu.PrefetchScalarGridSpec(num...  18.6 us
    unnamed x5, other arithmetic  11.4 us
    pallas_call x1, Pallas kernels, merge_blocks(): pl.pallas_call(functools.partial(merge_kernel, wide, cap - TILE_ROWS), gr...  10.3 us
  transfers between devices with their start and end apart: 2, of which 2 were waited for; matrix products, arithmetic and copies ran while one was open for 0% of the time, Pallas kernels for 0%

profile of v1, /device:TPU:0, one launch (start us, length us, event | category | flops | bytes accessed | tf_op | source)
XLA Modules:
  0.0 418.9 jit_solution(17273297930425419271)
XLA Ops:
  7.2 9.3 %reduce = bf16[221568]{0:T(1024)(128)(2,1)S(1)} reduce(f32[1,221568]{1,0:T(1,128)} %param.9, f32[]{:T(128)} %constant.30), dimensions={0}, to_apply=%param.9.reduce_sub_computation | reduce | bytes 1329412 | tf_op args[3]
  16.6 4.1 dynamic_update_slice.3
  21.6 0.8 pad_maximum_fusion.3
  22.6 108.6 %all-gather.2.cloned.1.call-done = bf16[9728,768]{1,0:T(8,128)(2,1)} async-done(((bf16[304,768]{1,0:T(8,128)(2,1)}), bf16[9728,768]{1,0:T(8,128)(2,1)}) %all-gather.2.cloned.1.call-update) | async-done | bytes 14942224 | tf_op jit(solution)/shard_map/all_gather | solution.py:519
  131.2 10.3 %merge_weights.1.mq_ref.wo_ref.tail_ref.up_ref.down_ref = bf16[4,2320,768]{2,1,0:T(8,128)(2,1)} custom-call(bf16[4,8,304,768]{3,2,1,0:T(8,128)(2,1)} %bitcast.52), custom_call_target="tpu_custom_call" | custom-call | tf_op jit(solution)/shard_map/merge_weights/pallas_call | solution.py:99
  141.5 18.6 %attention_forward.1 = (bf16[4,512,576]{2,1,0:T(8,128)(2,1)}, bf16[4,768,576]{2,1,0:T(8,128)(2,1)}, bf16[512,768]{1,0:T(8,128)(2,1)}, bf16[4,512,192]{2,1,0:T(8,...) custom-call(s32[4]{0:T(128)} %bitcast.59, bf16[512,768]{1,0:T(8,128)(2,1)} %x_ref.1, ...), custom_call_target="tpu_custom_call" | custom-call | tf_op jit(solution)/shard_map/attention_forward/pallas_call | solution.py:212
  160.1 26.7 %feed_forward.1 = (bf16[512,768]{1,0:T(8,128)(2,1)}, bf16[4,768,768]{2,1,0:T(8,128)(2,1)}, bf16[4,768,768]{2,1,0:T(8,128)(2,1)}, f32[512,768]{1,0:T(8,128)}, bf1...) custom-call(f32[512,768]{1,0:T(8,128)} %get-tuple-element.25.n1_ref, ...), custom_call_target="tpu_custom_call" | custom-call | tf_op jit(solution)/shard_map/feed_forward/pallas_call | solution.py:329
  186.8 24.0 %attention_backward.1 = (bf16[4,768,768]{2,1,0:T(8,128)(2,1)}, f32[512,768]{1,0:T(8,128)}, f32[4,8,768]{2,1,0:T(8,128)}, f32[4,8,576]{2,1,0:T(8,128)}) custom-call(bf16[512,768]{1,0:T(8,128)(2,1)} %get-tuple-element.28.ga_ref, bf16[4,2320,768]{2,1,0:T(8,128)(2,1)} %merge_weights.1.mq_ref.wo_ref.tail_ref.up_ref.down_ref, ...), custom_call_target="tpu_custom_call" | custom-call | tf_op jit(solution)/shard_map/attention_backward/pallas_call | solution.py:456
  210.8 1.0 slice_reduce_fusion
  211.8 0.8 slice_reduce_fusion.3
  212.6 0.9 slice.154
  213.9 0.9 slice.155
  214.8 0.9 convert.45
  215.7 0.7 add_convert_fusion
  217.2 1.8 bitcast_dynamic-update-slice_fusion.4
  219.0 1.8 bitcast_dynamic-update-slice_fusion.3
  220.9 2.0 fusion.7
  222.9 0.7 slice-done.1
  224.3 6.3 %copy.35 = bf16[4,8,304,768]{3,2,1,0:T(8,128)(2,1)} copy(bf16[4,8,304,768]{3,2,0,1:T(8,128)(2,1)S(1)} %fusion.3) | data formatting | bytes 29884416 | tf_op jit(solution)/shard_map/stack | solution.py:531
  230.6 166.4 %reduce-scatter.2.cloned.1.call-done = bf16[304,768]{1,0:T(8,128)(2,1)} async-done(((bf16[9728,768]{1,0:T(8,128)(2,1)}), bf16[304,768]{1,0:T(8,128)(2,1)}) %reduce-scatter.2.cloned.1.call-update) | async-done | bytes 466960 | tf_op jit(solution)/shard_map/reduce_scatter | solution.py:534
  397.0 1.1 slice.135
  399.9 4.9 %reshape.97 = f32[1,221568]{1,0:T(1,128)} reshape(f32[221568]{0:T(1024)S(1)} %get-tuple-element.50) | data formatting | bytes 1772544 | tf_op jit(solution)/shard_map/reshape | solution.py:540
  404.8 5.3 %fusion.10 = (bf16[1,221568]{1,0:T(2,128)(2,1)}, f32[1,221568]{1,0:T(1,128)S(1)}, f32[1,221568]{1,0:T(1,128)}) fusion(f32[1,221568]{1,0:T(1,128)S(1)} %copy-done.3, f32[221568]{0:T(1024)S(1)} %get-tuple-element.49, f32[1,221568]{1,0:T(1,128)S(1)} %copy-done.4), kind=kLoop, calls=%fused_computation.41 | loop fusion | flops 1329408 | bytes 4874496 | tf_op jit(solution)/shard_map/convert_element_type | solution.py:589
  410.2 1.9 add_multiply_fusion
  (62 shorter events, 4.6 us)
Async XLA Ops:
  7.2 124.0 %all-gather.2.cloned.1.call-start = ((), (), s32[]{:S(2)}) async-start(), calls=%async_computation.1 | async-start | bytes 15409152 | tf_op jit(solution)/shard_map/all_gather | solution.py:519
  22.4 374.6 %reduce-scatter.2.cloned.1.call-start = ((), (), s32[]{:S(2)}) async-start(), calls=%async_computation.2 | async-start | bytes 15409152 | tf_op jit(solution)/shard_map/reduce_scatter | solution.py:534
  186.8 27.9 %copy-start.6 = (f32[8,768]{1,0:T(8,128)S(1)}, f32[8,768]{1,0:T(8,128)}, u32[]{:S(2)}) copy-start(f32[8,768]{1,0:T(8,128)} %get-tuple-element.42) | copy-start | bytes 73732
  217.2 3.7 copy-start
  219.0 3.9 slice-start
  219.0 4.8 %slice-start.2 = ((s8[4718592]{0:T(1024)(128)(4,1)}), s8[4194304]{0:T(1024)(128)(4,1)S(1)}, s32[]{:S(2)}) async-start(s8[4718592]{0:T(1024)(128)(4,1)} %bitcast.50), calls=%async_computation.5 | async-start | bytes 8388608
  220.9 2.7 slice-start.1
  220.9 3.0 slice-start.3
  397.0 2.2 copy-start.1
  399.4 5.4 %copy-start.3 = (f32[1,221568]{1,0:T(1,128)S(1)}, f32[1,221568]{1,0:T(1,128)}, u32[]{:S(2)}) copy-start(f32[1,221568]{1,0:T(1,128)} %param.9) | copy-start | bytes 2658820
  399.6 5.3 %copy-start.4 = (f32[1,221568]{1,0:T(1,128)S(1)}, f32[1,221568]{1,0:T(1,128)}, u32[]{:S(2)}) copy-start(f32[1,221568]{1,0:T(1,128)} %param.10) | copy-start | bytes 2658820
  399.6 10.6 %copy-start.5 = (f32[1,221568]{1,0:T(1,128)S(1)}, f32[1,221568]{1,0:T(1,128)}, u32[]{:S(2)}) copy-start(f32[1,221568]{1,0:T(1,128)} %param.11) | copy-start | bytes 2658820
  410.2 1.9 copy-start.2
Sparse Core Ops, SparseCore 0:
  22.5 108.6 all-gather.1
  230.7 166.2 reduce-scatter.1

commit v2 on v1

v2 whole, which is shorter than its diff:
```python
import functools
import math

import jax
import jax.numpy as jnp
from jax import lax
from jax.experimental import pallas as pl
from jax.experimental.pallas import tpu as pltpu
from jax.sharding import PartitionSpec as P

D = 768
HEADS = 12
FF = 3072
HD = 64
BUCKETS = 256
L = 512
RANKS = 4
PART = D // RANKS
HPR = HEADS // RANKS
SLOTS = 2
QKV_ROWS = 3 * PART
TILE_ROWS = 16
MAT_ROWS = 3 * D
PAD_ROWS = MAT_ROWS + TILE_ROWS
ATT_ROWS = D + TILE_ROWS
FF_ROWS = 2 * D
BLK = 128
NBLK = L // BLK
NEG = -1000000000.0
VMEM_LIMIT = 60 * 1024 * 1024
BF = jnp.bfloat16
F32 = jnp.float32


def mm(a, b):
    return jnp.dot(a, b, preferred_element_type=F32)


def mm_nt(a, b):
    return lax.dot_general(a, b, (((1,), (1,)), ((), ())), preferred_element_type=F32)


def mm_tn(a, b):
    return lax.dot_general(a, b, (((0,), (0,)), ((), ())), preferred_element_type=F32)


def qkv_pieces():
    for b in range(2):
        for j in range(4):
            for c in range(3):
                t, q = divmod(3 * j + c, 4)
                yield 288 * b + 96 * t, PART * q, PART * j + 96 * b, PART * c


def column_order():
    d = lax.broadcasted_iota(jnp.int32, (D, D), 0)
    n = lax.broadcasted_iota(jnp.int32, (D, D), 1)
    j = (n >= PART).astype(jnp.int32) + (n >= 2 * PART).astype(jnp.int32) + (n >= 3 * PART).astype(jnp.int32)
    return (d == 4 * (n - PART * j) + j).astype(F32).astype(BF)


def slot_of(r, place_ref):
    return ((r // 2) ^ place_ref[1]) + 2 * ((r % 2) ^ place_ref[2])


def slice_of(slot, place_ref):
    return 2 * ((slot % 2) ^ place_ref[1]) + ((slot // 2) ^ place_ref[2])


def vector_rows(tails_ref, place_ref):
    chunks = []
    for r in range(RANKS):
        k = slot_of(r, place_ref)
        chunks.append(tails_ref[k, 2:3, 384:768])
        chunks.append(tails_ref[k, 3:4, 0:384])
        chunks.append(tails_ref[k, 3:4, 384:768])
    return [
        jnp.concatenate([chunks[2 * v], chunks[2 * v + 1]], axis=1).astype(F32) for v in range(6)
    ]


def table_order():
    src = lax.broadcasted_iota(jnp.int32, (D, D), 0)
    dst = lax.broadcasted_iota(jnp.int32, (D, D), 1)
    hh = (dst >= BUCKETS).astype(jnp.int32) + (dst >= 2 * BUCKETS).astype(jnp.int32)
    return (src == 3 * (dst - BUCKETS * hh) + hh).astype(F32).astype(BF)


def normalize(values):
    centred = values - jnp.mean(values, axis=-1, keepdims=True)
    inv = lax.rsqrt(jnp.mean(centred * centred, axis=-1, keepdims=True) + 1e-05)
    return centred * inv, inv


def norm_backward(e, normed, inv):
    return inv * (
        e - jnp.mean(e, axis=-1, keepdims=True) - normed * jnp.mean(e * normed, axis=-1, keepdims=True)
    )


def col_sum(values):
    return jnp.sum(values, axis=0, keepdims=True)


def call(kernel, name, grid, in_specs, out_specs, out_shape, scratch, args, vmem=VMEM_LIMIT, flops=0, moved=0):
    return pl.pallas_call(
        kernel,
        grid_spec=pltpu.PrefetchScalarGridSpec(
            num_scalar_prefetch=1,
            grid=grid,
            in_specs=in_specs,
            out_specs=out_specs,
            scratch_shapes=scratch,
        ),
        out_shape=out_shape,
        compiler_params=pltpu.CompilerParams(vmem_limit_bytes=vmem),
        cost_estimate=pl.CostEstimate(flops=flops, bytes_accessed=moved, transcendentals=0),
        name=name,
    )(*args)


def whole(*shape):
    return pl.BlockSpec(shape, lambda *_: (0,) * len(shape))


def shaped(dtype, *shape):
    return jax.ShapeDtypeStruct(shape, dtype)


def block_kernel(rows, lead, shift, place_ref, flat_ref, out_ref, rows_s):
    w = place_ref[0]
    count = flat_ref.shape[1] // 128
    rows_s[0:lead, :] = jnp.zeros((lead, 128), F32)
    rows_s[lead : lead + count, :] = flat_ref[...].reshape(count, 128)
    rows_s[lead + count :, :] = jnp.zeros((rows_s.shape[0] - lead - count, 128), F32)
    start = lead - shift * w
    third = rows // 3

    @pl.when(w < 2)
    def _():
        for t in range(3):
            for c in range(6):
                out_ref[third * t : third * (t + 1), 128 * c : 128 * (c + 1)] = rows_s[
                    pl.ds(start + 6 * t + c, third, stride=18), :
                ].astype(BF)

    @pl.when(w >= 2)
    def _():
        for c in range(6):
            out_ref[0:rows, 128 * c : 128 * (c + 1)] = rows_s[
                pl.ds(start + c, rows, stride=6), :
            ].astype(BF)

    for c in range(6):
        out_ref[rows : rows + TILE_ROWS, 128 * c : 128 * (c + 1)] = rows_s[
            pl.ds(start + 6 * rows + c, TILE_ROWS, stride=6), :
        ].astype(BF)


def own_block(place, params, rows, spare, wide):
    count = params.shape[1] // 128
    lead = spare // 128 * wide
    total = -(-(lead + 6 * (rows + TILE_ROWS)) // 8) * 8
    return call(
        functools.partial(block_kernel, rows, lead, spare // 128),
        "own_block", (1,),
        [whole(*params.shape)],
        whole(rows + TILE_ROWS, D),
        shaped(BF, rows + TILE_ROWS, D),
        [pltpu.VMEM((total, 128), F32)],
        (place, params),
        vmem=16 * 1024 * 1024,
    )


def update_kernel(
    rows, lead, shift, rate, place_ref, kept_ref, near_ref, second_ref, ring_ref, params_ref, momentum_ref, average_ref,
    grads_ref, new_params_ref, new_momentum_ref, new_average_ref, low_ref, rows_s,
):
    w = place_ref[0]
    count = params_ref.shape[1] // 128
    block = (
        kept_ref[...].astype(F32) + near_ref[0].astype(F32) + second_ref[...].astype(F32) + ring_ref[...].astype(F32)
    )
    start = lead - shift * w
    third = rows // 3

    @pl.when(w < 2)
    def _():
        for t in range(3):
            for c in range(6):
                rows_s[pl.ds(start + 6 * t + c, third, stride=18), :] = block[
                    third * t : third * (t + 1), 128 * c : 128 * (c + 1)
                ]

    @pl.when(w >= 2)
    def _():
        for c in range(6):
            rows_s[pl.ds(start + c, rows, stride=6), :] = block[0:rows, 128 * c : 128 * (c + 1)]

    for c in range(6):
        rows_s[pl.ds(start + 6 * rows + c, TILE_ROWS, stride=6), :] = block[
            rows : rows + TILE_ROWS, 128 * c : 128 * (c + 1)
        ]
    grads = rows_s[lead : lead + count, :].reshape(params_ref.shape)
    grads_ref[...] = grads
    params = params_ref[...]
    new_momentum = 0.5 * momentum_ref[...] + rate * grads
    new_params = params - (rate * grads + 0.5 * new_momentum)
    new_momentum_ref[...] = new_momentum
    new_params_ref[...] = new_params
    new_average_ref[...] = 0.5 * average_ref[...] + 0.5 * new_params
    low_ref[...] = new_params.astype(BF)


def update_shard(place, parts, params, momentum, average, rate, rows, spare, wide):
    count = params.shape[1] // 128
    lead = spare // 128 * wide
    total = -(-(lead + 6 * (rows + TILE_ROWS)) // 8) * 8
    kept, near, second, ring = parts
    cap = rows + TILE_ROWS
    flat = whole(*params.shape)
    return call(
        functools.partial(update_kernel, rows, lead, spare // 128, rate),
        "update_shard", (1,),
        [whole(cap, D), pl.BlockSpec((1, cap, D), lambda *_: (1, 0, 0)), whole(cap, D), whole(cap, D), flat, flat, flat],
        [flat] * 5,
        [shaped(F32, *params.shape)] * 4 + [shaped(BF, *params.shape)],
        [pltpu.VMEM((total, 128), F32)],
        (place, kept, near, second, ring, params, momentum, average),
        vmem=32 * 1024 * 1024,
    )


def merge_kernel(rows, at_ref, *refs):
    pieces, (att_ref, ff_ref), (mats, edges, in_sem, out_sem) = refs[:16], refs[16:18], refs[18:]
    copies = {}
    for slot in range(SLOTS):
        for i in range(8):
            w = at_ref[i]
            piece = pieces[8 * slot + i]
            main = pltpu.make_async_copy(
                piece.at[0:rows],
                mats.at[slot, pl.ds(pl.multiple_of(rows * w, TILE_ROWS), rows)],
                in_sem.at[slot, i, 0],
            )
            edge = pltpu.make_async_copy(
                piece.at[rows : rows + TILE_ROWS], edges.at[slot, w], in_sem.at[slot, i, 1]
            )
            main.start()
            edge.start()
            copies[slot, i] = (main, edge)
    outs = []
    for slot in range(SLOTS):
        for i in range(8):
            for c in copies[slot, i]:
                c.wait()
        for w in range(1, 8):
            at = rows * w
            mats[slot, at : at + TILE_ROWS, :] = mats[slot, at : at + TILE_ROWS, :] + edges[slot, w - 1]
        mats[slot, MAT_ROWS:PAD_ROWS, :] = edges[slot, 7]
        for n, (src, dst) in enumerate(
            (
                (mats.at[slot, 0:D], att_ref.at[slot, 0:D]),
                (mats.at[slot, MAT_ROWS:PAD_ROWS], att_ref.at[slot, D:ATT_ROWS]),
                (mats.at[slot, D:MAT_ROWS], ff_ref.at[slot]),
            )
        ):
            copy = pltpu.make_async_copy(src, dst, out_sem.at[slot, n])
            copy.start()
            outs.append(copy)
    for copy in outs:
        copy.wait()


def merge_blocks(at, pieces, rows):
    hbm = pl.BlockSpec(memory_space=pl.ANY)
    return call(
        functools.partial(merge_kernel, rows),
        "merge_weights", (1,),
        [hbm] * 16,
        [hbm] * 2,
        [shaped(BF, SLOTS, ATT_ROWS, D), shaped(BF, SLOTS, FF_ROWS, D)],
        [
            pltpu.VMEM((SLOTS, PAD_ROWS, D), BF),
            pltpu.VMEM((SLOTS, 8, TILE_ROWS, D), BF),
            pltpu.SemaphoreType.DMA((SLOTS, 8, 2)),
            pltpu.SemaphoreType.DMA((SLOTS, 3)),
        ],
        (at, *pieces),
    )


def window_kernel(rows, kinds, at_ref, own_att, own_ff, got_att, got_ff, *refs):
    outs, (own_s, got_s, own_sem, got_sem) = refs[:-4], refs[-4:]
    cap = rows + TILE_ROWS

    def fetch(w, slot, att, ff, buf, sem):
        @pl.when(w < 2)
        def _():
            src = att.at[slot, pl.ds(pl.multiple_of(rows * w, TILE_ROWS), cap)]
            pltpu.make_async_copy(src, buf, sem).start()

        @pl.when(w == 2)
        def _():
            pltpu.make_async_copy(att.at[slot, 2 * rows : D], buf.at[0 : D - 2 * rows], sem).start()
            pltpu.make_async_copy(ff.at[slot, 0 : 3 * rows + TILE_ROWS - D], buf.at[D - 2 * rows : cap], sem).start()

        @pl.when((w > 2) & (w < 7))
        def _():
            src = ff.at[slot, pl.ds(pl.multiple_of(rows * w - D, TILE_ROWS), cap)]
            pltpu.make_async_copy(src, buf, sem).start()

        @pl.when(w == 7)
        def _():
            pltpu.make_async_copy(ff.at[slot, 7 * rows - D : FF_ROWS], buf.at[0:rows], sem).start()
            pltpu.make_async_copy(att.at[slot, D:ATT_ROWS], buf.at[rows:cap], sem).start()

    windows = [(q, xo, slot) for q in range(len(kinds)) for xo in range(2) for slot in range(SLOTS)]
    for n, (q, xo, slot) in enumerate(windows):
        w = at_ref[2 * q + xo]
        fetch(w, slot, own_att, own_ff, own_s.at[n], own_sem.at[n])
        fetch(w, slot, got_att, got_ff, got_s.at[n], got_sem.at[n])
    for n, (q, xo, slot) in enumerate(windows):
        pltpu.make_async_copy(own_ff.at[0, 0:cap], own_s.at[n], own_sem.at[n]).wait()
        pltpu.make_async_copy(own_ff.at[0, 0:cap], got_s.at[n], got_sem.at[n]).wait()
        total = (own_s[n].astype(F32) + got_s[n].astype(F32)).astype(BF)
        send, pass_on, keep = outs[3 * q : 3 * q + 3]
        if xo == 0 and slot == 0:
            keep[...] = total
        elif xo == 1 and slot == 1:
            send[0] = total
        elif (slot == 1) == (kinds[q] == "y"):
            send[1] = total
        else:
            pass_on[...] = total


def split_windows(at, kinds, own, got, rows):
    hbm = pl.BlockSpec(memory_space=pl.ANY)
    cap = rows + TILE_ROWS
    n = 4 * len(kinds)
    outs = call(
        functools.partial(window_kernel, rows, kinds),
        "split_windows", (1,),
        [hbm] * 4,
        [whole(2, cap, D), whole(cap, D), whole(cap, D)] * len(kinds),
        [shaped(BF, 2, cap, D), shaped(BF, cap, D), shaped(BF, cap, D)] * len(kinds),
        [
            pltpu.VMEM((n, cap, D), BF),
            pltpu.VMEM((n, cap, D), BF),
            pltpu.SemaphoreType.DMA((n,)),
            pltpu.SemaphoreType.DMA((n,)),
        ],
        (at, *own, *got),
    )
    return [outs[3 * q : 3 * q + 3] for q in range(len(kinds))]


def segment_of(pos, len_ref):
    end0 = len_ref[0]
    end1 = end0 + len_ref[1]
    end2 = end1 + len_ref[2]
    return (
        (pos >= end0).astype(jnp.int32)
        + (pos >= end1).astype(jnp.int32)
        + (pos >= end2).astype(jnp.int32)
    )


def att_fwd_kernel(
    scal_ref, x_ref, mq0_ref, wo0_ref, mq1_ref, wo1_ref, tails_ref,
    qkv_ref, wq_ref, mixed_ref, probs_ref, xp_ref, n1_ref, r1_ref,
    table_s, acc_s, wo_s,
):
    s = pl.program_id(0)
    len_ref = scal_ref

    @pl.when(s == 0)
    def _():
        xp_ref[...] = mm(x_ref[...], column_order()).astype(BF)
        acc_s[...] = jnp.zeros_like(acc_s)
        flat = jnp.concatenate(
            [
                jnp.concatenate([tails_ref[k, 1:2, 384:768], tails_ref[k, 2:3, 0:384]], axis=1).astype(F32)
                for k in range(RANKS)
            ]
            + [jnp.zeros((8 - RANKS, D), F32)],
            axis=0,
        ).astype(BF)
        tables = mm(flat, table_order())
        for k in range(RANKS):
            for h in range(HPR):
                row = tables[k : k + 1, BUCKETS * h : BUCKETS * (h + 1)]
                table_s[k, h : h + 1, :] = jnp.concatenate(
                    [
                        row,
                        jnp.broadcast_to(row[:, 255:256], (1, BLK)),
                        jnp.broadcast_to(row[:, 0:1], (1, BLK)),
                    ],
                    axis=1,
                )

    def load(mq_ref, wo_ref):
        for src_row, src_col, dst_row, dst_col in qkv_pieces():
            wq_ref[0, dst_row : dst_row + 96, dst_col : dst_col + PART] = mq_ref[
                0, src_row : src_row + 96, src_col : src_col + PART
            ]
        wo_s[...] = wo_ref[0]

    @pl.when(s < SLOTS)
    def _():
        load(mq0_ref, wo0_ref)

    @pl.when(s >= SLOTS)
    def _():
        load(mq1_ref, wo1_ref)

    first = tails_ref[s, 0:1, :]
    bias = jnp.concatenate(
        [first[:, 0:PART], jnp.zeros((1, PART), BF), first[:, PART : 2 * PART]], axis=1
    ).astype(F32)
    qkv = (mm(xp_ref[...], wq_ref[0]) + bias).astype(BF)
    qkv_ref[0] = qkv

    seg_j = segment_of(lax.broadcasted_iota(jnp.int32, (1, L), 1), len_ref)
    table = table_s[s]
    heads = []
    for h in range(HPR):
        q = qkv[:, HD * h : HD * (h + 1)]
        k = qkv[:, PART + HD * h : PART + HD * (h + 1)]
        v = qkv[:, 2 * PART + HD * h : 2 * PART + HD * (h + 1)]
        row = table[h : h + 1, :]
        near = pltpu.roll(jnp.broadcast_to(row, (BLK, 4 * BLK)), 0, 1, stride=1, stride_axis=0)
        far_right = jnp.broadcast_to(row[:, 255:256], (BLK, BLK))
        far_left = jnp.broadcast_to(row[:, 511:512], (BLK, BLK))
        for i in range(NBLK):
            seg_i = segment_of(
                lax.broadcasted_iota(jnp.int32, (BLK, 1), 0) + BLK * i, len_ref
            )
            parts = []
            for jb in range(NBLK):
                delta = jb - i
                if abs(delta) <= 1:
                    parts.append(near[:, BLK * (delta + 1) : BLK * (delta + 2)])
                else:
                    parts.append(far_right if delta > 0 else far_left)
            logits = mm_nt(q[BLK * i : BLK * (i + 1)], k) * 0.125 + jnp.concatenate(parts, axis=1)
            logits = jnp.where(seg_i == seg_j, logits, NEG)
            top = jnp.max(logits, axis=-1, keepdims=True)
            expo = jnp.exp(logits - top)
            total = jnp.sum(expo, axis=-1, keepdims=True)
            probs_ref[0, h, BLK * i : BLK * (i + 1), :] = (expo * (1.0 / total)).astype(BF)
        heads.append(mm(probs_ref[0, h], v))
    mixed = jnp.concatenate(heads, axis=1).astype(BF)
    mixed_ref[0] = mixed
    acc_s[...] += mm(mixed, wo_s[...])

    @pl.when(s == RANKS - 1)
    def _():
        vec = vector_rows(tails_ref, PlaceView(scal_ref))
        normed, inv = normalize(x_ref[...].astype(F32) + acc_s[...] + vec[0])
        n1_ref[...] = normed
        r1_ref[...] = jnp.broadcast_to(inv, (L, BLK))


class PlaceView:
    def __init__(self, ref):
        self.ref = ref

    def __getitem__(self, i):
        return self.ref[4 + i]


def attention_forward(scalars, x, own_att, got_att, tails):
    per = lambda *shape: pl.BlockSpec((1, *shape), lambda s, n: (s,) + (0,) * len(shape))
    own = lambda rows, at: pl.BlockSpec((1, rows, D), lambda s, n: (jnp.minimum(s, 1), at, 0))
    got = lambda rows, at: pl.BlockSpec((1, rows, D), lambda s, n: (jnp.maximum(s - 2, 0), at, 0))
    return call(
        att_fwd_kernel,
        "attention_forward", (RANKS,),
        [
            whole(L, D),
            own(QKV_ROWS, 0), own(PART, QKV_ROWS // PART),
            got(QKV_ROWS, 0), got(PART, QKV_ROWS // PART),
            whole(RANKS, TILE_ROWS, D),
        ],
        [per(L, QKV_ROWS), per(D, QKV_ROWS), per(L, PART), per(HPR, L, L), whole(L, D), whole(L, D), whole(L, BLK)],
        [
            shaped(BF, RANKS, L, QKV_ROWS),
            shaped(BF, RANKS, D, QKV_ROWS),
            shaped(BF, RANKS, L, PART),
            shaped(BF, RANKS, HPR, L, L),
            shaped(BF, L, D),
            shaped(F32, L, D),
            shaped(F32, L, BLK),
        ],
        [pltpu.VMEM((RANKS, 8, 512), F32), pltpu.VMEM((L, D), F32), pltpu.VMEM((PART, D), BF)],
        (scalars, x, own_att, own_att, got_att, got_att, tails),
        flops=6_000_000_000, moved=24_000_000,
    )


def ffn_kernel(
    place_ref, n1_ref, r1_ref, og_ref, up0_ref, down0_ref, up1_ref, down1_ref, tails_ref,
    block_ref, grad0_ref, grad1_ref, grad_one_ref, ga_ref, vec_ref, bup_ref,
    fn_s, fl_s, up_s, act_s, down_s, gd_s, gf_s,
):
    step = pl.program_id(0)
    inv_root2 = 1.0 / math.sqrt(2.0)

    @pl.when(step == 0)
    def _():
        vec = vector_rows(tails_ref, place_ref)
        first = n1_ref[...] * vec[2] + vec[3]
        fn_s[...] = first
        fl_s[...] = first.astype(BF)
        down_s[...] = jnp.zeros_like(down_s)

    def forward(slot, up_ref, down_ref):
        bias = jnp.concatenate([tails_ref[slot, 0:1, 384:768], tails_ref[slot, 1:2, 0:384]], axis=1)
        up = mm(fl_s[...], up_ref[0]) + bias.astype(F32)
        up_s[slot] = up
        act = (0.5 * up * (1.0 + lax.erf(up * inv_root2))).astype(BF)
        act_s[slot] = act
        down_s[...] += mm(act, down_ref[0])

    @pl.when(step < 2)
    def _():
        forward(step, up0_ref, down0_ref)

    @pl.when((step == 2) | (step == 3))
    def _():
        forward(step, up1_ref, down1_ref)

    @pl.when(step == RANKS)
    def _():
        vec = vector_rows(tails_ref, place_ref)
        normed, inv = normalize(fn_s[...] + down_s[...] + vec[1])
        block_ref[...] = (normed * vec[4] + vec[5]).astype(BF)
        og = og_ref[...].astype(F32)
        vec_ref[4:5, :] = col_sum(og * normed)
        vec_ref[5:6, :] = col_sum(og)
        grad_two = norm_backward(og * vec[4], normed, inv)
        low = grad_two.astype(BF)
        gd_s[...] = low
        vec_ref[1:2, :] = col_sum(low.astype(F32))
        vec_ref[6:8, :] = jnp.zeros((2, D), F32)
        gf_s[...] = grad_two

    def backward(slot, up_ref, down_ref, grad_ref):
        gd = gd_s[...]
        grad_ref[0, D:FF_ROWS, :] = mm_tn(act_s[slot], gd).astype(BF)
        up = up_s[slot]
        slope = 0.5 * (1.0 + lax.erf(up * inv_root2)) + up * jnp.exp(-0.5 * up * up) * (
            1.0 / math.sqrt(2.0 * math.pi)
        )
        gu = (mm_nt(gd, down_ref[0]) * slope).astype(BF)
        bup_ref[0, 0:1, :] = col_sum(gu.astype(F32))
        bup_ref[0, 1:8, :] = jnp.zeros((7, D), F32)
        grad_ref[0, 0:D, :] = mm_tn(fl_s[...], gu).astype(BF)
        gf_s[...] += mm_nt(gu, up_ref[0])

    @pl.when((step == 4) | (step == 5))
    def _():
        backward(step - 2, up1_ref, down1_ref, grad1_ref)

    @pl.when(step >= 6)
    def _():
        backward(step - 6, up0_ref, down0_ref, grad0_ref)

    @pl.when(step == 2 * RANKS - 1)
    def _():
        vec = vector_rows(tails_ref, place_ref)
        f = gf_s[...]
        normed = n1_ref[...]
        vec_ref[2:3, :] = col_sum(f * normed)
        vec_ref[3:4, :] = col_sum(f)
        grad_one = norm_backward(f * vec[2], normed, r1_ref[:, 0:1])
        grad_one_ref[...] = grad_one
        low = grad_one.astype(BF)
        ga_ref[...] = low
        vec_ref[0:1, :] = col_sum(low.astype(F32))


def feed_forward(place, n1, r1, out_grad, own_ff, got_ff, tails):
    def own_at(half):
        return lambda s, n: ((((s >= 1) & (s <= 3)) | (s == 7)).astype(jnp.int32), half, 0)

    def got_at(half):
        return lambda s, n: (((s == 3) | (s >= 5)).astype(jnp.int32), half, 0)

    wt = lambda index: pl.BlockSpec((1, D, D), index)
    return call(
        ffn_kernel,
        "feed_forward", (2 * RANKS,),
        [
            whole(L, D), whole(L, BLK), whole(L, D),
            wt(own_at(0)), wt(own_at(1)), wt(got_at(0)), wt(got_at(1)),
            whole(RANKS, TILE_ROWS, D),
        ],
        [
            whole(L, D),
            pl.BlockSpec((1, FF_ROWS, D), lambda s, n: ((s >= 7).astype(jnp.int32), 0, 0)),
            pl.BlockSpec((1, FF_ROWS, D), lambda s, n: ((s >= 5).astype(jnp.int32), 0, 0)),
            whole(L, D), whole(L, D), whole(8, D),
            pl.BlockSpec((1, 8, D), lambda s, n: (lax.rem(jnp.maximum(s, 4) - 2, 4), 0, 0)),
        ],
        [
            shaped(BF, L, D),
            shaped(BF, SLOTS, FF_ROWS, D),
            shaped(BF, SLOTS, FF_ROWS, D),
            shaped(F32, L, D),
            shaped(BF, L, D),
            shaped(F32, 8, D),
            shaped(F32, RANKS, 8, D),
        ],
        [
            pltpu.VMEM((L, D), F32),
            pltpu.VMEM((L, D), BF),
            pltpu.VMEM((RANKS, L, D), F32),
            pltpu.VMEM((RANKS, L, D), BF),
            pltpu.VMEM((L, D), F32),
            pltpu.VMEM((L, D), BF),
            pltpu.VMEM((L, D), F32),
        ],
        (place, n1, r1, out_grad, own_ff, own_ff, got_ff, got_ff, tails),
        flops=14_500_000_000, moved=36_000_000,
    )


def diagonal_sums(block):
    half = block.shape[0] // 2
    while half >= 8:
        block = block[:half] + pltpu.roll(block[half:], 4 * BLK - half, 1)
        half //= 2
    row = lax.broadcasted_iota(jnp.int32, (8, 1), 0)
    for bit in (4, 2, 1):
        block = jnp.where((row & bit) > 0, pltpu.roll(block, 4 * BLK - bit, 1), block)
    return col_sum(block)


def att_bwd_kernel(
    place_ref, ga_ref, wo0_ref, wo1_ref, qkv_ref, probs_ref, mixed_ref, wq_ref, xp_ref, vec_ref, bup_ref, grad_one_ref,
    da0_ref, da1_ref, in_grad_ref,
    ds_s, near_s, sums_s, dx_s, order_s, wo_s, da_s,
):
    s = pl.program_id(0)
    slot = lax.rem(s + SLOTS, RANKS)

    @pl.when(s == 0)
    def _():
        order_s[...] = table_order()
        dx_s[...] = jnp.zeros_like(dx_s)
        sums_s[...] = jnp.zeros_like(sums_s)
        da_s[D:ATT_ROWS, :] = jnp.zeros((TILE_ROWS, D), BF)

    @pl.when(slot < SLOTS)
    def _():
        wo_s[...] = wo0_ref[0]

    @pl.when(slot >= SLOTS)
    def _():
        wo_s[...] = wo1_ref[0]

    ga = ga_ref[...]
    da_s[QKV_ROWS:D, :] = mm_tn(mixed_ref[0], ga).astype(BF)
    dm_all = mm_nt(ga, wo_s[...]).astype(BF)
    qkv = qkv_ref[0]
    dq, dk, dv = [], [], []
    for h in range(HPR):
        q = qkv[:, HD * h : HD * (h + 1)]
        k = qkv[:, PART + HD * h : PART + HD * (h + 1)]
        v = qkv[:, 2 * PART + HD * h : 2 * PART + HD * (h + 1)]
        dm = dm_all[:, HD * h : HD * (h + 1)]
        far_left = jnp.zeros((BLK, BLK), F32)
        far_right = jnp.zeros((BLK, BLK), F32)
        for i in range(NBLK):
            rows = slice(BLK * i, BLK * (i + 1))
            p = probs_ref[0, h, rows, :].astype(F32)
            dp = mm_nt(dm[rows], v)
            ds = (p * (dp - jnp.sum(p * dp, axis=-1, keepdims=True))).astype(BF)
            ds_s[rows, :] = ds
            ds = ds.astype(F32)
            for jb in range(NBLK):
                piece = ds[:, BLK * jb : BLK * (jb + 1)]
                delta = jb - i
                if abs(delta) <= 1:
                    cols = slice(BLK * (delta + 1), BLK * (delta + 2))
                    if i == max(0, -delta):
                        near_s[:, cols] = piece
                    else:
                        near_s[:, cols] += piece
                elif delta > 0:
                    far_right += piece
                else:
                    far_left += piece
        near_s[:, 3 * BLK :] = jnp.zeros((BLK, BLK), F32)
        sums_s[h : h + 1, 0 : 4 * BLK] = diagonal_sums(near_s[...])
        sums_s[h : h + 1, 4 * BLK : 5 * BLK] = col_sum(far_left)
        sums_s[h : h + 1, 5 * BLK : 6 * BLK] = col_sum(far_right)
        dscore = ds_s[...]
        dq.append(mm(dscore, k) * 0.125)
        dk.append(mm_tn(dscore, q) * 0.125)
        dv.append(mm_tn(probs_ref[0, h], dm))
    dqkv = jnp.concatenate(dq + dk + dv, axis=1).astype(BF)

    qv = col_sum(dqkv.astype(F32))
    sums = sums_s[...]
    lane = lax.broadcasted_iota(jnp.int32, (1, 6 * BLK), 1)
    is_left = (lane == 0) | ((lane >= 3 * BLK) & (lane < 5 * BLK))
    is_right = ((lane >= BUCKETS - 1) & (lane < 3 * BLK)) | (lane >= 5 * BLK)
    left = jnp.sum(jnp.where(is_left, sums, 0.0), axis=-1, keepdims=True)
    right = jnp.sum(jnp.where(is_right, sums, 0.0), axis=-1, keepdims=True)
    sums = jnp.where(lane == 0, left, jnp.where(lane == BUCKETS - 1, right, sums))
    table = jnp.concatenate([sums[h : h + 1, :BUCKETS] for h in range(HPR)], axis=1)
    table = jnp.broadcast_to(table, (8, D)).astype(BF)
    table = mm_nt(table, order_s[...])[0:1]
    r = slice_of(slot, place_ref)
    vecs = []
    for i in range(3):
        m = 3 * r + i
        row = vec_ref[pl.ds(m // 2, 1), :]
        vecs.append(jnp.where(m % 2 == 0, row[:, 0:384], row[:, 384:768]))
    bup = bup_ref[0, 0:1, :]
    tail = jnp.concatenate(
        [
            jnp.concatenate([qv[:, 0:PART], qv[:, 2 * PART :], bup[:, 0:384]], axis=1),
            jnp.concatenate([bup[:, 384:768], table[:, 0:384]], axis=1),
            jnp.concatenate([table[:, 384:768], vecs[0]], axis=1),
            jnp.concatenate([vecs[1], vecs[2]], axis=1),
            jnp.zeros((TILE_ROWS - 4, D), F32),
        ],
        axis=0,
    )
    da_s[D:ATT_ROWS, :] = tail.astype(BF)

    dw = mm_tn(xp_ref[...], dqkv).astype(BF)
    for src_row, src_col, dst_row, dst_col in qkv_pieces():
        da_s[src_row : src_row + 96, src_col : src_col + PART] = dw[
            dst_row : dst_row + 96, dst_col : dst_col + PART
        ]
    dx_s[...] += mm_nt(dqkv, wq_ref[0])

    @pl.when(slot < SLOTS)
    def _():
        da0_ref[0] = da_s[...]

    @pl.when(slot >= SLOTS)
    def _():
        da1_ref[0] = da_s[...]

    @pl.when(s == RANKS - 1)
    def _():
        in_grad_ref[...] = grad_one_ref[...] + mm_nt(dx_s[...].astype(BF), column_order())


def attention_backward(place, ga, own_att, got_att, qkv, wq, mixed, probs, xp, vec_g, up_g, grad_one):
    per = lambda *shape: pl.BlockSpec(
        (1, *shape), lambda s, n: (lax.rem(s + SLOTS, RANKS),) + (0,) * len(shape)
    )
    own = lambda s: jnp.maximum(s - 2, 0)
    got = lambda s: jnp.minimum(s, 1)
    return call(
        att_bwd_kernel,
        "attention_backward", (RANKS,),
        [
            whole(L, D),
            pl.BlockSpec((1, PART, D), lambda s, n: (own(s), QKV_ROWS // PART, 0)),
            pl.BlockSpec((1, PART, D), lambda s, n: (got(s), QKV_ROWS // PART, 0)),
            per(L, QKV_ROWS), per(HPR, L, L), per(L, PART), per(D, QKV_ROWS),
            whole(L, D), whole(8, D), per(8, D), whole(L, D),
        ],
        [
            pl.BlockSpec((1, ATT_ROWS, D), lambda s, n: (own(s), 0, 0)),
            pl.BlockSpec((1, ATT_ROWS, D), lambda s, n: (got(s), 0, 0)),
            whole(L, D),
        ],
        [shaped(BF, SLOTS, ATT_ROWS, D), shaped(BF, SLOTS, ATT_ROWS, D), shaped(F32, L, D)],
        [
            pltpu.VMEM((L, L), BF),
            pltpu.VMEM((BLK, 4 * BLK), F32),
            pltpu.VMEM((8, 6 * BLK), F32),
            pltpu.VMEM((L, D), F32),
            pltpu.VMEM((D, D), BF),
            pltpu.VMEM((PART, D), BF),
            pltpu.VMEM((ATT_ROWS, D), BF),
        ],
        (place, ga, own_att, got_att, qkv, probs, mixed, wq, xp, vec_g, up_g, grad_one),
        flops=12_000_000_000, moved=30_000_000,
    )


X_SWAP = [(w, w ^ 1) for w in range(8)]
Z_RING = [(w, (w + 2) % 8) for w in range(8)]
Y_SWAP = [(n, n ^ 2) for n in range(4)]
CORE_SWAP = [(n, n ^ 1) for n in range(4)]


def swap_x(a):
    return lax.ppermute(a, "wide", X_SWAP)


def swap_y(a):
    return lax.ppermute(a, "narrow", Y_SWAP)


def ring_z(a):
    return lax.ppermute(a, "wide", Z_RING)


def swap_core(a):
    return lax.ppermute(a, "narrow", CORE_SWAP)


together = lax.optimization_barrier


def aligned_plan(shard, wide, ranks):
    unit = TILE_ROWS * D
    tiles, spare = divmod(shard, unit)
    rows = tiles * TILE_ROWS
    fits = (
        wide == 8
        and ranks == RANKS
        and spare * wide <= unit
        and spare % 128 == 0
        and rows * wide == MAT_ROWS
        and rows == QKV_ROWS // 2
    )
    return rows, spare, fits


def gather_blocks(block, z, x, rows):
    ring, by_x, by_y, corner = [block], [], [], [None] * 4
    r1, x0, y0 = together((ring_z(block), swap_x(block), swap_y(block)))
    r2, x1, y1 = together((ring_z(r1), swap_x(r1), swap_y(r1)))
    r3, x2, y2, d0, d1 = together((ring_z(r2), swap_x(r2), swap_y(r2), swap_y(x0), swap_x(y1)))
    x3, y3, d2 = swap_x(r3), swap_y(r3), swap_y(x2)
    d3 = swap_x(y3)
    planes = jnp.mod(z - jnp.arange(4, dtype=jnp.int32), 4)
    at = jnp.concatenate([2 * planes + x, 2 * planes + 1 - x])
    pieces = [block, r1, r2, r3, x0, x1, x2, x3, y0, y1, y2, y3, d0, d1, d2, d3]
    return merge_blocks(at, pieces, rows)


def add_low(*terms):
    total = terms[0].astype(F32)
    for term in terms[1:]:
        total = total + term.astype(F32)
    return total.astype(BF)


def reduce_windows(own, got, z, x, rows):
    kinds = ("y", "x", "y", "x")
    planes = jnp.mod(z - jnp.array([1, 2, 3, 0], jnp.int32), 4)
    at = jnp.stack([2 * planes + x, 2 * planes + 1 - x], axis=1).reshape(-1)
    parts = split_windows(at[:4], kinds[:2], own, got, rows) + split_windows(
        at[4:], kinds[2:], own, got, rows
    )
    first, second = [], []
    for kind, (send, pass_on, keep) in zip(kinds, parts):
        one, two = (swap_y, swap_x) if kind == "y" else (swap_x, swap_y)
        first.append(one(send))
        second.append(two(add_low(pass_on, first[-1][0])))
    ring = None
    for q in range(3):
        terms = [parts[q][2], first[q][1], second[q]] + ([] if ring is None else [ring])
        ring = ring_z(add_low(*terms))
    return parts[3][2], first[3], second[3], ring


def gather_plain(params):
    flat = lax.all_gather(params.astype(BF)[0], "wide", axis=0, tiled=True)
    flat = jnp.pad(flat, (0, PAD_ROWS * D - flat.shape[0])).reshape(PAD_ROWS, D)
    head = jnp.swapaxes(flat[:QKV_ROWS].reshape(2, 96, 3, D), 1, 2).reshape(QKV_ROWS, D)
    flat = jnp.concatenate([head, flat[QKV_ROWS:]], axis=0)
    mats = lax.all_gather(flat, "narrow", axis=0, tiled=True).reshape(2, 2, PAD_ROWS, D)
    pairs = []
    for core in range(2):
        pair = mats[:, core]
        pairs.append((jnp.concatenate([pair[:, :D], pair[:, MAT_ROWS:]], axis=1), pair[:, D:MAT_ROWS]))
    return pairs


def scatter_plain(pairs, shard, wide):
    mats = [jnp.concatenate([att[:, :D], ff, att[:, D:]], axis=1) for att, ff in pairs]
    grads = jnp.stack(mats, axis=1).reshape(-1, D)
    mine = lax.psum_scatter(grads, "narrow", scatter_dimension=0, tiled=True)
    head = jnp.swapaxes(mine[:QKV_ROWS].reshape(2, 3, 96, D), 1, 2).reshape(QKV_ROWS, D)
    flat = jnp.concatenate([head, mine[QKV_ROWS:]], axis=0).reshape(-1)[: shard * wide]
    return lax.psum_scatter(flat.astype(F32), "wide", scatter_dimension=0, tiled=True).reshape(1, shard)


def body(hidden_in, out_grad, pair_lengths, params, momentum, average):
    wide, ranks = lax.axis_size("wide"), lax.axis_size("narrow")
    shard = params.shape[1]
    rows, spare, fits = aligned_plan(shard, wide, ranks)
    at_wide, at_narrow = lax.axis_index("wide"), lax.axis_index("narrow")
    if fits:
        place = jnp.stack([at_wide, at_narrow // 2, at_narrow % 2]).astype(jnp.int32)
        block = own_block(place, params, rows, spare, wide)
        own_att, own_ff = gather_blocks(block, at_wide // 2, at_wide % 2, rows)
        got_att, got_ff = swap_core(own_att), swap_core(own_ff)
    else:
        place = jnp.zeros((3,), jnp.int32)
        (own_att, own_ff), (got_att, got_ff) = gather_plain(params)
    scalars = jnp.concatenate([pair_lengths[0], place])
    tails = jnp.concatenate([own_att[:, D:], got_att[:, D:]], axis=0)

    qkv, wq, mixed, probs, xp, n1, r1 = attention_forward(scalars, hidden_in, own_att, got_att, tails)
    block_out, own_ffg, got_ffg, grad_one, ga, vec_g, up_g = feed_forward(
        place, n1, r1, out_grad, own_ff, got_ff, tails
    )
    own_attg, got_attg, in_grad = attention_backward(
        place, ga, own_att, got_att, qkv, wq, mixed, probs, xp, vec_g, up_g, grad_one
    )

    device_count = wide * ranks
    rate = 1.0 / (32.0 * math.sqrt(hidden_in.shape[0] * device_count))
    if fits:
        got = swap_core(got_attg), swap_core(got_ffg)
        parts = reduce_windows((own_attg, own_ffg), got, at_wide // 2, at_wide % 2, rows)
        grads, new_params, new_momentum, new_average, low = update_shard(
            place, parts, params, momentum, average, rate, rows, spare, wide
        )
    else:
        grads = scatter_plain(((own_attg, own_ffg), (got_attg, got_ffg)), shard, wide)
        new_momentum = 0.5 * momentum + rate * grads
        new_params = params - (rate * grads + 0.5 * new_momentum)
        new_average = 0.5 * average + 0.5 * new_params
        low = new_params.astype(BF)
    return (
        block_out,
        in_grad,
        grads,
        new_params,
        new_momentum,
        new_average,
        low,
    )


def solution(mesh):
    rows = P(("wide", "narrow"), None)
    flat = P("narrow", "wide")
    return jax.shard_map(
        body,
        mesh=mesh,
        in_specs=(rows, rows, rows, flat, flat, flat),
        out_specs=(rows, rows, flat, flat, flat, flat, flat),
        check_vma=False,
    )
```

time: 419 us -> 283 us (0.68)
  waiting for transfers between devices: 275 us -> 142 us
  starting transfers between devices: 0.26 us -> 27.7 us
  Pallas kernels: 79.6 us -> 102 us
  local copies, waits for them, and re-layouts: 25.9 us -> 5.77 us
  other arithmetic: 23.8 us -> 4.26 us
  between operations: 14.4 us -> 1.01 us
    reduce_scatter x1 -> x0, waiting for transfers between devices: 166 us -> none  [scatter_grads(): lax.psum_scatter(windows.reshape(-1, D), ('narrow', 'wide'), scatter_dime...]
    ppermute x0 -> x30, waiting for transfers between devices: none -> 142 us  [the longest x10 89.1 us: swap_y(): return lax.ppermute(a, 'narrow', Y_SWAP)]
    all_gather x1 -> x0, waiting for transfers between devices: 109 us -> none  [gather_weights(): gathered = lax.all_gather(block, ('narrow', 'wide'), axis=0, tiled=True)]
    ppermute x0 -> x30, starting transfers between devices: none -> 27.7 us  [the longest x10 12.7 us: swap_y(): return lax.ppermute(a, 'narrow', Y_SWAP)]
    pallas_call x4 -> x8, Pallas kernels: 79.6 us -> 102 us  [call(): pl.pallas_call(kernel, grid_spec=pltpu.PrefetchScalarGridSpec(num_scalar_...]
    unnamed x5 -> x0, other arithmetic: 11.4 us -> none
    reshape x8 -> x0, local copies, waits for them, and re-layouts: 6.59 us -> none  [the longest x1 4.91 us: scatter_grads(): return lax.dynamic_slice(flat, (at * spare,), (shard,)).reshape(1, shard)]
    another operation x1 -> x0, local copies, waits for them, and re-layouts: 6.28 us -> none  [scatter_grads(): jnp.stack([grads[:, rows * w:rows * (w + 1) + TILE_ROWS] for w in range(w...]
  transfers between devices with their start and end apart: 2 -> 30, of which waited for: 2 -> 20; matrix products, arithmetic and copies ran while one was open for 0% -> 2% of each run, Pallas kernels for 0% -> 20%
where the time goes in v2:
time: 283 us; the launch traced here: 282 us
  waiting for transfers between devices  142 us (50%)
  Pallas kernels  102 us (36%)
  starting transfers between devices  27.7 us (10%)
  local copies, waits for them, and re-layouts  5.77 us (2%)
  other arithmetic  4.26 us (2%)
    pallas_call x8, Pallas kernels, call(): pl.pallas_call(kernel, grid_spec=pltpu.PrefetchScalarGridSpec(num_scalar_...  102 us
    ppermute x10, waiting for transfers between devices, swap_y(): return lax.ppermute(a, 'narrow', Y_SWAP)  89.1 us
    ppermute x6, waiting for transfers between devices, ring_z(): return lax.ppermute(a, 'wide', Z_RING)  24.4 us
    ppermute x10, waiting for transfers between devices, swap_x(): return lax.ppermute(a, 'wide', X_SWAP)  14.8 us
    ppermute x4, waiting for transfers between devices, swap_core(): return lax.ppermute(a, 'narrow', CORE_SWAP)  13.3 us
    ppermute x10, starting transfers between devices, swap_y(): return lax.ppermute(a, 'narrow', Y_SWAP)  12.7 us
    ppermute x10, starting transfers between devices, swap_x(): return lax.ppermute(a, 'wide', X_SWAP)  12.1 us
  transfers between devices with their start and end apart: 30, of which 20 were waited for; matrix products, arithmetic and copies ran while one was open for 2% of the time, Pallas kernels for 20%

profile of v2, /device:TPU:0, one launch (start us, length us, event | category | flops | bytes accessed | tf_op | source)
XLA Modules:
  0.0 282.3 jit_solution(17865170140787415572)
XLA Ops:
  2.6 3.1 %collective-permute-start.2 = (bf16[304,768]{1,0:T(8,128)(2,1)S(1)}, bf16[304,768]{1,0:T(8,128)(2,1)S(1)}, u32[]{:S(2)}, u32[]{:S(2)}) collective-permute-start(bf16[304,768]{1,0:T(8,128)(2,1)S(1)} %own_block.1.refs_0_), channel_id=1, source_target_pairs={{0,2},{1,3},{2,0},{3,1},{4,6},{5,7},{6,4},{7,5},{8,10},{9,11},{10,... | collective-permute-start | bytes 1400840 | tf_op jit(solution)/shard_map/ppermute | solution.py:805
  8.7 7.6 %collective-permute-done.2.refs_8_ = bf16[304,768]{1,0:T(8,128)(2,1)S(1)} collective-permute-done((bf16[304,768]{1,0:T(8,128)(2,1)S(1)}, bf16[304,768]{1,0:T(8,128)(2,1)S(1)}, u32[]{:S(2)}, u32[]{:S(2)}) %collective-permute-start.2) | collective-permute-done | bytes 466976 | tf_op jit(solution)/shard_map/ppermute | solution.py:805
  17.8 3.1 %collective-permute-done.refs_1_ = bf16[304,768]{1,0:T(8,128)(2,1)S(1)} collective-permute-done((bf16[304,768]{1,0:T(8,128)(2,1)S(1)}, bf16[304,768]{1,0:T(8,128)(2,1)S(1)}, u32[]{:S(2)}, u32[]{:S(2)}) %collective-permute-start) | collective-permute-done | bytes 466976 | tf_op jit(solution)/shard_map/ppermute | solution.py:809
  23.5 11.0 %collective-permute-done.5.refs_9_ = bf16[304,768]{1,0:T(8,128)(2,1)S(1)} collective-permute-done((bf16[304,768]{1,0:T(8,128)(2,1)S(1)}, bf16[304,768]{1,0:T(8,128)(2,1)S(1)}, u32[]{:S(2)}, u32[]{:S(2)}) %collective-permute-start.5) | collective-permute-done | bytes 466976 | tf_op jit(solution)/shard_map/ppermute | solution.py:805
  37.8 6.7 %collective-permute-done.9.refs_12_ = bf16[304,768]{1,0:T(8,128)(2,1)S(1)} collective-permute-done((bf16[304,768]{1,0:T(8,128)(2,1)S(1)}, bf16[304,768]{1,0:T(8,128)(2,1)S(1)}, u32[]{:S(2)}, u32[]{:S(2)}) %collective-permute-start.9) | collective-permute-done | bytes 466976 | tf_op jit(solution)/shard_map/ppermute | solution.py:805
  44.5 3.6 %collective-permute-done.10.refs_13_ = bf16[304,768]{1,0:T(8,128)(2,1)S(1)} collective-permute-done((bf16[304,768]{1,0:T(8,128)(2,1)S(1)}, bf16[304,768]{1,0:T(8,128)(2,1)S(1)}, u32[]{:S(2)}, u32[]{:S(2)}) %collective-permute-start.10) | collective-permute-done | bytes 466976 | tf_op jit(solution)/shard_map/ppermute | solution.py:801
  48.1 3.9 %collective-permute-done.8.refs_10_ = bf16[304,768]{1,0:T(8,128)(2,1)S(1)} collective-permute-done((bf16[304,768]{1,0:T(8,128)(2,1)S(1)}, bf16[304,768]{1,0:T(8,128)(2,1)S(1)}, u32[]{:S(2)}, u32[]{:S(2)}) %collective-permute-start.8) | collective-permute-done | bytes 466976 | tf_op jit(solution)/shard_map/ppermute | solution.py:805
  57.8 10.7 %collective-permute-done.12.refs_11_ = bf16[304,768]{1,0:T(8,128)(2,1)} collective-permute-done((bf16[304,768]{1,0:T(8,128)(2,1)}, bf16[304,768]{1,0:T(8,128)(2,1)}, u32[]{:S(2)}, u32[]{:S(2)}) %collective-permute-start.12) | collective-permute-done | bytes 466976 | tf_op jit(solution)/shard_map/ppermute | solution.py:805
  70.2 3.5 %collective-permute-done.13.refs_14_ = bf16[304,768]{1,0:T(8,128)(2,1)} collective-permute-done((bf16[304,768]{1,0:T(8,128)(2,1)}, bf16[304,768]{1,0:T(8,128)(2,1)}, u32[]{:S(2)}, u32[]{:S(2)}) %collective-permute-start.13) | collective-permute-done | bytes 466976 | tf_op jit(solution)/shard_map/ppermute | solution.py:805
  73.8 3.6 %collective-permute-done.14.refs_15_ = bf16[304,768]{1,0:T(8,128)(2,1)} collective-permute-done((bf16[304,768]{1,0:T(8,128)(2,1)}, bf16[304,768]{1,0:T(8,128)(2,1)}, u32[]{:S(2)}, u32[]{:S(2)}) %collective-permute-start.14) | collective-permute-done | bytes 466976 | tf_op jit(solution)/shard_map/ppermute | solution.py:801
  77.4 6.4 %merge_weights.1 = (bf16[2,784,768]{2,1,0:T(8,128)(2,1)}, bf16[2,1536,768]{2,1,0:T(8,128)(2,1)}) custom-call(s32[8]{0:T(128)} %pad_add_fusion.3.at_ref, bf16[304,768]{1,0:T(8,128)(2,1)} %copy-done.2, bf16[304,768]{1,0:T(8,128)(2,1)} %copy-done.12, bf16[304,768]{1,0:T(8,128)(2,1)} %copy-done.15, bf16[304,768]{1,0:T(8,128)(2,1)} %collective-permute-done.6.refs_3_, ...), custom_call_target="tpu_custom_call" | custom-call | tf_op jit(solution)/shard_map/merge_weights/pallas_call | solution.py:106
  85.7 9.7 %collective-permute-done.15.mq1_ref.wo1_ref = bf16[2,784,768]{2,1,0:T(8,128)(2,1)S(1)} collective-permute-done((bf16[2,784,768]{2,1,0:T(8,128)(2,1)}, bf16[2,784,768]{2,1,0:T(8,128)(2,1)S(1)}, u32[]{:S(2)}, u32[]{:S(2)}) %collective-permute-start.15) | collective-permute-done | bytes 2408480 | tf_op jit(solution)/shard_map/ppermute | solution.py:813
  96.9 20.0 %attention_forward.1 = (bf16[4,512,576]{2,1,0:T(8,128)(2,1)}, bf16[4,768,576]{2,1,0:T(8,128)(2,1)}, bf16[4,512,192]{2,1,0:T(8,128)(2,1)}, bf16[4,3,512,512]{3,2,...) custom-call(s32[7]{0:T(128)} %pad_add_fusion.2.scal_ref, ...), custom_call_target="tpu_custom_call" | custom-call | flops 6000000000 | bytes 24000000 | tf_op jit(solution)/shard_map/attention_forward/pallas_call | solution.py:106
  116.9 29.9 %feed_forward.1 = (bf16[512,768]{1,0:T(8,128)(2,1)}, bf16[2,1536,768]{2,1,0:T(8,128)(2,1)}, bf16[2,1536,768]{2,1,0:T(8,128)(2,1)}, f32[512,768]{1,0:T(8,128)}, b...) custom-call(s32[3]{0:T(128)} %copy-done.6, f32[512,768]{1,0:T(8,128)} %get-tuple-element.66.n1_ref, ...), custom_call_target="tpu_custom_call" | custom-call | flops 14499999744 | bytes 36000000 | tf_op jit(solution)/shard_map/feed_forward/pallas_call | solution.py:106
  147.0 29.7 %attention_backward.1 = (bf16[2,784,768]{2,1,0:T(8,128)(2,1)}, bf16[2,784,768]{2,1,0:T(8,128)(2,1)}, f32[512,768]{1,0:T(8,128)}) custom-call(s32[3]{0:T(128)} %copy-done.6, bf16[512,768]{1,0:T(8,128)(2,1)} %get-tuple-element.70.ga_ref, bf16[2,784,768]{2,1,0:T(8,128)(2,1)} %get-tuple-element.65.mq0_ref.wo0_ref, bf16[2,784,768]{2,1,0:T(8,128)(2,1)} %copy-done.24, ...), custom_call_target="tpu_custom_call" | custom-call | flops 12000000000 | bytes 30000000 | tf_op jit(solution)/shard_map/attention_backward/pallas_call | solution.py:106
  178.0 3.6 %collective-permute-done.17.got_att = bf16[2,784,768]{2,1,0:T(8,128)(2,1)S(1)} collective-permute-done((bf16[2,784,768]{2,1,0:T(8,128)(2,1)}, bf16[2,784,768]{2,1,0:T(8,128)(2,1)S(1)}, u32[]{:S(2)}, u32[]{:S(2)}) %collective-permute-start.17) | collective-permute-done | bytes 2408480 | tf_op jit(solution)/shard_map/ppermute | solution.py:813
  183.0 5.8 %split_windows.3 = (bf16[2,304,768]{2,1,0:T(8,128)(2,1)}, bf16[304,768]{1,0:T(8,128)(2,1)}, bf16[304,768]{1,0:T(8,128)(2,1)}, bf16[2,304,768]{2,1,0:T(8,128)(2,1...) custom-call(s32[4]{0:T(128)} %slice.47.at_ref, bf16[2,784,768]{2,1,0:T(8,128)(2,1)} %get-tuple-element.80.own_att, ...), custom_call_target="tpu_custom_call" | custom-call | tf_op jit(solution)/shard_map/split_windows/pallas_call | solution.py:106
  191.7 20.4 %collective-permute-done.25 = bf16[2,304,768]{2,1,0:T(8,128)(2,1)S(1)} collective-permute-done((bf16[2,304,768]{2,1,0:T(8,128)(2,1)}, bf16[2,304,768]{2,1,0:T(8,128)(2,1)S(1)}, u32[]{:S(2)}, u32[]{:S(2)}) %collective-permute-start.25) | collective-permute-done | bytes 933920 | tf_op jit(solution)/shard_map/ppermute | solution.py:805
  215.2 5.9 %split_windows.2 = (bf16[2,304,768]{2,1,0:T(8,128)(2,1)}, bf16[304,768]{1,0:T(8,128)(2,1)}, bf16[304,768]{1,0:T(8,128)(2,1)}, bf16[2,304,768]{2,1,0:T(8,128)(2,1...) custom-call(s32[4]{0:T(128)} %slice.42.at_ref, bf16[2,784,768]{2,1,0:T(8,128)(2,1)} %get-tuple-element.80.own_att, ...), custom_call_target="tpu_custom_call" | custom-call | tf_op jit(solution)/shard_map/split_windows/pallas_call | solution.py:106
  226.9 18.1 %collective-permute-done.21 = bf16[2,304,768]{2,1,0:T(8,128)(2,1)S(1)} collective-permute-done((bf16[2,304,768]{2,1,0:T(8,128)(2,1)}, bf16[2,304,768]{2,1,0:T(8,128)(2,1)S(1)}, u32[]{:S(2)}, u32[]{:S(2)}) %collective-permute-start.21) | collective-permute-done | bytes 933920 | tf_op jit(solution)/shard_map/ppermute | solution.py:805
  246.1 7.2 %collective-permute-done.24 = bf16[304,768]{1,0:T(8,128)(2,1)S(1)} collective-permute-done((bf16[304,768]{1,0:T(8,128)(2,1)S(1)}, bf16[304,768]{1,0:T(8,128)(2,1)S(1)}, u32[]{:S(2)}, u32[]{:S(2)}) %collective-permute-start.24) | collective-permute-done | bytes 466976 | tf_op jit(solution)/shard_map/ppermute | solution.py:805
  257.0 9.4 %collective-permute-done.28 = bf16[304,768]{1,0:T(8,128)(2,1)S(1)} collective-permute-done((bf16[304,768]{1,0:T(8,128)(2,1)S(1)}, bf16[304,768]{1,0:T(8,128)(2,1)S(1)}, u32[]{:S(2)}, u32[]{:S(2)}) %collective-permute-start.28) | collective-permute-done | bytes 466976 | tf_op jit(solution)/shard_map/ppermute | solution.py:809
  266.8 11.9 %collective-permute-done.29.ring_ref = bf16[304,768]{1,0:T(8,128)(2,1)S(1)} collective-permute-done((bf16[304,768]{1,0:T(8,128)(2,1)S(1)}, bf16[304,768]{1,0:T(8,128)(2,1)S(1)}, u32[]{:S(2)}, u32[]{:S(2)}) %collective-permute-start.29) | collective-permute-done | bytes 466976 | tf_op jit(solution)/shard_map/ppermute | solution.py:809
  278.7 3.6 %update_shard.1 = (f32[1,221568]{1,0:T(1,128)}, f32[1,221568]{1,0:T(1,128)}, f32[1,221568]{1,0:T(1,128)}, f32[1,221568]{1,0:T(1,128)}, bf16[1,221568]{1,0:T(2,128)(2,1)}) custom-call(s32[3]{0:T(128)S(1)} %copy-done.7, bf16[304,768]{1,0:T(8,128)(2,1)S(1)} %copy-done.5, bf16[2,304,768]{2,1,0:T(8,128)(2,1)S(1)} %collective-permute-done.19.near_ref, ...), custom_call_target="tpu_custom_call" | custom-call | tf_op jit(solution)/shard_map/update_shard/pallas_call | solution.py:106
  (122 shorter events, 42.9 us)
Async XLA Ops:
  2.6 13.8 %collective-permute-start.2 = (bf16[304,768]{1,0:T(8,128)(2,1)S(1)}, bf16[304,768]{1,0:T(8,128)(2,1)S(1)}, u32[]{:S(2)}, u32[]{:S(2)}) collective-permute-start(bf16[304,768]{1,0:T(8,128)(2,1)S(1)} %own_block.1.refs_0_), channel_id=1, source_target_pairs={{0,2},{1,3},{2,0},{3,1},{4,6},{5,7},{6,4},{7,5},{8,10},{9,11},{10,... | collective-permute-start | bytes 1400840 | tf_op jit(solution)/shard_map/ppermute | solution.py:805
  7.2 13.7 %collective-permute-start = (bf16[304,768]{1,0:T(8,128)(2,1)S(1)}, bf16[304,768]{1,0:T(8,128)(2,1)S(1)}, u32[]{:S(2)}, u32[]{:S(2)}) collective-permute-start(bf16[304,768]{1,0:T(8,128)(2,1)S(1)} %own_block.1.refs_0_), channel_id=1, source_target_pairs={{0,8},{4,12},{8,16},{12,20},{16,24},{20,28},{24,0},{28,4},{1,9},{5... | collective-permute-start | bytes 1400840 | tf_op jit(solution)/shard_map/ppermute | solution.py:809
  20.9 13.6 %collective-permute-start.5 = (bf16[304,768]{1,0:T(8,128)(2,1)S(1)}, bf16[304,768]{1,0:T(8,128)(2,1)S(1)}, u32[]{:S(2)}, u32[]{:S(2)}) collective-permute-start(bf16[304,768]{1,0:T(8,128)(2,1)S(1)} %collective-permute-done.refs_1_), channel_id=1, source_target_pairs={{0,2},{1,3},{2,0},{3,1},{4,6},{5,7},{6,4},{7,5},{8,10},{9,11},{10,... | collective-permute-start | bytes 1400840 | tf_op jit(solution)/shard_map/ppermute | solution.py:805
  21.4 13.1 %collective-permute-start.4 = (bf16[304,768]{1,0:T(8,128)(2,1)S(1)}, bf16[304,768]{1,0:T(8,128)(2,1)S(1)}, u32[]{:S(2)}, u32[]{:S(2)}) collective-permute-start(bf16[304,768]{1,0:T(8,128)(2,1)S(1)} %collective-permute-done.refs_1_), channel_id=1, source_target_pairs={{0,4},{4,0},{8,12},{12,8},{16,20},{20,16},{24,28},{28,24},{1,5},{5... | collective-permute-start | bytes 1400840 | tf_op jit(solution)/shard_map/ppermute | solution.py:801
  21.9 12.5 %collective-permute-start.3 = (bf16[304,768]{1,0:T(8,128)(2,1)S(1)}, bf16[304,768]{1,0:T(8,128)(2,1)S(1)}, u32[]{:S(2)}, u32[]{:S(2)}) collective-permute-start(bf16[304,768]{1,0:T(8,128)(2,1)S(1)} %collective-permute-done.refs_1_), channel_id=1, source_target_pairs={{0,8},{4,12},{8,16},{12,20},{16,24},{20,28},{24,0},{28,4},{1,9},{5... | collective-permute-start | bytes 1400840 | tf_op jit(solution)/shard_map/ppermute | solution.py:809
  21.9 22.5 %collective-permute-start.9 = (bf16[304,768]{1,0:T(8,128)(2,1)S(1)}, bf16[304,768]{1,0:T(8,128)(2,1)S(1)}, u32[]{:S(2)}, u32[]{:S(2)}) collective-permute-start(bf16[304,768]{1,0:T(8,128)(2,1)S(1)} %collective-permute-done.1.refs_4_), channel_id=1, source_target_pairs={{0,2},{1,3},{2,0},{3,1},{4,6},{5,7},{6,4},{7,5},{8,10},{9,11},{10,... | collective-permute-start | bytes 1400840 | tf_op jit(solution)/shard_map/ppermute | solution.py:805
  34.5 13.6 %collective-permute-start.10 = (bf16[304,768]{1,0:T(8,128)(2,1)S(1)}, bf16[304,768]{1,0:T(8,128)(2,1)S(1)}, u32[]{:S(2)}, u32[]{:S(2)}) collective-permute-start(bf16[304,768]{1,0:T(8,128)(2,1)S(1)} %collective-permute-done.5.refs_9_), channel_id=1, source_target_pairs={{0,4},{4,0},{8,12},{12,8},{16,20},{20,16},{24,28},{28,24},{1,5},{5... | collective-permute-start | bytes 1400840 | tf_op jit(solution)/shard_map/ppermute | solution.py:801
  35.7 16.2 %collective-permute-start.8 = (bf16[304,768]{1,0:T(8,128)(2,1)S(1)}, bf16[304,768]{1,0:T(8,128)(2,1)S(1)}, u32[]{:S(2)}, u32[]{:S(2)}) collective-permute-start(bf16[304,768]{1,0:T(8,128)(2,1)S(1)} %collective-permute-done.3.refs_2_), channel_id=1, source_target_pairs={{0,2},{1,3},{2,0},{3,1},{4,6},{5,7},{6,4},{7,5},{8,10},{9,11},{10,... | collective-permute-start | bytes 1400840 | tf_op jit(solution)/shard_map/ppermute | solution.py:805
  37.3 17.3 %collective-permute-start.7 = (bf16[304,768]{1,0:T(8,128)(2,1)S(1)}, bf16[304,768]{1,0:T(8,128)(2,1)}, u32[]{:S(2)}, u32[]{:S(2)}) collective-permute-start(bf16[304,768]{1,0:T(8,128)(2,1)S(1)} %collective-permute-done.3.refs_2_), channel_id=1, source_target_pairs={{0,4},{4,0},{8,12},{12,8},{16,20},{20,16},{24,28},{28,24},{1,5},{5... | collective-permute-start | bytes 1400840 | tf_op jit(solution)/shard_map/ppermute | solution.py:801
  37.8 16.8 %collective-permute-start.6 = (bf16[304,768]{1,0:T(8,128)(2,1)S(1)}, bf16[304,768]{1,0:T(8,128)(2,1)}, u32[]{:S(2)}, u32[]{:S(2)}) collective-permute-start(bf16[304,768]{1,0:T(8,128)(2,1)S(1)} %collective-permute-done.3.refs_2_), channel_id=1, source_target_pairs={{0,8},{4,12},{8,16},{12,20},{16,24},{20,28},{24,0},{28,4},{1,9},{5... | collective-permute-start | bytes 1400840 | tf_op jit(solution)/shard_map/ppermute | solution.py:809
  54.6 13.9 %collective-permute-start.12 = (bf16[304,768]{1,0:T(8,128)(2,1)}, bf16[304,768]{1,0:T(8,128)(2,1)}, u32[]{:S(2)}, u32[]{:S(2)}) collective-permute-start(bf16[304,768]{1,0:T(8,128)(2,1)} %collective-permute-done.6.refs_3_), channel_id=1, source_target_pairs={{0,2},{1,3},{2,0},{3,1},{4,6},{5,7},{6,4},{7,5},{8,10},{9,11},{10,... | collective-permute-start | bytes 1400840 | tf_op jit(solution)/shard_map/ppermute | solution.py:805
  55.6 18.2 %collective-permute-start.11 = (bf16[304,768]{1,0:T(8,128)(2,1)}, bf16[304,768]{1,0:T(8,128)(2,1)}, u32[]{:S(2)}, u32[]{:S(2)}) collective-permute-start(bf16[304,768]{1,0:T(8,128)(2,1)} %collective-permute-done.6.refs_3_), channel_id=1, source_target_pairs={{0,4},{4,0},{8,12},{12,8},{16,20},{20,16},{24,28},{28,24},{1,5},{5... | collective-permute-start | bytes 1400840 | tf_op jit(solution)/shard_map/ppermute | solution.py:801
  57.7 16.1 %collective-permute-start.13 = (bf16[304,768]{1,0:T(8,128)(2,1)}, bf16[304,768]{1,0:T(8,128)(2,1)}, u32[]{:S(2)}, u32[]{:S(2)}) collective-permute-start(bf16[304,768]{1,0:T(8,128)(2,1)} %collective-permute-done.7.refs_6_), channel_id=1, source_target_pairs={{0,2},{1,3},{2,0},{3,1},{4,6},{5,7},{6,4},{7,5},{8,10},{9,11},{10,... | collective-permute-start | bytes 1400840 | tf_op jit(solution)/shard_map/ppermute | solution.py:805
  83.8 33.1 %collective-permute-start.16 = (bf16[2,1536,768]{2,1,0:T(8,128)(2,1)}, bf16[2,1536,768]{2,1,0:T(8,128)(2,1)}, u32[]{:S(2)}, u32[]{:S(2)}) collective-permute-start(bf16[2,1536,768]{2,1,0:T(8,128)(2,1)} %get-tuple-element.68.up0_ref.down0_ref), channel_id=1, source_target_pairs={{0,1},{1,0},{2,3},{3,2},{4,5},{5,4},{6,7},{7,6},{8,9},{9,8},{10,11... | collective-permute-start | bytes 14155784 | tf_op jit(solution)/shard_map/ppermute | solution.py:813
  146.8 34.8 %collective-permute-start.18 = (bf16[2,1536,768]{2,1,0:T(8,128)(2,1)}, bf16[2,1536,768]{2,1,0:T(8,128)(2,1)}, u32[]{:S(2)}, u32[]{:S(2)}) collective-permute-start(bf16[2,1536,768]{2,1,0:T(8,128)(2,1)} %get-tuple-element.83), channel_id=1, source_target_pairs={{0,1},{1,0},{2,3},{3,2},{4,5},{5,4},{6,7},{7,6},{8,9},{9,8},{10,11... | collective-permute-start | bytes 14155784 | tf_op jit(solution)/shard_map/ppermute | solution.py:813
  188.9 23.3 %collective-permute-start.25 = (bf16[2,304,768]{2,1,0:T(8,128)(2,1)}, bf16[2,304,768]{2,1,0:T(8,128)(2,1)S(1)}, u32[]{:S(2)}, u32[]{:S(2)}) collective-permute-start(bf16[2,304,768]{2,1,0:T(8,128)(2,1)} %get-tuple-element.94), channel_id=1, source_target_pairs={{0,2},{1,3},{2,0},{3,1},{4,6},{5,7},{6,4},{7,5},{8,10},{9,11},{10,... | collective-permute-start | bytes 2801672 | tf_op jit(solution)/shard_map/ppermute | solution.py:805
  190.0 32.9 %collective-permute-start.23 = (bf16[2,304,768]{2,1,0:T(8,128)(2,1)}, bf16[2,304,768]{2,1,0:T(8,128)(2,1)S(1)}, u32[]{:S(2)}, u32[]{:S(2)}) collective-permute-start(bf16[2,304,768]{2,1,0:T(8,128)(2,1)} %get-tuple-element.91), channel_id=1, source_target_pairs={{0,4},{4,0},{8,12},{12,8},{16,20},{20,16},{24,28},{28,24},{1,5},{5... | collective-permute-start | bytes 2801672 | tf_op jit(solution)/shard_map/ppermute | solution.py:801
  213.2 12.2 %collective-permute-start.26 = (bf16[304,768]{1,0:T(8,128)(2,1)S(1)}, bf16[304,768]{1,0:T(8,128)(2,1)S(1)}, u32[]{:S(2)}, u32[]{:S(2)}) collective-permute-start(bf16[304,768]{1,0:T(8,128)(2,1)S(1)} %fusion), channel_id=1, source_target_pairs={{0,4},{4,0},{8,12},{12,8},{16,20},{20,16},{24,28},{28,24},{1,5},{5... | collective-permute-start | bytes 1400840 | tf_op jit(solution)/shard_map/ppermute | solution.py:801
  221.1 23.8 %collective-permute-start.21 = (bf16[2,304,768]{2,1,0:T(8,128)(2,1)}, bf16[2,304,768]{2,1,0:T(8,128)(2,1)S(1)}, u32[]{:S(2)}, u32[]{:S(2)}) collective-permute-start(bf16[2,304,768]{2,1,0:T(8,128)(2,1)} %get-tuple-element.88), channel_id=1, source_target_pairs={{0,2},{1,3},{2,0},{3,1},{4,6},{5,7},{6,4},{7,5},{8,10},{9,11},{10,... | collective-permute-start | bytes 2801672 | tf_op jit(solution)/shard_map/ppermute | solution.py:805
  223.0 30.3 %collective-permute-start.24 = (bf16[304,768]{1,0:T(8,128)(2,1)S(1)}, bf16[304,768]{1,0:T(8,128)(2,1)S(1)}, u32[]{:S(2)}, u32[]{:S(2)}) collective-permute-start(bf16[304,768]{1,0:T(8,128)(2,1)S(1)} %fusion.3), channel_id=1, source_target_pairs={{0,2},{1,3},{2,0},{3,1},{4,6},{5,7},{6,4},{7,5},{8,10},{9,11},{10,... | collective-permute-start | bytes 1400840 | tf_op jit(solution)/shard_map/ppermute | solution.py:805
  225.6 27.7 %collective-permute-start.27 = (bf16[304,768]{1,0:T(8,128)(2,1)S(1)}, bf16[304,768]{1,0:T(8,128)(2,1)S(1)}, u32[]{:S(2)}, u32[]{:S(2)}) collective-permute-start(bf16[304,768]{1,0:T(8,128)(2,1)S(1)} %fusion.2), channel_id=1, source_target_pairs={{0,8},{4,12},{8,16},{12,20},{16,24},{20,28},{24,0},{28,4},{1,9},{5... | collective-permute-start | bytes 1400840 | tf_op jit(solution)/shard_map/ppermute | solution.py:809
  225.7 28.0 %collective-permute-start.19 = (bf16[2,304,768]{2,1,0:T(8,128)(2,1)S(1)}, bf16[2,304,768]{2,1,0:T(8,128)(2,1)S(1)}, u32[]{:S(2)}, u32[]{:S(2)}) collective-permute-start(bf16[2,304,768]{2,1,0:T(8,128)(2,1)S(1)} %copy-done.27), channel_id=1, source_target_pairs={{0,4},{4,0},{8,12},{12,8},{16,20},{20,16},{24,28},{28,24},{1,5},{5... | collective-permute-start | bytes 2801672 | tf_op jit(solution)/shard_map/ppermute | solution.py:801
  253.6 12.8 %collective-permute-start.28 = (bf16[304,768]{1,0:T(8,128)(2,1)S(1)}, bf16[304,768]{1,0:T(8,128)(2,1)S(1)}, u32[]{:S(2)}, u32[]{:S(2)}) collective-permute-start(bf16[304,768]{1,0:T(8,128)(2,1)S(1)} %fusion.6), channel_id=1, source_target_pairs={{0,8},{4,12},{8,16},{12,20},{16,24},{20,28},{24,0},{28,4},{1,9},{5... | collective-permute-start | bytes 1400840 | tf_op jit(solution)/shard_map/ppermute | solution.py:809
  253.8 13.0 %collective-permute-start.20 = (bf16[304,768]{1,0:T(8,128)(2,1)S(1)}, bf16[304,768]{1,0:T(8,128)(2,1)S(1)}, u32[]{:S(2)}, u32[]{:S(2)}) collective-permute-start(bf16[304,768]{1,0:T(8,128)(2,1)S(1)} %fusion.11), channel_id=1, source_target_pairs={{0,2},{1,3},{2,0},{3,1},{4,6},{5,7},{6,4},{7,5},{8,10},{9,11},{10,... | collective-permute-start | bytes 1400840 | tf_op jit(solution)/shard_map/ppermute | solution.py:805
  (34 other events, 869.6 us)

commit v3 on v2

--- a/solution.py
+++ b/solution.py
@@ -180,7 +180,7 @@
     w = place_ref[0]
     count = params_ref.shape[1] // 128
     block = (
-        kept_ref[...].astype(F32) + near_ref[0].astype(F32) + second_ref[...].astype(F32) + ring_ref[...].astype(F32)
+        kept_ref[...].astype(F32) + near_ref[...].astype(F32) + second_ref[...].astype(F32) + ring_ref[...].astype(F32)
     )
     start = lead - shift * w
     third = rows // 3
@@ -223,7 +223,7 @@
     return call(
         functools.partial(update_kernel, rows, lead, spare // 128, rate),
         "update_shard", (1,),
-        [whole(cap, D), pl.BlockSpec((1, cap, D), lambda *_: (1, 0, 0)), whole(cap, D), whole(cap, D), flat, flat, flat],
+        [whole(cap, D)] * 4 + [flat] * 3,
         [flat] * 5,
         [shaped(F32, *params.shape)] * 4 + [shaped(BF, *params.shape)],
         [pltpu.VMEM((total, 128), F32)],
@@ -291,7 +291,7 @@
     )
 
 
-def window_kernel(rows, kinds, at_ref, own_att, own_ff, got_att, got_ff, *refs):
+def window_kernel(rows, windows, at_ref, own_att, own_ff, got_att, got_ff, *refs):
     outs, (own_s, got_s, own_sem, got_sem) = refs[:-4], refs[-4:]
     cap = rows + TILE_ROWS
 
@@ -316,36 +316,27 @@
             pltpu.make_async_copy(ff.at[slot, 7 * rows - D : FF_ROWS], buf.at[0:rows], sem).start()
             pltpu.make_async_copy(att.at[slot, D:ATT_ROWS], buf.at[rows:cap], sem).start()
 
-    windows = [(q, xo, slot) for q in range(len(kinds)) for xo in range(2) for slot in range(SLOTS)]
-    for n, (q, xo, slot) in enumerate(windows):
-        w = at_ref[2 * q + xo]
+    for n, (slot, where) in enumerate(windows):
+        w = at_ref[where]
         fetch(w, slot, own_att, own_ff, own_s.at[n], own_sem.at[n])
         fetch(w, slot, got_att, got_ff, got_s.at[n], got_sem.at[n])
-    for n, (q, xo, slot) in enumerate(windows):
+    for n in range(len(windows)):
         pltpu.make_async_copy(own_ff.at[0, 0:cap], own_s.at[n], own_sem.at[n]).wait()
         pltpu.make_async_copy(own_ff.at[0, 0:cap], got_s.at[n], got_sem.at[n]).wait()
-        total = (own_s[n].astype(F32) + got_s[n].astype(F32)).astype(BF)
-        send, pass_on, keep = outs[3 * q : 3 * q + 3]
-        if xo == 0 and slot == 0:
-            keep[...] = total
-        elif xo == 1 and slot == 1:
-            send[0] = total
-        elif (slot == 1) == (kinds[q] == "y"):
-            send[1] = total
-        else:
-            pass_on[...] = total
-
-
-def split_windows(at, kinds, own, got, rows):
+        outs[n][...] = (own_s[n].astype(F32) + got_s[n].astype(F32)).astype(BF)
+
+
+def split_windows(at, names, own, got, rows):
     hbm = pl.BlockSpec(memory_space=pl.ANY)
     cap = rows + TILE_ROWS
-    n = 4 * len(kinds)
+    n = len(names)
+    windows = [(int(name[0] in "YD"), int(name[1]) + 4 * int(name[0] in "XD")) for name in names]
     outs = call(
-        functools.partial(window_kernel, rows, kinds),
+        functools.partial(window_kernel, rows, windows),
         "split_windows", (1,),
         [hbm] * 4,
-        [whole(2, cap, D), whole(cap, D), whole(cap, D)] * len(kinds),
-        [shaped(BF, 2, cap, D), shaped(BF, cap, D), shaped(BF, cap, D)] * len(kinds),
+        [whole(cap, D)] * n,
+        [shaped(BF, cap, D)] * n,
         [
             pltpu.VMEM((n, cap, D), BF),
             pltpu.VMEM((n, cap, D), BF),
@@ -354,7 +345,7 @@
         ],
         (at, *own, *got),
     )
-    return [outs[3 * q : 3 * q + 3] for q in range(len(kinds))]
+    return dict(zip(names, outs))
 
 
 def segment_of(pos, len_ref):
@@ -809,11 +800,16 @@
     return lax.ppermute(a, "wide", Z_RING)
 
 
+def ring_back(a):
+    return lax.ppermute(a, "wide", [(j, i) for i, j in Z_RING])
+
+
 def swap_core(a):
     return lax.ppermute(a, "narrow", CORE_SWAP)
 
 
-together = lax.optimization_barrier
+def after(value, earlier):
+    return lax.optimization_barrier((value, earlier))[0]
 
 
 def aligned_plan(shard, wide, ranks):
@@ -831,17 +827,19 @@
     return rows, spare, fits
 
 
-def gather_blocks(block, z, x, rows):
-    ring, by_x, by_y, corner = [block], [], [], [None] * 4
-    r1, x0, y0 = together((ring_z(block), swap_x(block), swap_y(block)))
-    r2, x1, y1 = together((ring_z(r1), swap_x(r1), swap_y(r1)))
-    r3, x2, y2, d0, d1 = together((ring_z(r2), swap_x(r2), swap_y(r2), swap_y(x0), swap_x(y1)))
-    x3, y3, d2 = swap_x(r3), swap_y(r3), swap_y(x2)
-    d3 = swap_x(y3)
+def window_places(z, x):
     planes = jnp.mod(z - jnp.arange(4, dtype=jnp.int32), 4)
-    at = jnp.concatenate([2 * planes + x, 2 * planes + 1 - x])
-    pieces = [block, r1, r2, r3, x0, x1, x2, x3, y0, y1, y2, y3, d0, d1, d2, d3]
-    return merge_blocks(at, pieces, rows)
+    return jnp.concatenate([2 * planes + x, 2 * planes + 1 - x])
+
+
+def gather_blocks(r0, z, x, rows):
+    r1, x0, y0 = ring_z(r0), swap_x(r0), swap_y(r0)
+    r2, x1, d0 = ring_z(r1), swap_x(after(r1, x0)), swap_y(after(x0, y0))
+    r3, x2, y1 = ring_z(r2), swap_x(after(r2, x1)), swap_y(after(r1, d0))
+    d1, x3, y2 = ring_z(after(d0, r3)), swap_x(after(r3, x2)), swap_y(after(r2, y1))
+    y3, d2, d3 = ring_z(after(y2, d1)), swap_x(after(y2, x3)), swap_y(after(x3, y2))
+    pieces = [r0, r1, r2, r3, x0, x1, x2, x3, y0, y1, y2, y3, d0, d1, d2, d3]
+    return merge_blocks(window_places(z, x), pieces, rows)
 
 
 def add_low(*terms):
@@ -852,22 +850,25 @@
 
 
 def reduce_windows(own, got, z, x, rows):
-    kinds = ("y", "x", "y", "x")
-    planes = jnp.mod(z - jnp.array([1, 2, 3, 0], jnp.int32), 4)
-    at = jnp.stack([2 * planes + x, 2 * planes + 1 - x], axis=1).reshape(-1)
-    parts = split_windows(at[:4], kinds[:2], own, got, rows) + split_windows(
-        at[4:], kinds[2:], own, got, rows
-    )
-    first, second = [], []
-    for kind, (send, pass_on, keep) in zip(kinds, parts):
-        one, two = (swap_y, swap_x) if kind == "y" else (swap_x, swap_y)
-        first.append(one(send))
-        second.append(two(add_low(pass_on, first[-1][0])))
-    ring = None
-    for q in range(3):
-        terms = [parts[q][2], first[q][1], second[q]] + ([] if ring is None else [ring])
-        ring = ring_z(add_low(*terms))
-    return parts[3][2], first[3], second[3], ring
+    at = window_places(z, x)
+    a = split_windows(at, ("Y3", "D2", "D3", "Y2", "X3", "D1"), own, got, rows)
+    a |= split_windows(
+        at, ("X2", "Y1", "R3", "R2", "D0", "X1", "R1", "X0", "Y0", "R0"), own, got, rows
+    )
+    z1, x1, y1 = ring_back(a["Y3"]), swap_x(a["D2"]), swap_y(a["D3"])
+    z2 = ring_back(after(a["D1"], z1))
+    x2 = swap_x(add_low(a["X3"], y1))
+    y2 = swap_y(add_low(a["Y2"], z1, x1))
+    z3 = ring_back(add_low(a["R3"], x2))
+    x3 = swap_x(after(a["X2"], x2))
+    y3 = swap_y(after(a["Y1"], y2))
+    z4 = ring_back(add_low(a["R2"], y2, z3, x3))
+    x4 = swap_x(after(a["X1"], x3))
+    y4 = swap_y(after(add_low(a["D0"], z2), y3))
+    z5 = ring_back(add_low(a["R1"], y3, z4, x4))
+    x5 = swap_x(add_low(a["X0"], y4))
+    y5 = swap_y(after(a["Y0"], y4))
+    return a["R0"], z5, x5, y5
 
 
 def gather_plain(params):
@@ -901,7 +902,8 @@
         place = jnp.stack([at_wide, at_narrow // 2, at_narrow % 2]).astype(jnp.int32)
         block = own_block(place, params, rows, spare, wide)
         own_att, own_ff = gather_blocks(block, at_wide // 2, at_wide % 2, rows)
-        got_att, got_ff = swap_core(own_att), swap_core(own_ff)
+        got_att = swap_core(own_att)
+        got_ff = swap_core(after(own_ff, got_att))
     else:
         place = jnp.zeros((3,), jnp.int32)
         (own_att, own_ff), (got_att, got_ff) = gather_plain(params)

time: 283 us -> 251 us (0.89)
  waiting for transfers between devices: 142 us -> 99.8 us
  starting transfers between devices: 27.7 us -> 36.1 us
  other arithmetic: 4.26 us -> 7.31 us
    ppermute x10, waiting for transfers between devices: 89.1 us -> 22.5 us  [swap_y(): return lax.ppermute(a, 'narrow', Y_SWAP)]
    ppermute x0 -> x5, waiting for transfers between devices: none -> 34.6 us  [ring_back(): return lax.ppermute(a, 'wide', [(j, i) for i, j in Z_RING])]
    ppermute x6 -> x5, waiting for transfers between devices: 24.4 us -> 11.3 us  [ring_z(): return lax.ppermute(a, 'wide', Z_RING)]
    ppermute x0 -> x5, starting transfers between devices: none -> 12.9 us  [ring_back(): return lax.ppermute(a, 'wide', [(j, i) for i, j in Z_RING])]
    ppermute x10, waiting for transfers between devices: 14.8 us -> 21.8 us  [swap_x(): return lax.ppermute(a, 'wide', X_SWAP)]
    ppermute x4, waiting for transfers between devices: 13.3 us -> 9.6 us  [swap_core(): return lax.ppermute(a, 'narrow', CORE_SWAP)]
    convert_element_type x7, other arithmetic: 2.19 us -> 5.26 us  [add_low(): return total.astype(BF)]
  transfers between devices with their start and end apart: 30 -> 34, of which waited for: 20 -> 23; matrix products, arithmetic and copies ran while one was open for 2% -> 3% of each run, Pallas kernels for 20% -> 22%
where the time goes in v3:
time: 251 us; the launch traced here: 250 us
  Pallas kernels  102 us (41%)
  waiting for transfers between devices  99.8 us (40%)
  starting transfers between devices  36.1 us (14%)
  other arithmetic  7.31 us (3%)
  local copies, waits for them, and re-layouts  4.26 us (2%)
    pallas_call x8, Pallas kernels, call(): pl.pallas_call(kernel, grid_spec=pltpu.PrefetchScalarGridSpec(num_scalar_...  102 us
    ppermute x5, waiting for transfers between devices, ring_back(): return lax.ppermute(a, 'wide', [(j, i) for i, j in Z_RING])  34.6 us
    ppermute x10, waiting for transfers between devices, swap_y(): return lax.ppermute(a, 'narrow', Y_SWAP)  22.5 us
    ppermute x10, waiting for transfers between devices, swap_x(): return lax.ppermute(a, 'wide', X_SWAP)  21.8 us
    ppermute x5, starting transfers between devices, ring_back(): return lax.ppermute(a, 'wide', [(j, i) for i, j in Z_RING])  12.9 us
    ppermute x5, waiting for transfers between devices, ring_z(): return lax.ppermute(a, 'wide', Z_RING)  11.3 us
    ppermute x10, starting transfers between devices, swap_x(): return lax.ppermute(a, 'wide', X_SWAP)  10.8 us
    ppermute x10, starting transfers between devices, swap_y(): return lax.ppermute(a, 'narrow', Y_SWAP)  9.87 us
  transfers between devices with their start and end apart: 34, of which 23 were waited for; matrix products, arithmetic and copies ran while one was open for 3% of the time, Pallas kernels for 22%

profile of v3, /device:TPU:0, one launch (start us, length us, event | category | flops | bytes accessed | tf_op | source)
XLA Modules:
  0.0 250.2 jit_solution(10412893393090210577)
XLA Ops:
  2.6 3.1 %collective-permute-start.7 = (bf16[304,768]{1,0:T(8,128)(2,1)S(1)}, bf16[304,768]{1,0:T(8,128)(2,1)S(1)}, u32[]{:S(2)}, u32[]{:S(2)}) collective-permute-start(bf16[304,768]{1,0:T(8,128)(2,1)S(1)} %own_block.1.refs_0_), channel_id=1, source_target_pairs={{0,2},{1,3},{2,0},{3,1},{4,6},{5,7},{6,4},{7,5},{8,10},{9,11},{10,... | collective-permute-start | bytes 1400840 | tf_op jit(solution)/shard_map/ppermute | solution.py:796
  8.7 7.6 %collective-permute-done.7.refs_8_ = bf16[304,768]{1,0:T(8,128)(2,1)S(1)} collective-permute-done((bf16[304,768]{1,0:T(8,128)(2,1)S(1)}, bf16[304,768]{1,0:T(8,128)(2,1)S(1)}, u32[]{:S(2)}, u32[]{:S(2)}) %collective-permute-start.7) | collective-permute-done | bytes 466976 | tf_op jit(solution)/shard_map/ppermute | solution.py:796
  21.4 7.7 %collective-permute-done.8.refs_12_ = bf16[304,768]{1,0:T(8,128)(2,1)S(1)} collective-permute-done((bf16[304,768]{1,0:T(8,128)(2,1)S(1)}, bf16[304,768]{1,0:T(8,128)(2,1)S(1)}, u32[]{:S(2)}, u32[]{:S(2)}) %collective-permute-start.8) | collective-permute-done | bytes 466976 | tf_op jit(solution)/shard_map/ppermute | solution.py:796
  35.5 4.5 %collective-permute-done.9.refs_9_ = bf16[304,768]{1,0:T(8,128)(2,1)S(1)} collective-permute-done((bf16[304,768]{1,0:T(8,128)(2,1)S(1)}, bf16[304,768]{1,0:T(8,128)(2,1)S(1)}, u32[]{:S(2)}, u32[]{:S(2)}) %collective-permute-start.9) | collective-permute-done | bytes 466976 | tf_op jit(solution)/shard_map/ppermute | solution.py:796
  40.6 3.3 %collective-permute-done.5.refs_6_ = bf16[304,768]{1,0:T(8,128)(2,1)S(1)} collective-permute-done((bf16[304,768]{1,0:T(8,128)(2,1)S(1)}, bf16[304,768]{1,0:T(8,128)(2,1)S(1)}, u32[]{:S(2)}, u32[]{:S(2)}) %collective-permute-start.5) | collective-permute-done | bytes 466976 | tf_op jit(solution)/shard_map/ppermute | solution.py:792
  49.7 7.9 %collective-permute-done.6.refs_7_ = bf16[304,768]{1,0:T(8,128)(2,1)} collective-permute-done((bf16[304,768]{1,0:T(8,128)(2,1)S(1)}, bf16[304,768]{1,0:T(8,128)(2,1)}, u32[]{:S(2)}, u32[]{:S(2)}) %collective-permute-start.6) | collective-permute-done | bytes 466976 | tf_op jit(solution)/shard_map/ppermute | solution.py:792
  60.5 6.0 %collective-permute-done.13.refs_14_ = bf16[304,768]{1,0:T(8,128)(2,1)} collective-permute-done((bf16[304,768]{1,0:T(8,128)(2,1)}, bf16[304,768]{1,0:T(8,128)(2,1)}, u32[]{:S(2)}, u32[]{:S(2)}) %collective-permute-start.13) | collective-permute-done | bytes 466976 | tf_op jit(solution)/shard_map/ppermute | solution.py:792
  67.0 3.6 %collective-permute-done.12.refs_11_ = bf16[304,768]{1,0:T(8,128)(2,1)} collective-permute-done((bf16[304,768]{1,0:T(8,128)(2,1)}, bf16[304,768]{1,0:T(8,128)(2,1)}, u32[]{:S(2)}, u32[]{:S(2)}) %collective-permute-start.12) | collective-permute-done | bytes 466976 | tf_op jit(solution)/shard_map/ppermute | solution.py:800
  70.7 6.4 %merge_weights.1 = (bf16[2,784,768]{2,1,0:T(8,128)(2,1)}, bf16[2,1536,768]{2,1,0:T(8,128)(2,1)}) custom-call(s32[8]{0:T(128)} %pad_add_fusion.2.at_ref, bf16[304,768]{1,0:T(8,128)(2,1)} %copy-done.2, bf16[304,768]{1,0:T(8,128)(2,1)} %copy-done.11, bf16[304,768]{1,0:T(8,128)(2,1)} %copy-done.14, bf16[304,768]{1,0:T(8,128)(2,1)} %copy-done.17, ...), custom_call_target="tpu_custom_call" | custom-call | tf_op jit(solution)/shard_map/merge_weights/pallas_call | solution.py:106
  77.1 4.8 %collective-permute-done.15.mq1_ref.wo1_ref = bf16[2,784,768]{2,1,0:T(8,128)(2,1)S(1)} collective-permute-done((bf16[2,784,768]{2,1,0:T(8,128)(2,1)}, bf16[2,784,768]{2,1,0:T(8,128)(2,1)S(1)}, u32[]{:S(2)}, u32[]{:S(2)}) %collective-permute-start.15) | collective-permute-done | bytes 2408480 | tf_op jit(solution)/shard_map/ppermute | solution.py:808
  84.3 20.0 %attention_forward.1 = (bf16[4,512,576]{2,1,0:T(8,128)(2,1)}, bf16[4,768,576]{2,1,0:T(8,128)(2,1)}, bf16[4,512,192]{2,1,0:T(8,128)(2,1)}, bf16[4,3,512,512]{3,2,...) custom-call(s32[7]{0:T(128)} %pad_add_fusion.1.scal_ref, ...), custom_call_target="tpu_custom_call" | custom-call | flops 6000000000 | bytes 24000000 | tf_op jit(solution)/shard_map/attention_forward/pallas_call | solution.py:106
  104.3 30.0 %feed_forward.1 = (bf16[512,768]{1,0:T(8,128)(2,1)}, bf16[2,1536,768]{2,1,0:T(8,128)(2,1)}, bf16[2,1536,768]{2,1,0:T(8,128)(2,1)}, f32[512,768]{1,0:T(8,128)}, b...) custom-call(s32[3]{0:T(128)} %copy-done.6, f32[512,768]{1,0:T(8,128)} %get-tuple-element.75.n1_ref, ...), custom_call_target="tpu_custom_call" | custom-call | flops 14499999744 | bytes 36000000 | tf_op jit(solution)/shard_map/feed_forward/pallas_call | solution.py:106
  134.8 29.6 %attention_backward.1 = (bf16[2,784,768]{2,1,0:T(8,128)(2,1)}, bf16[2,784,768]{2,1,0:T(8,128)(2,1)}, f32[512,768]{1,0:T(8,128)}) custom-call(s32[3]{0:T(128)} %copy-done.6, bf16[512,768]{1,0:T(8,128)(2,1)} %get-tuple-element.80.ga_ref, bf16[2,784,768]{2,1,0:T(8,128)(2,1)} %get-tuple-element.74.mq0_ref.wo0_ref, bf16[2,784,768]{2,1,0:T(8,128)(2,1)} %copy-done.22, ...), custom_call_target="tpu_custom_call" | custom-call | flops 12000000000 | bytes 30000000 | tf_op jit(solution)/shard_map/attention_backward/pallas_call | solution.py:106
  164.5 4.8 %collective-permute-done.17.got_att = bf16[2,784,768]{2,1,0:T(8,128)(2,1)S(1)} collective-permute-done((bf16[2,784,768]{2,1,0:T(8,128)(2,1)}, bf16[2,784,768]{2,1,0:T(8,128)(2,1)S(1)}, u32[]{:S(2)}, u32[]{:S(2)}) %collective-permute-start.17) | collective-permute-done | bytes 2408480 | tf_op jit(solution)/shard_map/ppermute | solution.py:808
  170.7 4.9 %split_windows.3 = (bf16[304,768]{1,0:T(8,128)(2,1)}, bf16[304,768]{1,0:T(8,128)(2,1)}, bf16[304,768]{1,0:T(8,128)(2,1)}, bf16[304,768]{1,0:T(8,128)(2,1)}, bf16...) custom-call(s32[8]{0:T(128)} %pad_add_fusion.2.at_ref, bf16[2,784,768]{2,1,0:T(8,128)(2,1)} %get-tuple-element.90.own_att, ...), custom_call_target="tpu_custom_call" | custom-call | tf_op jit(solution)/shard_map/split_windows/pallas_call | solution.py:106
  178.3 10.3 %collective-permute-done.19 = bf16[304,768]{1,0:T(8,128)(2,1)S(1)} collective-permute-done((bf16[304,768]{1,0:T(8,128)(2,1)}, bf16[304,768]{1,0:T(8,128)(2,1)S(1)}, u32[]{:S(2)}, u32[]{:S(2)}) %collective-permute-start.19) | collective-permute-done | bytes 466976 | tf_op jit(solution)/shard_map/ppermute | solution.py:804
  193.8 6.7 %split_windows.2 = (bf16[304,768]{1,0:T(8,128)(2,1)}, bf16[304,768]{1,0:T(8,128)(2,1)}, bf16[304,768]{1,0:T(8,128)(2,1)}, bf16[304,768]{1,0:T(8,128)(2,1)}, bf16...) custom-call(s32[8]{0:T(128)} %pad_add_fusion.2.at_ref, ...), custom_call_target="tpu_custom_call" | custom-call | tf_op jit(solution)/shard_map/split_windows/pallas_call | solution.py:106
  208.9 5.3 %collective-permute-done.30 = bf16[304,768]{1,0:T(8,128)(2,1)S(1)} collective-permute-done((bf16[304,768]{1,0:T(8,128)(2,1)S(1)}, bf16[304,768]{1,0:T(8,128)(2,1)S(1)}, u32[]{:S(2)}, u32[]{:S(2)}) %collective-permute-start.30) | collective-permute-done | bytes 466976 | tf_op jit(solution)/shard_map/ppermute | solution.py:804
  216.9 5.1 %collective-permute-done.25 = bf16[304,768]{1,0:T(8,128)(2,1)S(1)} collective-permute-done((bf16[304,768]{1,0:T(8,128)(2,1)S(1)}, bf16[304,768]{1,0:T(8,128)(2,1)S(1)}, u32[]{:S(2)}, u32[]{:S(2)}) %collective-permute-start.25) | collective-permute-done | bytes 466976 | tf_op jit(solution)/shard_map/ppermute | solution.py:804
  222.2 4.1 %collective-permute-start.27 = (bf16[304,768]{1,0:T(8,128)(2,1)S(1)}, bf16[304,768]{1,0:T(8,128)(2,1)S(1)}, u32[]{:S(2)}, u32[]{:S(2)}) collective-permute-start(bf16[304,768]{1,0:T(8,128)(2,1)S(1)} %add_convert_fusion.3), channel_id=1, source_target_pairs={{8,0},{12,4},{16,8},{20,12},{24,16},{28,20},{0,24},{4,28},{9,1},{1... | collective-permute-start | bytes 1400840 | tf_op jit(solution)/shard_map/ppermute | solution.py:804
  228.0 6.6 %collective-permute-done.27 = bf16[304,768]{1,0:T(8,128)(2,1)S(1)} collective-permute-done((bf16[304,768]{1,0:T(8,128)(2,1)S(1)}, bf16[304,768]{1,0:T(8,128)(2,1)S(1)}, u32[]{:S(2)}, u32[]{:S(2)}) %collective-permute-start.27) | collective-permute-done | bytes 466976 | tf_op jit(solution)/shard_map/ppermute | solution.py:804
  234.9 4.3 %collective-permute-start.29 = (bf16[304,768]{1,0:T(8,128)(2,1)S(1)}, bf16[304,768]{1,0:T(8,128)(2,1)S(1)}, u32[]{:S(2)}, u32[]{:S(2)}) collective-permute-start(bf16[304,768]{1,0:T(8,128)(2,1)S(1)} %add_convert_fusion.2), channel_id=1, source_target_pairs={{8,0},{12,4},{16,8},{20,12},{24,16},{28,20},{0,24},{4,28},{9,1},{1... | collective-permute-start | bytes 1400840 | tf_op jit(solution)/shard_map/ppermute | solution.py:804
  239.2 7.4 %collective-permute-done.29.near_ref = bf16[304,768]{1,0:T(8,128)(2,1)S(1)} collective-permute-done((bf16[304,768]{1,0:T(8,128)(2,1)S(1)}, bf16[304,768]{1,0:T(8,128)(2,1)S(1)}, u32[]{:S(2)}, u32[]{:S(2)}) %collective-permute-start.29) | collective-permute-done | bytes 466976 | tf_op jit(solution)/shard_map/ppermute | solution.py:804
  246.6 3.6 %update_shard.1 = (f32[1,221568]{1,0:T(1,128)}, f32[1,221568]{1,0:T(1,128)}, f32[1,221568]{1,0:T(1,128)}, f32[1,221568]{1,0:T(1,128)}, bf16[1,221568]{1,0:T(2,128)(2,1)}) custom-call(s32[3]{0:T(128)S(1)} %copy-done.7, bf16[304,768]{1,0:T(8,128)(2,1)S(1)} %copy-done.5, bf16[304,768]{1,0:T(8,128)(2,1)S(1)} %collective-permute-done.29.near_ref, ...), custom_call_target="tpu_custom_call" | custom-call | tf_op jit(solution)/shard_map/update_shard/pallas_call | solution.py:106
  (120 shorter events, 51.8 us)
Async XLA Ops:
  2.6 13.8 %collective-permute-start.7 = (bf16[304,768]{1,0:T(8,128)(2,1)S(1)}, bf16[304,768]{1,0:T(8,128)(2,1)S(1)}, u32[]{:S(2)}, u32[]{:S(2)}) collective-permute-start(bf16[304,768]{1,0:T(8,128)(2,1)S(1)} %own_block.1.refs_0_), channel_id=1, source_target_pairs={{0,2},{1,3},{2,0},{3,1},{4,6},{5,7},{6,4},{7,5},{8,10},{9,11},{10,... | collective-permute-start | bytes 1400840 | tf_op jit(solution)/shard_map/ppermute | solution.py:796
  5.7 12.2 %collective-permute-start.3 = (bf16[304,768]{1,0:T(8,128)(2,1)S(1)}, bf16[304,768]{1,0:T(8,128)(2,1)S(1)}, u32[]{:S(2)}, u32[]{:S(2)}) collective-permute-start(bf16[304,768]{1,0:T(8,128)(2,1)S(1)} %own_block.1.refs_0_), channel_id=1, source_target_pairs={{0,4},{4,0},{8,12},{12,8},{16,20},{20,16},{24,28},{28,24},{1,5},{5... | collective-permute-start | bytes 1400840 | tf_op jit(solution)/shard_map/ppermute | solution.py:792
  7.2 13.7 %collective-permute-start = (bf16[304,768]{1,0:T(8,128)(2,1)S(1)}, bf16[304,768]{1,0:T(8,128)(2,1)S(1)}, u32[]{:S(2)}, u32[]{:S(2)}) collective-permute-start(bf16[304,768]{1,0:T(8,128)(2,1)S(1)} %own_block.1.refs_0_), channel_id=1, source_target_pairs={{0,8},{4,12},{8,16},{12,20},{16,24},{20,28},{24,0},{28,4},{1,9},{5... | collective-permute-start | bytes 1400840 | tf_op jit(solution)/shard_map/ppermute | solution.py:800
  17.8 11.3 %collective-permute-start.8 = (bf16[304,768]{1,0:T(8,128)(2,1)S(1)}, bf16[304,768]{1,0:T(8,128)(2,1)S(1)}, u32[]{:S(2)}, u32[]{:S(2)}) collective-permute-start(bf16[304,768]{1,0:T(8,128)(2,1)S(1)} %collective-permute-done.3.refs_4_), channel_id=1, source_target_pairs={{0,2},{1,3},{2,0},{3,1},{4,6},{5,7},{6,4},{7,5},{8,10},{9,11},{10,... | collective-permute-start | bytes 1400840 | tf_op jit(solution)/shard_map/ppermute | solution.py:796
  20.9 11.1 %collective-permute-start.4 = (bf16[304,768]{1,0:T(8,128)(2,1)S(1)}, bf16[304,768]{1,0:T(8,128)(2,1)S(1)}, u32[]{:S(2)}, u32[]{:S(2)}) collective-permute-start(bf16[304,768]{1,0:T(8,128)(2,1)S(1)} %collective-permute-done.refs_1_), channel_id=1, source_target_pairs={{0,4},{4,0},{8,12},{12,8},{16,20},{20,16},{24,28},{28,24},{1,5},{5... | collective-permute-start | bytes 1400840 | tf_op jit(solution)/shard_map/ppermute | solution.py:792
  21.4 12.6 %collective-permute-start.1 = (bf16[304,768]{1,0:T(8,128)(2,1)S(1)}, bf16[304,768]{1,0:T(8,128)(2,1)S(1)}, u32[]{:S(2)}, u32[]{:S(2)}) collective-permute-start(bf16[304,768]{1,0:T(8,128)(2,1)S(1)} %collective-permute-done.refs_1_), channel_id=1, source_target_pairs={{0,8},{4,12},{8,16},{12,20},{16,24},{20,28},{24,0},{28,4},{1,9},{5... | collective-permute-start | bytes 1400840 | tf_op jit(solution)/shard_map/ppermute | solution.py:800
  35.5 11.5 %collective-permute-start.2 = (bf16[304,768]{1,0:T(8,128)(2,1)S(1)}, bf16[304,768]{1,0:T(8,128)(2,1)S(1)}, u32[]{:S(2)}, u32[]{:S(2)}) collective-permute-start(bf16[304,768]{1,0:T(8,128)(2,1)S(1)} %collective-permute-done.1.refs_2_), channel_id=1, source_target_pairs={{0,8},{4,12},{8,16},{12,20},{16,24},{20,28},{24,0},{28,4},{1,9},{5... | collective-permute-start | bytes 1400840 | tf_op jit(solution)/shard_map/ppermute | solution.py:800
  47.5 11.6 %collective-permute-start.11 = (bf16[304,768]{1,0:T(8,128)(2,1)S(1)}, bf16[304,768]{1,0:T(8,128)(2,1)S(1)}, u32[]{:S(2)}, u32[]{:S(2)}) collective-permute-start(bf16[304,768]{1,0:T(8,128)(2,1)S(1)} %collective-permute-done.8.refs_12_), channel_id=1, source_target_pairs={{0,8},{4,12},{8,16},{12,20},{16,24},{20,28},{24,0},{28,4},{1,9},{5... | collective-permute-start | bytes 1400840 | tf_op jit(solution)/shard_map/ppermute | solution.py:800
  81.9 22.3 %collective-permute-start.16 = (bf16[2,1536,768]{2,1,0:T(8,128)(2,1)}, bf16[2,1536,768]{2,1,0:T(8,128)(2,1)}, u32[]{:S(2)}, u32[]{:S(2)}) collective-permute-start(bf16[2,1536,768]{2,1,0:T(8,128)(2,1)} %get-tuple-element.78.up0_ref.down0_ref), channel_id=1, source_target_pairs={{0,1},{1,0},{2,3},{3,2},{4,5},{5,4},{6,7},{7,6},{8,9},{9,8},{10,11... | collective-permute-start | bytes 14155784 | tf_op jit(solution)/shard_map/ppermute | solution.py:808
  134.2 35.1 %collective-permute-start.18 = (bf16[2,1536,768]{2,1,0:T(8,128)(2,1)}, bf16[2,1536,768]{2,1,0:T(8,128)(2,1)}, u32[]{:S(2)}, u32[]{:S(2)}) collective-permute-start(bf16[2,1536,768]{2,1,0:T(8,128)(2,1)} %get-tuple-element.93), channel_id=1, source_target_pairs={{0,1},{1,0},{2,3},{3,2},{4,5},{5,4},{6,7},{7,6},{8,9},{9,8},{10,11... | collective-permute-start | bytes 14155784 | tf_op jit(solution)/shard_map/ppermute | solution.py:808
  175.6 13.0 %collective-permute-start.19 = (bf16[304,768]{1,0:T(8,128)(2,1)}, bf16[304,768]{1,0:T(8,128)(2,1)S(1)}, u32[]{:S(2)}, u32[]{:S(2)}) collective-permute-start(bf16[304,768]{1,0:T(8,128)(2,1)} %get-tuple-element.98), channel_id=1, source_target_pairs={{8,0},{12,4},{16,8},{20,12},{24,16},{28,20},{0,24},{4,28},{9,1},{1... | collective-permute-start | bytes 1400840 | tf_op jit(solution)/shard_map/ppermute | solution.py:804
  175.6 13.0 %collective-permute-start.20 = (bf16[304,768]{1,0:T(8,128)(2,1)}, bf16[304,768]{1,0:T(8,128)(2,1)S(1)}, u32[]{:S(2)}, u32[]{:S(2)}) collective-permute-start(bf16[304,768]{1,0:T(8,128)(2,1)} %get-tuple-element.99), channel_id=1, source_target_pairs={{0,4},{4,0},{8,12},{12,8},{16,20},{20,16},{24,28},{28,24},{1,5},{5... | collective-permute-start | bytes 1400840 | tf_op jit(solution)/shard_map/ppermute | solution.py:792
  176.8 14.2 %collective-permute-start.23 = (bf16[304,768]{1,0:T(8,128)(2,1)}, bf16[304,768]{1,0:T(8,128)(2,1)S(1)}, u32[]{:S(2)}, u32[]{:S(2)}) collective-permute-start(bf16[304,768]{1,0:T(8,128)(2,1)} %get-tuple-element.104), channel_id=1, source_target_pairs={{0,2},{1,3},{2,0},{3,1},{4,6},{5,7},{6,4},{7,5},{8,10},{9,11},{10,... | collective-permute-start | bytes 1400840 | tf_op jit(solution)/shard_map/ppermute | solution.py:796
  189.9 12.7 %collective-permute-start.21 = (bf16[304,768]{1,0:T(8,128)(2,1)S(1)}, bf16[304,768]{1,0:T(8,128)(2,1)S(1)}, u32[]{:S(2)}, u32[]{:S(2)}) collective-permute-start(bf16[304,768]{1,0:T(8,128)(2,1)S(1)} %add_convert_fusion.6), channel_id=1, source_target_pairs={{0,2},{1,3},{2,0},{3,1},{4,6},{5,7},{6,4},{7,5},{8,10},{9,11},{10,... | collective-permute-start | bytes 1400840 | tf_op jit(solution)/shard_map/ppermute | solution.py:796
  192.2 11.7 %collective-permute-start.24 = (bf16[304,768]{1,0:T(8,128)(2,1)S(1)}, bf16[304,768]{1,0:T(8,128)(2,1)S(1)}, u32[]{:S(2)}, u32[]{:S(2)}) collective-permute-start(bf16[304,768]{1,0:T(8,128)(2,1)S(1)} %add_convert_fusion.5), channel_id=1, source_target_pairs={{0,4},{4,0},{8,12},{12,8},{16,20},{20,16},{24,28},{28,24},{1,5},{5... | collective-permute-start | bytes 1400840 | tf_op jit(solution)/shard_map/ppermute | solution.py:792
  200.5 13.6 %collective-permute-start.30 = (bf16[304,768]{1,0:T(8,128)(2,1)S(1)}, bf16[304,768]{1,0:T(8,128)(2,1)S(1)}, u32[]{:S(2)}, u32[]{:S(2)}) collective-permute-start(bf16[304,768]{1,0:T(8,128)(2,1)S(1)} %copy-done.26), channel_id=1, source_target_pairs={{8,0},{12,4},{16,8},{20,12},{24,16},{28,20},{0,24},{4,28},{9,1},{1... | collective-permute-start | bytes 1400840 | tf_op jit(solution)/shard_map/ppermute | solution.py:804
  202.6 12.7 %collective-permute-start.22 = (bf16[304,768]{1,0:T(8,128)(2,1)}, bf16[304,768]{1,0:T(8,128)(2,1)S(1)}, u32[]{:S(2)}, u32[]{:S(2)}) collective-permute-start(bf16[304,768]{1,0:T(8,128)(2,1)} %get-tuple-element.100), channel_id=1, source_target_pairs={{0,2},{1,3},{2,0},{3,1},{4,6},{5,7},{6,4},{7,5},{8,10},{9,11},{10,... | collective-permute-start | bytes 1400840 | tf_op jit(solution)/shard_map/ppermute | solution.py:796
  203.8 12.0 %collective-permute-start.26 = (bf16[304,768]{1,0:T(8,128)(2,1)}, bf16[304,768]{1,0:T(8,128)(2,1)S(1)}, u32[]{:S(2)}, u32[]{:S(2)}) collective-permute-start(bf16[304,768]{1,0:T(8,128)(2,1)} %get-tuple-element.106), channel_id=1, source_target_pairs={{0,4},{4,0},{8,12},{12,8},{16,20},{20,16},{24,28},{28,24},{1,5},{5... | collective-permute-start | bytes 1400840 | tf_op jit(solution)/shard_map/ppermute | solution.py:792
  206.5 15.4 %collective-permute-start.25 = (bf16[304,768]{1,0:T(8,128)(2,1)S(1)}, bf16[304,768]{1,0:T(8,128)(2,1)S(1)}, u32[]{:S(2)}, u32[]{:S(2)}) collective-permute-start(bf16[304,768]{1,0:T(8,128)(2,1)S(1)} %add_convert_fusion.4), channel_id=1, source_target_pairs={{8,0},{12,4},{16,8},{20,12},{24,16},{28,20},{0,24},{4,28},{9,1},{1... | collective-permute-start | bytes 1400840 | tf_op jit(solution)/shard_map/ppermute | solution.py:804
  215.9 12.1 %collective-permute-start.28 = (bf16[304,768]{1,0:T(8,128)(2,1)S(1)}, bf16[304,768]{1,0:T(8,128)(2,1)S(1)}, u32[]{:S(2)}, u32[]{:S(2)}) collective-permute-start(bf16[304,768]{1,0:T(8,128)(2,1)S(1)} %copy-done.25), channel_id=1, source_target_pairs={{0,4},{4,0},{8,12},{12,8},{16,20},{20,16},{24,28},{28,24},{1,5},{5... | collective-permute-start | bytes 1400840 | tf_op jit(solution)/shard_map/ppermute | solution.py:792
  222.2 12.4 %collective-permute-start.27 = (bf16[304,768]{1,0:T(8,128)(2,1)S(1)}, bf16[304,768]{1,0:T(8,128)(2,1)S(1)}, u32[]{:S(2)}, u32[]{:S(2)}) collective-permute-start(bf16[304,768]{1,0:T(8,128)(2,1)S(1)} %add_convert_fusion.3), channel_id=1, source_target_pairs={{8,0},{12,4},{16,8},{20,12},{24,16},{28,20},{0,24},{4,28},{9,1},{1... | collective-permute-start | bytes 1400840 | tf_op jit(solution)/shard_map/ppermute | solution.py:804
  226.3 12.8 %collective-permute-start.33 = (bf16[304,768]{1,0:T(8,128)(2,1)S(1)}, bf16[304,768]{1,0:T(8,128)(2,1)S(1)}, u32[]{:S(2)}, u32[]{:S(2)}) collective-permute-start(bf16[304,768]{1,0:T(8,128)(2,1)S(1)} %copy-done.24), channel_id=1, source_target_pairs={{0,2},{1,3},{2,0},{3,1},{4,6},{5,7},{6,4},{7,5},{8,10},{9,11},{10,... | collective-permute-start | bytes 1400840 | tf_op jit(solution)/shard_map/ppermute | solution.py:796
  227.0 12.2 %collective-permute-start.32 = (bf16[304,768]{1,0:T(8,128)(2,1)S(1)}, bf16[304,768]{1,0:T(8,128)(2,1)S(1)}, u32[]{:S(2)}, u32[]{:S(2)}) collective-permute-start(bf16[304,768]{1,0:T(8,128)(2,1)S(1)} %add_convert_fusion), channel_id=1, source_target_pairs={{0,4},{4,0},{8,12},{12,8},{16,20},{20,16},{24,28},{28,24},{1,5},{5... | collective-permute-start | bytes 1400840 | tf_op jit(solution)/shard_map/ppermute | solution.py:792
  234.9 11.7 %collective-permute-start.29 = (bf16[304,768]{1,0:T(8,128)(2,1)S(1)}, bf16[304,768]{1,0:T(8,128)(2,1)S(1)}, u32[]{:S(2)}, u32[]{:S(2)}) collective-permute-start(bf16[304,768]{1,0:T(8,128)(2,1)S(1)} %add_convert_fusion.2), channel_id=1, source_target_pairs={{8,0},{12,4},{16,8},{20,12},{24,16},{28,20},{0,24},{4,28},{9,1},{1... | collective-permute-start | bytes 1400840 | tf_op jit(solution)/shard_map/ppermute | solution.py:804
  (37 other events, 829.7 us)

commit v4 on v3

--- a/solution.py
+++ b/solution.py
@@ -19,7 +19,7 @@
 HPR = HEADS // RANKS
 SLOTS = 2
 QKV_ROWS = 3 * PART
-TILE_ROWS = 16
+TILE_ROWS = 8
 MAT_ROWS = 3 * D
 PAD_ROWS = MAT_ROWS + TILE_ROWS
 ATT_ROWS = D + TILE_ROWS
@@ -495,7 +495,7 @@
 def ffn_kernel(
     place_ref, n1_ref, r1_ref, og_ref, up0_ref, down0_ref, up1_ref, down1_ref, tails_ref,
     block_ref, grad0_ref, grad1_ref, grad_one_ref, ga_ref, vec_ref, bup_ref,
-    fn_s, fl_s, up_s, act_s, down_s, gd_s, gf_s,
+    fn_s, fl_s, slope_s, act_s, down_s, gd_s, gf_s,
 ):
     step = pl.program_id(0)
     inv_root2 = 1.0 / math.sqrt(2.0)
@@ -511,8 +511,9 @@
     def forward(slot, up_ref, down_ref):
         bias = jnp.concatenate([tails_ref[slot, 0:1, 384:768], tails_ref[slot, 1:2, 0:384]], axis=1)
         up = mm(fl_s[...], up_ref[0]) + bias.astype(F32)
-        up_s[slot] = up
-        act = (0.5 * up * (1.0 + lax.erf(up * inv_root2))).astype(BF)
+        half = 0.5 * (1.0 + lax.erf(up * inv_root2))
+        act = (up * half).astype(BF)
+        slope_s[slot] = half + up * jnp.exp(-0.5 * up * up) * (1.0 / math.sqrt(2.0 * math.pi))
         act_s[slot] = act
         down_s[...] += mm(act, down_ref[0])
 
@@ -542,11 +543,7 @@
     def backward(slot, up_ref, down_ref, grad_ref):
         gd = gd_s[...]
         grad_ref[0, D:FF_ROWS, :] = mm_tn(act_s[slot], gd).astype(BF)
-        up = up_s[slot]
-        slope = 0.5 * (1.0 + lax.erf(up * inv_root2)) + up * jnp.exp(-0.5 * up * up) * (
-            1.0 / math.sqrt(2.0 * math.pi)
-        )
-        gu = (mm_nt(gd, down_ref[0]) * slope).astype(BF)
+        gu = (mm_nt(gd, down_ref[0]) * slope_s[slot]).astype(BF)
         bup_ref[0, 0:1, :] = col_sum(gu.astype(F32))
         bup_ref[0, 1:8, :] = jnp.zeros((7, D), F32)
         grad_ref[0, 0:D, :] = mm_tn(fl_s[...], gu).astype(BF)
@@ -834,10 +831,12 @@
 
 def gather_blocks(r0, z, x, rows):
     r1, x0, y0 = ring_z(r0), swap_x(r0), swap_y(r0)
-    r2, x1, d0 = ring_z(r1), swap_x(after(r1, x0)), swap_y(after(x0, y0))
-    r3, x2, y1 = ring_z(r2), swap_x(after(r2, x1)), swap_y(after(r1, d0))
-    d1, x3, y2 = ring_z(after(d0, r3)), swap_x(after(r3, x2)), swap_y(after(r2, y1))
-    y3, d2, d3 = ring_z(after(y2, d1)), swap_x(after(y2, x3)), swap_y(after(x3, y2))
+    d0 = swap_y(after(x0, y0))
+    r2, x1, y1 = ring_z(r1), swap_x(after(r1, x0)), swap_y(after(r1, y0))
+    r3, x2, y2 = ring_z(r2), swap_x(after(r2, x0)), swap_y(after(r2, d0))
+    d1 = ring_z(after(d0, y1))
+    x3 = swap_x(after(r3, x1))
+    y3, d2, d3 = ring_z(after(y2, r3)), swap_x(after(y2, x2)), swap_y(after(x3, y1))
     pieces = [r0, r1, r2, r3, x0, x1, x2, x3, y0, y1, y2, y3, d0, d1, d2, d3]
     return merge_blocks(window_places(z, x), pieces, rows)
 
@@ -851,23 +850,24 @@
 
 def reduce_windows(own, got, z, x, rows):
     at = window_places(z, x)
-    a = split_windows(at, ("Y3", "D2", "D3", "Y2", "X3", "D1"), own, got, rows)
+    a = split_windows(at, ("D3", "Y3", "D2", "D1"), own, got, rows)
+    y1, z1, x1 = swap_y(a["D3"]), ring_back(a["Y3"]), swap_x(a["D2"])
     a |= split_windows(
-        at, ("X2", "Y1", "R3", "R2", "D0", "X1", "R1", "X0", "Y0", "R0"), own, got, rows
-    )
-    z1, x1, y1 = ring_back(a["Y3"]), swap_x(a["D2"]), swap_y(a["D3"])
-    z2 = ring_back(after(a["D1"], z1))
-    x2 = swap_x(add_low(a["X3"], y1))
+        at, ("X3", "Y2", "Y1", "R3", "X2", "R2", "X1", "R1", "D0", "X0", "Y0", "R0"), own, got, rows
+    )
+    z2 = ring_back(after(a["D1"], x1))
+    y3 = swap_y(after(a["Y1"], x1))
+    far = add_low(a["X3"], y1)
+    x2 = swap_x(far)
     y2 = swap_y(add_low(a["Y2"], z1, x1))
+    x3 = swap_x(after(a["X2"], x2))
     z3 = ring_back(add_low(a["R3"], x2))
-    x3 = swap_x(after(a["X2"], x2))
-    y3 = swap_y(after(a["Y1"], y2))
+    x4 = swap_x(after(a["X1"], x3))
+    y4 = swap_y(add_low(a["D0"], z2))
     z4 = ring_back(add_low(a["R2"], y2, z3, x3))
-    x4 = swap_x(after(a["X1"], x3))
-    y4 = swap_y(after(add_low(a["D0"], z2), y3))
+    y5 = swap_y(after(a["Y0"], y2))
     z5 = ring_back(add_low(a["R1"], y3, z4, x4))
     x5 = swap_x(add_low(a["X0"], y4))
-    y5 = swap_y(after(a["Y0"], y4))
     return a["R0"], z5, x5, y5
 
 

time: 251 us -> 234 us (0.932)
  waiting for transfers between devices: 99.8 us -> 88.6 us
    ppermute x5, waiting for transfers between devices: 34.6 us -> 1.1 us  [ring_back(): return lax.ppermute(a, 'wide', [(j, i) for i, j in Z_RING])]
    ppermute x5, waiting for transfers between devices: 11.3 us -> 32.2 us  [ring_z(): return lax.ppermute(a, 'wide', Z_RING)]
    ppermute x5, starting transfers between devices: 12.9 us -> 6.95 us  [ring_back(): return lax.ppermute(a, 'wide', [(j, i) for i, j in Z_RING])]
  transfers between devices with their start and end apart: 34 -> 34, of which waited for: 23 -> 18; matrix products, arithmetic and copies ran while one was open for 3% -> 3% of each run, Pallas kernels for 22% -> 24%
where the time goes in v4:
time: 234 us
  Pallas kernels  101 us (43%)
  waiting for transfers between devices  88.6 us (38%)
  starting transfers between devices  34.5 us (15%)
  other arithmetic  5.3 us (2%)
  local copies, waits for them, and re-layouts  3.44 us (1%)
    pallas_call x8, Pallas kernels, call(): pl.pallas_call(kernel, grid_spec=pltpu.PrefetchScalarGridSpec(num_scalar_...  101 us
    ppermute x5, waiting for transfers between devices, ring_z(): return lax.ppermute(a, 'wide', Z_RING)  32.2 us
    ppermute x10, waiting for transfers between devices, swap_x(): return lax.ppermute(a, 'wide', X_SWAP)  23.9 us
    ppermute x10, waiting for transfers between devices, swap_y(): return lax.ppermute(a, 'narrow', Y_SWAP)  21.9 us
    ppermute x10, starting transfers between devices, swap_y(): return lax.ppermute(a, 'narrow', Y_SWAP)  11.9 us
    ppermute x10, starting transfers between devices, swap_x(): return lax.ppermute(a, 'wide', X_SWAP)  11.6 us
    ppermute x4, waiting for transfers between devices, swap_core(): return lax.ppermute(a, 'narrow', CORE_SWAP)  9.52 us
    ppermute x5, starting transfers between devices, ring_back(): return lax.ppermute(a, 'wide', [(j, i) for i, j in Z_RING])  6.95 us
  transfers between devices with their start and end apart: 34, of which 18 were waited for; matrix products, arithmetic and copies ran while one was open for 3% of the time, Pallas kernels for 24%

profile of v4, /device:TPU:0, one launch (start us, length us, event | category | flops | bytes accessed | tf_op | source)
XLA Modules:
  0.0 233.9 jit_solution(13438111943649653216)
XLA Ops:
  2.6 3.1 %collective-permute-start = (bf16[296,768]{1,0:T(8,128)(2,1)S(1)}, bf16[296,768]{1,0:T(8,128)(2,1)S(1)}, u32[]{:S(2)}, u32[]{:S(2)}) collective-permute-start(bf16[296,768]{1,0:T(8,128)(2,1)S(1)} %own_block.1.refs_0_), channel_id=1, source_target_pairs={{0,8},{4,12},{8,16},{12,20},{16,24},{20,28},{24,0},{28,4},{1,9},{5... | collective-permute-start | bytes 1363976 | tf_op jit(solution)/shard_map/ppermute | solution.py:797
  8.7 9.4 %collective-permute-done.refs_1_ = bf16[296,768]{1,0:T(8,128)(2,1)S(1)} collective-permute-done((bf16[296,768]{1,0:T(8,128)(2,1)S(1)}, bf16[296,768]{1,0:T(8,128)(2,1)S(1)}, u32[]{:S(2)}, u32[]{:S(2)}) %collective-permute-start) | collective-permute-done | bytes 454688 | tf_op jit(solution)/shard_map/ppermute | solution.py:797
  21.3 10.3 %collective-permute-done.1.refs_2_ = bf16[296,768]{1,0:T(8,128)(2,1)S(1)} collective-permute-done((bf16[296,768]{1,0:T(8,128)(2,1)S(1)}, bf16[296,768]{1,0:T(8,128)(2,1)S(1)}, u32[]{:S(2)}, u32[]{:S(2)}) %collective-permute-start.1) | collective-permute-done | bytes 454688 | tf_op jit(solution)/shard_map/ppermute | solution.py:797
  34.9 9.2 %collective-permute-done.2.refs_3_ = bf16[296,768]{1,0:T(8,128)(2,1)S(1)} collective-permute-done((bf16[296,768]{1,0:T(8,128)(2,1)S(1)}, bf16[296,768]{1,0:T(8,128)(2,1)S(1)}, u32[]{:S(2)}, u32[]{:S(2)}) %collective-permute-start.2) | collective-permute-done | bytes 454688 | tf_op jit(solution)/shard_map/ppermute | solution.py:797
  45.2 7.0 %collective-permute-done.10.refs_10_ = bf16[296,768]{1,0:T(8,128)(2,1)} collective-permute-done((bf16[296,768]{1,0:T(8,128)(2,1)S(1)}, bf16[296,768]{1,0:T(8,128)(2,1)}, u32[]{:S(2)}, u32[]{:S(2)}) %collective-permute-start.10) | collective-permute-done | bytes 454688 | tf_op jit(solution)/shard_map/ppermute | solution.py:793
  53.2 2.4 %collective-permute-done.6.refs_7_ = bf16[296,768]{1,0:T(8,128)(2,1)} collective-permute-done((bf16[296,768]{1,0:T(8,128)(2,1)S(1)}, bf16[296,768]{1,0:T(8,128)(2,1)}, u32[]{:S(2)}, u32[]{:S(2)}) %collective-permute-start.6) | collective-permute-done | bytes 454688 | tf_op jit(solution)/shard_map/ppermute | solution.py:789
  57.9 5.9 %collective-permute-done.13.refs_14_ = bf16[296,768]{1,0:T(8,128)(2,1)} collective-permute-done((bf16[296,768]{1,0:T(8,128)(2,1)}, bf16[296,768]{1,0:T(8,128)(2,1)}, u32[]{:S(2)}, u32[]{:S(2)}) %collective-permute-start.13) | collective-permute-done | bytes 454688 | tf_op jit(solution)/shard_map/ppermute | solution.py:789
  63.8 2.3 %collective-permute-done.11.refs_11_ = bf16[296,768]{1,0:T(8,128)(2,1)} collective-permute-done((bf16[296,768]{1,0:T(8,128)(2,1)}, bf16[296,768]{1,0:T(8,128)(2,1)}, u32[]{:S(2)}, u32[]{:S(2)}) %collective-permute-start.11) | collective-permute-done | bytes 454688 | tf_op jit(solution)/shard_map/ppermute | solution.py:797
  66.2 6.3 %merge_weights.1 = (bf16[2,776,768]{2,1,0:T(8,128)(2,1)}, bf16[2,1536,768]{2,1,0:T(8,128)(2,1)}) custom-call(s32[8]{0:T(128)} %pad_add_fusion.2.at_ref, bf16[296,768]{1,0:T(8,128)(2,1)} %copy-done.2, bf16[296,768]{1,0:T(8,128)(2,1)} %copy-done.9, bf16[296,768]{1,0:T(8,128)(2,1)} %copy-done.12, bf16[296,768]{1,0:T(8,128)(2,1)} %copy-done.15, ...), custom_call_target="tpu_custom_call" | custom-call | tf_op jit(solution)/shard_map/merge_weights/pallas_call | solution.py:106
  72.6 4.8 %collective-permute-done.15.mq1_ref.wo1_ref = bf16[2,776,768]{2,1,0:T(8,128)(2,1)S(1)} collective-permute-done((bf16[2,776,768]{2,1,0:T(8,128)(2,1)}, bf16[2,776,768]{2,1,0:T(8,128)(2,1)S(1)}, u32[]{:S(2)}, u32[]{:S(2)}) %collective-permute-start.15) | collective-permute-done | bytes 2383904 | tf_op jit(solution)/shard_map/ppermute | solution.py:805
  79.6 20.0 %attention_forward.1 = (bf16[4,512,576]{2,1,0:T(8,128)(2,1)}, bf16[4,768,576]{2,1,0:T(8,128)(2,1)}, bf16[4,512,192]{2,1,0:T(8,128)(2,1)}, bf16[4,3,512,512]{3,2,...) custom-call(s32[7]{0:T(128)} %pad_add_fusion.1.scal_ref, ...), custom_call_target="tpu_custom_call" | custom-call | flops 6000000000 | bytes 24000000 | tf_op jit(solution)/shard_map/attention_forward/pallas_call | solution.py:106
  99.6 29.5 %feed_forward.1 = (bf16[512,768]{1,0:T(8,128)(2,1)}, bf16[2,1536,768]{2,1,0:T(8,128)(2,1)}, bf16[2,1536,768]{2,1,0:T(8,128)(2,1)}, f32[512,768]{1,0:T(8,128)}, b...) custom-call(s32[3]{0:T(128)} %copy-done.6, f32[512,768]{1,0:T(8,128)} %get-tuple-element.74.n1_ref, ...), custom_call_target="tpu_custom_call" | custom-call | flops 14499999744 | bytes 36000000 | tf_op jit(solution)/shard_map/feed_forward/pallas_call | solution.py:106
  129.8 29.6 %attention_backward.1 = (bf16[2,776,768]{2,1,0:T(8,128)(2,1)}, bf16[2,776,768]{2,1,0:T(8,128)(2,1)}, f32[512,768]{1,0:T(8,128)}) custom-call(s32[3]{0:T(128)} %copy-done.6, bf16[512,768]{1,0:T(8,128)(2,1)} %get-tuple-element.79.ga_ref, bf16[2,776,768]{2,1,0:T(8,128)(2,1)} %get-tuple-element.73.mq0_ref.wo0_ref, bf16[2,776,768]{2,1,0:T(8,128)(2,1)} %copy-done.24, ...), custom_call_target="tpu_custom_call" | custom-call | flops 12000000000 | bytes 30000000 | tf_op jit(solution)/shard_map/attention_backward/pallas_call | solution.py:106
  159.4 4.8 %collective-permute-done.17.got_att = bf16[2,776,768]{2,1,0:T(8,128)(2,1)S(1)} collective-permute-done((bf16[2,776,768]{2,1,0:T(8,128)(2,1)}, bf16[2,776,768]{2,1,0:T(8,128)(2,1)S(1)}, u32[]{:S(2)}, u32[]{:S(2)}) %collective-permute-start.17) | collective-permute-done | bytes 2383904 | tf_op jit(solution)/shard_map/ppermute | solution.py:805
  165.6 4.0 %split_windows.3 = (bf16[296,768]{1,0:T(8,128)(2,1)}, bf16[296,768]{1,0:T(8,128)(2,1)}, bf16[296,768]{1,0:T(8,128)(2,1)}, bf16[296,768]{1,0:T(8,128)(2,1)}) custom-call(s32[8]{0:T(128)} %pad_add_fusion.2.at_ref, bf16[2,776,768]{2,1,0:T(8,128)(2,1)} %get-tuple-element.89.own_att, bf16[2,1536,768]{2,1,0:T(8,128)(2,1)} %get-tuple-element.90.own_ff, ...), custom_call_target="tpu_custom_call" | custom-call | tf_op jit(solution)/shard_map/split_windows/pallas_call | solution.py:106
  173.2 7.4 %split_windows.2 = (bf16[296,768]{1,0:T(8,128)(2,1)}, bf16[296,768]{1,0:T(8,128)(2,1)}, bf16[296,768]{1,0:T(8,128)(2,1)}, bf16[296,768]{1,0:T(8,128)(2,1)}, bf16...) custom-call(s32[8]{0:T(128)} %pad_add_fusion.2.at_ref, ...), custom_call_target="tpu_custom_call" | custom-call | tf_op jit(solution)/shard_map/split_windows/pallas_call | solution.py:106
  180.7 1.6 collective-permute-done.23
  188.5 6.7 %collective-permute-done.24 = bf16[296,768]{1,0:T(8,128)(2,1)S(1)} collective-permute-done((bf16[296,768]{1,0:T(8,128)(2,1)S(1)}, bf16[296,768]{1,0:T(8,128)(2,1)S(1)}, u32[]{:S(2)}, u32[]{:S(2)}) %collective-permute-start.24) | collective-permute-done | bytes 454688 | tf_op jit(solution)/shard_map/ppermute | solution.py:789
  199.7 6.3 %collective-permute-done.26 = bf16[296,768]{1,0:T(8,128)(2,1)S(1)} collective-permute-done((bf16[296,768]{1,0:T(8,128)(2,1)S(1)}, bf16[296,768]{1,0:T(8,128)(2,1)S(1)}, u32[]{:S(2)}, u32[]{:S(2)}) %collective-permute-start.26) | collective-permute-done | bytes 454688 | tf_op jit(solution)/shard_map/ppermute | solution.py:789
  207.5 2.6 %collective-permute-start.27 = (bf16[296,768]{1,0:T(8,128)(2,1)S(1)}, bf16[296,768]{1,0:T(8,128)(2,1)S(1)}, u32[]{:S(2)}, u32[]{:S(2)}) collective-permute-start(bf16[296,768]{1,0:T(8,128)(2,1)S(1)} %add_convert_fusion.3), channel_id=1, source_target_pairs={{8,0},{12,4},{16,8},{20,12},{24,16},{28,20},{0,24},{4,28},{9,1},{1... | collective-permute-start | bytes 1363976 | tf_op jit(solution)/shard_map/ppermute | solution.py:801
  211.6 8.9 %collective-permute-done.31 = bf16[296,768]{1,0:T(8,128)(2,1)S(1)} collective-permute-done((bf16[296,768]{1,0:T(8,128)(2,1)S(1)}, bf16[296,768]{1,0:T(8,128)(2,1)S(1)}, u32[]{:S(2)}, u32[]{:S(2)}) %collective-permute-start.31) | collective-permute-done | bytes 454688 | tf_op jit(solution)/shard_map/ppermute | solution.py:793
  222.8 4.4 %collective-permute-done.33.ring_ref = bf16[296,768]{1,0:T(8,128)(2,1)S(1)} collective-permute-done((bf16[296,768]{1,0:T(8,128)(2,1)S(1)}, bf16[296,768]{1,0:T(8,128)(2,1)S(1)}, u32[]{:S(2)}, u32[]{:S(2)}) %collective-permute-start.33) | collective-permute-done | bytes 454688 | tf_op jit(solution)/shard_map/ppermute | solution.py:793
  227.3 1.9 collective-permute-done.32.second_ref
  230.3 3.6 %update_shard.1 = (f32[1,221568]{1,0:T(1,128)}, f32[1,221568]{1,0:T(1,128)}, f32[1,221568]{1,0:T(1,128)}, f32[1,221568]{1,0:T(1,128)}, bf16[1,221568]{1,0:T(2,128)(2,1)}) custom-call(s32[3]{0:T(128)S(1)} %copy-done.7, bf16[296,768]{1,0:T(8,128)(2,1)S(1)} %copy-done.5, bf16[296,768]{1,0:T(8,128)(2,1)S(1)} %collective-permute-done.29.near_ref, ...), custom_call_target="tpu_custom_call" | custom-call | tf_op jit(solution)/shard_map/update_shard/pallas_call | solution.py:106
  (126 shorter events, 40.9 us)
Async XLA Ops:
  2.6 15.6 %collective-permute-start = (bf16[296,768]{1,0:T(8,128)(2,1)S(1)}, bf16[296,768]{1,0:T(8,128)(2,1)S(1)}, u32[]{:S(2)}, u32[]{:S(2)}) collective-permute-start(bf16[296,768]{1,0:T(8,128)(2,1)S(1)} %own_block.1.refs_0_), channel_id=1, source_target_pairs={{0,8},{4,12},{8,16},{12,20},{16,24},{20,28},{24,0},{28,4},{1,9},{5... | collective-permute-start | bytes 1363976 | tf_op jit(solution)/shard_map/ppermute | solution.py:797
  5.7 12.5 %collective-permute-start.7 = (bf16[296,768]{1,0:T(8,128)(2,1)S(1)}, bf16[296,768]{1,0:T(8,128)(2,1)S(1)}, u32[]{:S(2)}, u32[]{:S(2)}) collective-permute-start(bf16[296,768]{1,0:T(8,128)(2,1)S(1)} %own_block.1.refs_0_), channel_id=1, source_target_pairs={{0,2},{1,3},{2,0},{3,1},{4,6},{5,7},{6,4},{7,5},{8,10},{9,11},{10,... | collective-permute-start | bytes 1363976 | tf_op jit(solution)/shard_map/ppermute | solution.py:793
  18.2 13.4 %collective-permute-start.1 = (bf16[296,768]{1,0:T(8,128)(2,1)S(1)}, bf16[296,768]{1,0:T(8,128)(2,1)S(1)}, u32[]{:S(2)}, u32[]{:S(2)}) collective-permute-start(bf16[296,768]{1,0:T(8,128)(2,1)S(1)} %collective-permute-done.refs_1_), channel_id=1, source_target_pairs={{0,8},{4,12},{8,16},{12,20},{16,24},{20,28},{24,0},{28,4},{1,9},{5... | collective-permute-start | bytes 1363976 | tf_op jit(solution)/shard_map/ppermute | solution.py:797
  18.8 14.0 %collective-permute-start.9 = (bf16[296,768]{1,0:T(8,128)(2,1)S(1)}, bf16[296,768]{1,0:T(8,128)(2,1)S(1)}, u32[]{:S(2)}, u32[]{:S(2)}) collective-permute-start(bf16[296,768]{1,0:T(8,128)(2,1)S(1)} %collective-permute-done.3.refs_4_), channel_id=1, source_target_pairs={{0,2},{1,3},{2,0},{3,1},{4,6},{5,7},{6,4},{7,5},{8,10},{9,11},{10,... | collective-permute-start | bytes 1363976 | tf_op jit(solution)/shard_map/ppermute | solution.py:793
  19.8 15.1 %collective-permute-start.4 = (bf16[296,768]{1,0:T(8,128)(2,1)S(1)}, bf16[296,768]{1,0:T(8,128)(2,1)S(1)}, u32[]{:S(2)}, u32[]{:S(2)}) collective-permute-start(bf16[296,768]{1,0:T(8,128)(2,1)S(1)} %collective-permute-done.refs_1_), channel_id=1, source_target_pairs={{0,4},{4,0},{8,12},{12,8},{16,20},{20,16},{24,28},{28,24},{1,5},{5... | collective-permute-start | bytes 1363976 | tf_op jit(solution)/shard_map/ppermute | solution.py:789
  31.6 12.5 %collective-permute-start.2 = (bf16[296,768]{1,0:T(8,128)(2,1)S(1)}, bf16[296,768]{1,0:T(8,128)(2,1)S(1)}, u32[]{:S(2)}, u32[]{:S(2)}) collective-permute-start(bf16[296,768]{1,0:T(8,128)(2,1)S(1)} %collective-permute-done.1.refs_2_), channel_id=1, source_target_pairs={{0,8},{4,12},{8,16},{12,20},{16,24},{20,28},{24,0},{28,4},{1,9},{5... | collective-permute-start | bytes 1363976 | tf_op jit(solution)/shard_map/ppermute | solution.py:797
  31.6 13.6 %collective-permute-start.8 = (bf16[296,768]{1,0:T(8,128)(2,1)S(1)}, bf16[296,768]{1,0:T(8,128)(2,1)S(1)}, u32[]{:S(2)}, u32[]{:S(2)}) collective-permute-start(bf16[296,768]{1,0:T(8,128)(2,1)S(1)} %collective-permute-done.refs_1_), channel_id=1, source_target_pairs={{0,2},{1,3},{2,0},{3,1},{4,6},{5,7},{6,4},{7,5},{8,10},{9,11},{10,... | collective-permute-start | bytes 1363976 | tf_op jit(solution)/shard_map/ppermute | solution.py:793
  32.9 12.3 %collective-permute-start.5 = (bf16[296,768]{1,0:T(8,128)(2,1)S(1)}, bf16[296,768]{1,0:T(8,128)(2,1)S(1)}, u32[]{:S(2)}, u32[]{:S(2)}) collective-permute-start(bf16[296,768]{1,0:T(8,128)(2,1)S(1)} %collective-permute-done.1.refs_2_), channel_id=1, source_target_pairs={{0,4},{4,0},{8,12},{12,8},{16,20},{20,16},{24,28},{28,24},{1,5},{5... | collective-permute-start | bytes 1363976 | tf_op jit(solution)/shard_map/ppermute | solution.py:789
  34.4 17.8 %collective-permute-start.10 = (bf16[296,768]{1,0:T(8,128)(2,1)S(1)}, bf16[296,768]{1,0:T(8,128)(2,1)}, u32[]{:S(2)}, u32[]{:S(2)}) collective-permute-start(bf16[296,768]{1,0:T(8,128)(2,1)S(1)} %collective-permute-done.1.refs_2_), channel_id=1, source_target_pairs={{0,2},{1,3},{2,0},{3,1},{4,6},{5,7},{6,4},{7,5},{8,10},{9,11},{10,... | collective-permute-start | bytes 1363976 | tf_op jit(solution)/shard_map/ppermute | solution.py:793
  45.2 12.8 %collective-permute-start.12 = (bf16[296,768]{1,0:T(8,128)(2,1)S(1)}, bf16[296,768]{1,0:T(8,128)(2,1)}, u32[]{:S(2)}, u32[]{:S(2)}) collective-permute-start(bf16[296,768]{1,0:T(8,128)(2,1)S(1)} %collective-permute-done.9.refs_12_), channel_id=1, source_target_pairs={{0,8},{4,12},{8,16},{12,20},{16,24},{20,28},{24,0},{28,4},{1,9},{5... | collective-permute-start | bytes 1363976 | tf_op jit(solution)/shard_map/ppermute | solution.py:797
  53.2 13.0 %collective-permute-start.11 = (bf16[296,768]{1,0:T(8,128)(2,1)}, bf16[296,768]{1,0:T(8,128)(2,1)}, u32[]{:S(2)}, u32[]{:S(2)}) collective-permute-start(bf16[296,768]{1,0:T(8,128)(2,1)} %collective-permute-done.10.refs_10_), channel_id=1, source_target_pairs={{0,8},{4,12},{8,16},{12,20},{16,24},{20,28},{24,0},{28,4},{1,9},{5... | collective-permute-start | bytes 1363976 | tf_op jit(solution)/shard_map/ppermute | solution.py:797
  77.4 22.2 %collective-permute-start.16 = (bf16[2,1536,768]{2,1,0:T(8,128)(2,1)}, bf16[2,1536,768]{2,1,0:T(8,128)(2,1)}, u32[]{:S(2)}, u32[]{:S(2)}) collective-permute-start(bf16[2,1536,768]{2,1,0:T(8,128)(2,1)} %get-tuple-element.77.up0_ref.down0_ref), channel_id=1, source_target_pairs={{0,1},{1,0},{2,3},{3,2},{4,5},{5,4},{6,7},{7,6},{8,9},{9,8},{10,11... | collective-permute-start | bytes 14155784 | tf_op jit(solution)/shard_map/ppermute | solution.py:805
  129.2 35.0 %collective-permute-start.18 = (bf16[2,1536,768]{2,1,0:T(8,128)(2,1)}, bf16[2,1536,768]{2,1,0:T(8,128)(2,1)}, u32[]{:S(2)}, u32[]{:S(2)}) collective-permute-start(bf16[2,1536,768]{2,1,0:T(8,128)(2,1)} %get-tuple-element.92), channel_id=1, source_target_pairs={{0,1},{1,0},{2,3},{3,2},{4,5},{5,4},{6,7},{7,6},{8,9},{9,8},{10,11... | collective-permute-start | bytes 14155784 | tf_op jit(solution)/shard_map/ppermute | solution.py:805
  169.6 12.7 %collective-permute-start.23 = (bf16[296,768]{1,0:T(8,128)(2,1)}, bf16[296,768]{1,0:T(8,128)(2,1)S(1)}, u32[]{:S(2)}, u32[]{:S(2)}) collective-permute-start(bf16[296,768]{1,0:T(8,128)(2,1)} %get-tuple-element.103), channel_id=1, source_target_pairs={{0,2},{1,3},{2,0},{3,1},{4,6},{5,7},{6,4},{7,5},{8,10},{9,11},{10,... | collective-permute-start | bytes 1363976 | tf_op jit(solution)/shard_map/ppermute | solution.py:793
  171.2 13.7 %collective-permute-start.19 = (bf16[296,768]{1,0:T(8,128)(2,1)}, bf16[296,768]{1,0:T(8,128)(2,1)S(1)}, u32[]{:S(2)}, u32[]{:S(2)}) collective-permute-start(bf16[296,768]{1,0:T(8,128)(2,1)} %get-tuple-element.96), channel_id=1, source_target_pairs={{0,4},{4,0},{8,12},{12,8},{16,20},{20,16},{24,28},{28,24},{1,5},{5... | collective-permute-start | bytes 1363976 | tf_op jit(solution)/shard_map/ppermute | solution.py:789
  171.7 14.0 %collective-permute-start.21 = (bf16[296,768]{1,0:T(8,128)(2,1)}, bf16[296,768]{1,0:T(8,128)(2,1)S(1)}, u32[]{:S(2)}, u32[]{:S(2)}) collective-permute-start(bf16[296,768]{1,0:T(8,128)(2,1)} %get-tuple-element.100), channel_id=1, source_target_pairs={{8,0},{12,4},{16,8},{20,12},{24,16},{28,20},{0,24},{4,28},{9,1},{1... | collective-permute-start | bytes 1363976 | tf_op jit(solution)/shard_map/ppermute | solution.py:801
  183.5 11.7 %collective-permute-start.24 = (bf16[296,768]{1,0:T(8,128)(2,1)S(1)}, bf16[296,768]{1,0:T(8,128)(2,1)S(1)}, u32[]{:S(2)}, u32[]{:S(2)}) collective-permute-start(bf16[296,768]{1,0:T(8,128)(2,1)S(1)} %add_convert_fusion.5), channel_id=1, source_target_pairs={{0,4},{4,0},{8,12},{12,8},{16,20},{20,16},{24,28},{28,24},{1,5},{5... | collective-permute-start | bytes 1363976 | tf_op jit(solution)/shard_map/ppermute | solution.py:789
  184.8 14.2 %collective-permute-start.30 = (bf16[296,768]{1,0:T(8,128)(2,1)S(1)}, bf16[296,768]{1,0:T(8,128)(2,1)S(1)}, u32[]{:S(2)}, u32[]{:S(2)}) collective-permute-start(bf16[296,768]{1,0:T(8,128)(2,1)S(1)} %copy-done.28), channel_id=1, source_target_pairs={{8,0},{12,4},{16,8},{20,12},{24,16},{28,20},{0,24},{4,28},{9,1},{1... | collective-permute-start | bytes 1363976 | tf_op jit(solution)/shard_map/ppermute | solution.py:801
  186.9 20.3 %collective-permute-start.22 = (bf16[296,768]{1,0:T(8,128)(2,1)S(1)}, bf16[296,768]{1,0:T(8,128)(2,1)S(1)}, u32[]{:S(2)}, u32[]{:S(2)}) collective-permute-start(bf16[296,768]{1,0:T(8,128)(2,1)S(1)} %add_convert_fusion.6), channel_id=1, source_target_pairs={{0,2},{1,3},{2,0},{3,1},{4,6},{5,7},{6,4},{7,5},{8,10},{9,11},{10,... | collective-permute-start | bytes 1363976 | tf_op jit(solution)/shard_map/ppermute | solution.py:793
  197.5 24.0 %collective-permute-start.20 = (bf16[296,768]{1,0:T(8,128)(2,1)S(1)}, bf16[296,768]{1,0:T(8,128)(2,1)S(1)}, u32[]{:S(2)}, u32[]{:S(2)}) collective-permute-start(bf16[296,768]{1,0:T(8,128)(2,1)S(1)} %copy-done.27), channel_id=1, source_target_pairs={{0,2},{1,3},{2,0},{3,1},{4,6},{5,7},{6,4},{7,5},{8,10},{9,11},{10,... | collective-permute-start | bytes 1363976 | tf_op jit(solution)/shard_map/ppermute | solution.py:793
  199.1 21.4 %collective-permute-start.31 = (bf16[296,768]{1,0:T(8,128)(2,1)S(1)}, bf16[296,768]{1,0:T(8,128)(2,1)S(1)}, u32[]{:S(2)}, u32[]{:S(2)}) collective-permute-start(bf16[296,768]{1,0:T(8,128)(2,1)S(1)} %add_convert_fusion.1), channel_id=1, source_target_pairs={{0,2},{1,3},{2,0},{3,1},{4,6},{5,7},{6,4},{7,5},{8,10},{9,11},{10,... | collective-permute-start | bytes 1363976 | tf_op jit(solution)/shard_map/ppermute | solution.py:793
  206.0 15.5 %collective-permute-start.28 = (bf16[296,768]{1,0:T(8,128)(2,1)S(1)}, bf16[296,768]{1,0:T(8,128)(2,1)S(1)}, u32[]{:S(2)}, u32[]{:S(2)}) collective-permute-start(bf16[296,768]{1,0:T(8,128)(2,1)S(1)} %copy-done.26), channel_id=1, source_target_pairs={{0,4},{4,0},{8,12},{12,8},{16,20},{20,16},{24,28},{28,24},{1,5},{5... | collective-permute-start | bytes 1363976 | tf_op jit(solution)/shard_map/ppermute | solution.py:789
  207.5 14.0 %collective-permute-start.27 = (bf16[296,768]{1,0:T(8,128)(2,1)S(1)}, bf16[296,768]{1,0:T(8,128)(2,1)S(1)}, u32[]{:S(2)}, u32[]{:S(2)}) collective-permute-start(bf16[296,768]{1,0:T(8,128)(2,1)S(1)} %add_convert_fusion.3), channel_id=1, source_target_pairs={{8,0},{12,4},{16,8},{20,12},{24,16},{28,20},{0,24},{4,28},{9,1},{1... | collective-permute-start | bytes 1363976 | tf_op jit(solution)/shard_map/ppermute | solution.py:801
  210.1 17.1 %collective-permute-start.33 = (bf16[296,768]{1,0:T(8,128)(2,1)S(1)}, bf16[296,768]{1,0:T(8,128)(2,1)S(1)}, u32[]{:S(2)}, u32[]{:S(2)}) collective-permute-start(bf16[296,768]{1,0:T(8,128)(2,1)S(1)} %copy-done.25), channel_id=1, source_target_pairs={{0,2},{1,3},{2,0},{3,1},{4,6},{5,7},{6,4},{7,5},{8,10},{9,11},{10,... | collective-permute-start | bytes 1363976 | tf_op jit(solution)/shard_map/ppermute | solution.py:793
  (40 other events, 847.5 us)

commit v5 on v4

--- a/solution.py
+++ b/solution.py
@@ -102,7 +102,7 @@
     return jnp.sum(values, axis=0, keepdims=True)
 
 
-def call(kernel, name, grid, in_specs, out_specs, out_shape, scratch, args, vmem=VMEM_LIMIT, flops=0, moved=0):
+def call(kernel, name, grid, in_specs, out_specs, out_shape, scratch, args, vmem=VMEM_LIMIT, flops=0, moved=0, aliases=None):
     return pl.pallas_call(
         kernel,
         grid_spec=pltpu.PrefetchScalarGridSpec(
@@ -113,6 +113,7 @@
             scratch_shapes=scratch,
         ),
         out_shape=out_shape,
+        input_output_aliases=aliases or {},
         compiler_params=pltpu.CompilerParams(vmem_limit_bytes=vmem),
         cost_estimate=pl.CostEstimate(flops=flops, bytes_accessed=moved, transcendentals=0),
         name=name,
@@ -127,8 +128,16 @@
     return jax.ShapeDtypeStruct(shape, dtype)
 
 
+class PlaceView:
+    def __init__(self, ref):
+        self.ref = ref
+
+    def __getitem__(self, i):
+        return self.ref[4 + i]
+
+
 def block_kernel(rows, lead, shift, place_ref, flat_ref, out_ref, rows_s):
-    w = place_ref[0]
+    w = place_ref[4]
     count = flat_ref.shape[1] // 128
     rows_s[0:lead, :] = jnp.zeros((lead, 128), F32)
     rows_s[lead : lead + count, :] = flat_ref[...].reshape(count, 128)
@@ -177,7 +186,7 @@
     rows, lead, shift, rate, place_ref, kept_ref, near_ref, second_ref, ring_ref, params_ref, momentum_ref, average_ref,
     grads_ref, new_params_ref, new_momentum_ref, new_average_ref, low_ref, rows_s,
 ):
-    w = place_ref[0]
+    w = place_ref[4]
     count = params_ref.shape[1] // 128
     block = (
         kept_ref[...].astype(F32) + near_ref[...].astype(F32) + second_ref[...].astype(F32) + ring_ref[...].astype(F32)
@@ -232,78 +241,73 @@
     )
 
 
-def merge_kernel(rows, at_ref, *refs):
-    pieces, (att_ref, ff_ref), (mats, edges, in_sem, out_sem) = refs[:16], refs[16:18], refs[18:]
-    copies = {}
-    for slot in range(SLOTS):
-        for i in range(8):
-            w = at_ref[i]
-            piece = pieces[8 * slot + i]
-            main = pltpu.make_async_copy(
-                piece.at[0:rows],
-                mats.at[slot, pl.ds(pl.multiple_of(rows * w, TILE_ROWS), rows)],
-                in_sem.at[slot, i, 0],
-            )
-            edge = pltpu.make_async_copy(
-                piece.at[rows : rows + TILE_ROWS], edges.at[slot, w], in_sem.at[slot, i, 1]
-            )
-            main.start()
-            edge.start()
-            copies[slot, i] = (main, edge)
-    outs = []
-    for slot in range(SLOTS):
-        for i in range(8):
-            for c in copies[slot, i]:
-                c.wait()
-        for w in range(1, 8):
-            at = rows * w
-            mats[slot, at : at + TILE_ROWS, :] = mats[slot, at : at + TILE_ROWS, :] + edges[slot, w - 1]
-        mats[slot, MAT_ROWS:PAD_ROWS, :] = edges[slot, 7]
+def merge_kernel(rows, slot, at_ref, *refs):
+    pieces, (att_ref, ff_ref, mat, edges, in_sem, out_sem) = refs[:8], refs[-6:]
+    copies = []
+    for i in range(8):
+        w = at_ref[i]
+        main = pltpu.make_async_copy(
+            pieces[i].at[0:rows], mat.at[pl.ds(pl.multiple_of(rows * w, TILE_ROWS), rows)], in_sem.at[i, 0]
+        )
+        edge = pltpu.make_async_copy(pieces[i].at[rows : rows + TILE_ROWS], edges.at[w], in_sem.at[i, 1])
+        main.start()
+        edge.start()
+        copies += [main, edge]
+    for copy in copies:
+        copy.wait()
+    for w in range(1, 8):
+        at = rows * w
+        mat[at : at + TILE_ROWS, :] = mat[at : at + TILE_ROWS, :] + edges[w - 1]
+    mat[MAT_ROWS:PAD_ROWS, :] = edges[7]
+    outs = [
+        pltpu.make_async_copy(src, dst, out_sem.at[n])
         for n, (src, dst) in enumerate(
             (
-                (mats.at[slot, 0:D], att_ref.at[slot, 0:D]),
-                (mats.at[slot, MAT_ROWS:PAD_ROWS], att_ref.at[slot, D:ATT_ROWS]),
-                (mats.at[slot, D:MAT_ROWS], ff_ref.at[slot]),
+                (mat.at[0:D], att_ref.at[0:D]),
+                (mat.at[MAT_ROWS:PAD_ROWS], att_ref.at[D:ATT_ROWS]),
+                (mat.at[D:MAT_ROWS], ff_ref.at[slot]),
             )
-        ):
-            copy = pltpu.make_async_copy(src, dst, out_sem.at[slot, n])
-            copy.start()
-            outs.append(copy)
+        )
+    ]
+    for copy in outs:
+        copy.start()
     for copy in outs:
         copy.wait()
 
 
-def merge_blocks(at, pieces, rows):
+def merge_blocks(at, pieces, rows, slot, ff=()):
     hbm = pl.BlockSpec(memory_space=pl.ANY)
     return call(
-        functools.partial(merge_kernel, rows),
+        functools.partial(merge_kernel, rows, slot),
         "merge_weights", (1,),
-        [hbm] * 16,
+        [hbm] * (8 + len(ff)),
         [hbm] * 2,
-        [shaped(BF, SLOTS, ATT_ROWS, D), shaped(BF, SLOTS, FF_ROWS, D)],
-        [
-            pltpu.VMEM((SLOTS, PAD_ROWS, D), BF),
-            pltpu.VMEM((SLOTS, 8, TILE_ROWS, D), BF),
-            pltpu.SemaphoreType.DMA((SLOTS, 8, 2)),
-            pltpu.SemaphoreType.DMA((SLOTS, 3)),
-        ],
-        (at, *pieces),
-    )
-
-
-def window_kernel(rows, windows, at_ref, own_att, own_ff, got_att, got_ff, *refs):
-    outs, (own_s, got_s, own_sem, got_sem) = refs[:-4], refs[-4:]
+        [shaped(BF, ATT_ROWS, D), shaped(BF, SLOTS, FF_ROWS, D)],
+        [
+            pltpu.VMEM((PAD_ROWS, D), BF),
+            pltpu.VMEM((8, TILE_ROWS, D), BF),
+            pltpu.SemaphoreType.DMA((8, 2)),
+            pltpu.SemaphoreType.DMA((3,)),
+        ],
+        (at, *pieces, *ff),
+        aliases={9: 1} if ff else {},
+    )
+
+
+def window_kernel(rows, windows, at_ref, *refs):
+    own_att, own_ff, got_att, got_ff = refs[0:2], refs[2], refs[3:5], refs[5]
+    outs, (own_s, got_s, own_sem, got_sem) = refs[6:-4], refs[-4:]
     cap = rows + TILE_ROWS
 
     def fetch(w, slot, att, ff, buf, sem):
         @pl.when(w < 2)
         def _():
-            src = att.at[slot, pl.ds(pl.multiple_of(rows * w, TILE_ROWS), cap)]
+            src = att.at[pl.ds(pl.multiple_of(rows * w, TILE_ROWS), cap)]
             pltpu.make_async_copy(src, buf, sem).start()
 
         @pl.when(w == 2)
         def _():
-            pltpu.make_async_copy(att.at[slot, 2 * rows : D], buf.at[0 : D - 2 * rows], sem).start()
+            pltpu.make_async_copy(att.at[2 * rows : D], buf.at[0 : D - 2 * rows], sem).start()
             pltpu.make_async_copy(ff.at[slot, 0 : 3 * rows + TILE_ROWS - D], buf.at[D - 2 * rows : cap], sem).start()
 
         @pl.when((w > 2) & (w < 7))
@@ -314,12 +318,12 @@
         @pl.when(w == 7)
         def _():
             pltpu.make_async_copy(ff.at[slot, 7 * rows - D : FF_ROWS], buf.at[0:rows], sem).start()
-            pltpu.make_async_copy(att.at[slot, D:ATT_ROWS], buf.at[rows:cap], sem).start()
+            pltpu.make_async_copy(att.at[D:ATT_ROWS], buf.at[rows:cap], sem).start()
 
     for n, (slot, where) in enumerate(windows):
         w = at_ref[where]
-        fetch(w, slot, own_att, own_ff, own_s.at[n], own_sem.at[n])
-        fetch(w, slot, got_att, got_ff, got_s.at[n], got_sem.at[n])
+        fetch(w, slot, own_att[slot], own_ff, own_s.at[n], own_sem.at[n])
+        fetch(w, slot, got_att[slot], got_ff, got_s.at[n], got_sem.at[n])
     for n in range(len(windows)):
         pltpu.make_async_copy(own_ff.at[0, 0:cap], own_s.at[n], own_sem.at[n]).wait()
         pltpu.make_async_copy(own_ff.at[0, 0:cap], got_s.at[n], got_sem.at[n]).wait()
@@ -334,7 +338,7 @@
     outs = call(
         functools.partial(window_kernel, rows, windows),
         "split_windows", (1,),
-        [hbm] * 4,
+        [hbm] * 6,
         [whole(cap, D)] * n,
         [shaped(BF, cap, D)] * n,
         [
@@ -360,15 +364,25 @@
 
 
 def att_fwd_kernel(
-    scal_ref, x_ref, mq0_ref, wo0_ref, mq1_ref, wo1_ref, tails_ref,
-    qkv_ref, wq_ref, mixed_ref, probs_ref, xp_ref, n1_ref, r1_ref,
-    table_s, acc_s, wo_s,
+    scal_ref, x_ref, att0_ref, att1_ref, att2_ref, att3_ref,
+    qkv_ref, wq_ref, mixed_ref, probs_ref, xp_ref, n1_ref, r1_ref, tails_ref,
+    table_s, acc_s, att_s, main_sem, tail_sem,
 ):
     s = pl.program_id(0)
     len_ref = scal_ref
+    atts = (att0_ref, att1_ref, att2_ref, att3_ref)
 
     @pl.when(s == 0)
     def _():
+        tails = [
+            pltpu.make_async_copy(att.at[D:ATT_ROWS], tails_ref.at[k], tail_sem.at[k]) for k, att in enumerate(atts)
+        ]
+        for copy in tails:
+            copy.start()
+        for k, att in enumerate(atts):
+            pltpu.make_async_copy(att.at[0:D], att_s.at[k], main_sem.at[k]).start()
+        for copy in tails:
+            copy.wait()
         xp_ref[...] = mm(x_ref[...], column_order()).astype(BF)
         acc_s[...] = jnp.zeros_like(acc_s)
         flat = jnp.concatenate(
@@ -392,20 +406,11 @@
                     axis=1,
                 )
 
-    def load(mq_ref, wo_ref):
-        for src_row, src_col, dst_row, dst_col in qkv_pieces():
-            wq_ref[0, dst_row : dst_row + 96, dst_col : dst_col + PART] = mq_ref[
-                0, src_row : src_row + 96, src_col : src_col + PART
-            ]
-        wo_s[...] = wo_ref[0]
-
-    @pl.when(s < SLOTS)
-    def _():
-        load(mq0_ref, wo0_ref)
-
-    @pl.when(s >= SLOTS)
-    def _():
-        load(mq1_ref, wo1_ref)
+    pltpu.make_async_copy(att0_ref.at[0:D], att_s.at[s], main_sem.at[s]).wait()
+    for src_row, src_col, dst_row, dst_col in qkv_pieces():
+        wq_ref[0, dst_row : dst_row + 96, dst_col : dst_col + PART] = att_s[
+            s, src_row : src_row + 96, src_col : src_col + PART
+        ]
 
     first = tails_ref[s, 0:1, :]
     bias = jnp.concatenate(
@@ -445,7 +450,7 @@
         heads.append(mm(probs_ref[0, h], v))
     mixed = jnp.concatenate(heads, axis=1).astype(BF)
     mixed_ref[0] = mixed
-    acc_s[...] += mm(mixed, wo_s[...])
+    acc_s[...] += mm(mixed, att_s[s, QKV_ROWS:D, :])
 
     @pl.when(s == RANKS - 1)
     def _():
@@ -455,28 +460,16 @@
         r1_ref[...] = jnp.broadcast_to(inv, (L, BLK))
 
 
-class PlaceView:
-    def __init__(self, ref):
-        self.ref = ref
-
-    def __getitem__(self, i):
-        return self.ref[4 + i]
-
-
-def attention_forward(scalars, x, own_att, got_att, tails):
+def attention_forward(scalars, x, atts):
     per = lambda *shape: pl.BlockSpec((1, *shape), lambda s, n: (s,) + (0,) * len(shape))
-    own = lambda rows, at: pl.BlockSpec((1, rows, D), lambda s, n: (jnp.minimum(s, 1), at, 0))
-    got = lambda rows, at: pl.BlockSpec((1, rows, D), lambda s, n: (jnp.maximum(s - 2, 0), at, 0))
     return call(
         att_fwd_kernel,
         "attention_forward", (RANKS,),
-        [
-            whole(L, D),
-            own(QKV_ROWS, 0), own(PART, QKV_ROWS // PART),
-            got(QKV_ROWS, 0), got(PART, QKV_ROWS // PART),
-            whole(RANKS, TILE_ROWS, D),
-        ],
-        [per(L, QKV_ROWS), per(D, QKV_ROWS), per(L, PART), per(HPR, L, L), whole(L, D), whole(L, D), whole(L, BLK)],
+        [whole(L, D)] + [pl.BlockSpec(memory_space=pl.ANY)] * RANKS,
+        [
+            per(L, QKV_ROWS), per(D, QKV_ROWS), per(L, PART), per(HPR, L, L),
+            whole(L, D), whole(L, D), whole(L, BLK), whole(RANKS, TILE_ROWS, D),
+        ],
         [
             shaped(BF, RANKS, L, QKV_ROWS),
             shaped(BF, RANKS, D, QKV_ROWS),
@@ -485,9 +478,16 @@
             shaped(BF, L, D),
             shaped(F32, L, D),
             shaped(F32, L, BLK),
-        ],
-        [pltpu.VMEM((RANKS, 8, 512), F32), pltpu.VMEM((L, D), F32), pltpu.VMEM((PART, D), BF)],
-        (scalars, x, own_att, own_att, got_att, got_att, tails),
+            shaped(BF, RANKS, TILE_ROWS, D),
+        ],
+        [
+            pltpu.VMEM((RANKS, 8, 512), F32),
+            pltpu.VMEM((L, D), F32),
+            pltpu.VMEM((RANKS, D, D), BF),
+            pltpu.SemaphoreType.DMA((RANKS,)),
+            pltpu.SemaphoreType.DMA((RANKS,)),
+        ],
+        (scalars, x, *atts),
         flops=6_000_000_000, moved=24_000_000,
     )
 
@@ -502,7 +502,7 @@
 
     @pl.when(step == 0)
     def _():
-        vec = vector_rows(tails_ref, place_ref)
+        vec = vector_rows(tails_ref, PlaceView(place_ref))
         first = n1_ref[...] * vec[2] + vec[3]
         fn_s[...] = first
         fl_s[...] = first.astype(BF)
@@ -527,7 +527,7 @@
 
     @pl.when(step == RANKS)
     def _():
-        vec = vector_rows(tails_ref, place_ref)
+        vec = vector_rows(tails_ref, PlaceView(place_ref))
         normed, inv = normalize(fn_s[...] + down_s[...] + vec[1])
         block_ref[...] = (normed * vec[4] + vec[5]).astype(BF)
         og = og_ref[...].astype(F32)
@@ -559,7 +559,7 @@
 
     @pl.when(step == 2 * RANKS - 1)
     def _():
-        vec = vector_rows(tails_ref, place_ref)
+        vec = vector_rows(tails_ref, PlaceView(place_ref))
         f = gf_s[...]
         normed = n1_ref[...]
         vec_ref[2:3, :] = col_sum(f * normed)
@@ -629,31 +629,37 @@
 
 
 def att_bwd_kernel(
-    place_ref, ga_ref, wo0_ref, wo1_ref, qkv_ref, probs_ref, mixed_ref, wq_ref, xp_ref, vec_ref, bup_ref, grad_one_ref,
-    da0_ref, da1_ref, in_grad_ref,
-    ds_s, near_s, sums_s, dx_s, order_s, wo_s, da_s,
+    place_ref, ga_ref, att0_ref, att1_ref, att2_ref, att3_ref,
+    qkv_ref, probs_ref, mixed_ref, wq_ref, xp_ref, vec_ref, bup_ref, grad_one_ref,
+    da0_ref, da1_ref, da2_ref, da3_ref, in_grad_ref,
+    ds_s, near_s, sums_s, dx_s, order_s, wo_s, das_s, sem, out_sem,
 ):
     s = pl.program_id(0)
-    slot = lax.rem(s + SLOTS, RANKS)
+    slot = RANKS - 1 - s
+    da_s = das_s.at[lax.rem(s, 2)]
+
+    def leave(k):
+        da_ref = (da0_ref, da1_ref, da2_ref, da3_ref)[k]
+        return pltpu.make_async_copy(das_s.at[(RANKS - 1 - k) % 2], da_ref, out_sem.at[k])
+
+    for k in range(2):
+
+        @pl.when(slot == k)
+        def _(k=k):
+            leave(k + 2).wait()
 
     @pl.when(s == 0)
     def _():
+        for k, att in enumerate((att0_ref, att1_ref, att2_ref, att3_ref)):
+            pltpu.make_async_copy(att.at[QKV_ROWS:D], wo_s.at[k], sem.at[k]).start()
         order_s[...] = table_order()
         dx_s[...] = jnp.zeros_like(dx_s)
         sums_s[...] = jnp.zeros_like(sums_s)
-        da_s[D:ATT_ROWS, :] = jnp.zeros((TILE_ROWS, D), BF)
-
-    @pl.when(slot < SLOTS)
-    def _():
-        wo_s[...] = wo0_ref[0]
-
-    @pl.when(slot >= SLOTS)
-    def _():
-        wo_s[...] = wo1_ref[0]
 
     ga = ga_ref[...]
     da_s[QKV_ROWS:D, :] = mm_tn(mixed_ref[0], ga).astype(BF)
-    dm_all = mm_nt(ga, wo_s[...]).astype(BF)
+    pltpu.make_async_copy(att0_ref.at[QKV_ROWS:D], wo_s.at[slot], sem.at[slot]).wait()
+    dm_all = mm_nt(ga, wo_s[slot]).astype(BF)
     qkv = qkv_ref[0]
     dq, dk, dv = [], [], []
     for h in range(HPR):
@@ -704,7 +710,7 @@
     table = jnp.concatenate([sums[h : h + 1, :BUCKETS] for h in range(HPR)], axis=1)
     table = jnp.broadcast_to(table, (8, D)).astype(BF)
     table = mm_nt(table, order_s[...])[0:1]
-    r = slice_of(slot, place_ref)
+    r = slice_of(slot, PlaceView(place_ref))
     vecs = []
     for i in range(3):
         m = 3 * r + i
@@ -730,51 +736,44 @@
         ]
     dx_s[...] += mm_nt(dqkv, wq_ref[0])
 
-    @pl.when(slot < SLOTS)
-    def _():
-        da0_ref[0] = da_s[...]
-
-    @pl.when(slot >= SLOTS)
-    def _():
-        da1_ref[0] = da_s[...]
+    for k in range(RANKS):
+
+        @pl.when(slot == k)
+        def _(k=k):
+            leave(k).start()
 
     @pl.when(s == RANKS - 1)
     def _():
         in_grad_ref[...] = grad_one_ref[...] + mm_nt(dx_s[...].astype(BF), column_order())
-
-
-def attention_backward(place, ga, own_att, got_att, qkv, wq, mixed, probs, xp, vec_g, up_g, grad_one):
-    per = lambda *shape: pl.BlockSpec(
-        (1, *shape), lambda s, n: (lax.rem(s + SLOTS, RANKS),) + (0,) * len(shape)
-    )
-    own = lambda s: jnp.maximum(s - 2, 0)
-    got = lambda s: jnp.minimum(s, 1)
+        for k in range(2):
+            leave(k).wait()
+
+
+def attention_backward(scalars, ga, atts, qkv, wq, mixed, probs, xp, vec_g, up_g, grad_one):
+    per = lambda *shape: pl.BlockSpec((1, *shape), lambda s, n: (RANKS - 1 - s,) + (0,) * len(shape))
     return call(
         att_bwd_kernel,
         "attention_backward", (RANKS,),
-        [
-            whole(L, D),
-            pl.BlockSpec((1, PART, D), lambda s, n: (own(s), QKV_ROWS // PART, 0)),
-            pl.BlockSpec((1, PART, D), lambda s, n: (got(s), QKV_ROWS // PART, 0)),
+        [whole(L, D)]
+        + [pl.BlockSpec(memory_space=pl.ANY)] * RANKS
+        + [
             per(L, QKV_ROWS), per(HPR, L, L), per(L, PART), per(D, QKV_ROWS),
             whole(L, D), whole(8, D), per(8, D), whole(L, D),
         ],
-        [
-            pl.BlockSpec((1, ATT_ROWS, D), lambda s, n: (own(s), 0, 0)),
-            pl.BlockSpec((1, ATT_ROWS, D), lambda s, n: (got(s), 0, 0)),
-            whole(L, D),
-        ],
-        [shaped(BF, SLOTS, ATT_ROWS, D), shaped(BF, SLOTS, ATT_ROWS, D), shaped(F32, L, D)],
+        [pl.BlockSpec(memory_space=pl.ANY)] * RANKS + [whole(L, D)],
+        [shaped(BF, ATT_ROWS, D)] * RANKS + [shaped(F32, L, D)],
         [
             pltpu.VMEM((L, L), BF),
             pltpu.VMEM((BLK, 4 * BLK), F32),
             pltpu.VMEM((8, 6 * BLK), F32),
             pltpu.VMEM((L, D), F32),
             pltpu.VMEM((D, D), BF),
-            pltpu.VMEM((PART, D), BF),
-            pltpu.VMEM((ATT_ROWS, D), BF),
-        ],
-        (place, ga, own_att, got_att, qkv, probs, mixed, wq, xp, vec_g, up_g, grad_one),
+            pltpu.VMEM((RANKS, PART, D), BF),
+            pltpu.VMEM((2, ATT_ROWS, D), BF),
+            pltpu.SemaphoreType.DMA((RANKS,)),
+            pltpu.SemaphoreType.DMA((RANKS,)),
+        ],
+        (scalars, ga, *atts, qkv, probs, mixed, wq, xp, vec_g, up_g, grad_one),
         flops=12_000_000_000, moved=30_000_000,
     )
 
@@ -837,8 +836,12 @@
     d1 = ring_z(after(d0, y1))
     x3 = swap_x(after(r3, x1))
     y3, d2, d3 = ring_z(after(y2, r3)), swap_x(after(y2, x2)), swap_y(after(x3, y1))
-    pieces = [r0, r1, r2, r3, x0, x1, x2, x3, y0, y1, y2, y3, d0, d1, d2, d3]
-    return merge_blocks(window_places(z, x), pieces, rows)
+    at = window_places(z, x)
+    near_att, ff = merge_blocks(at, (r0, r1, r2, r3, x0, x1, x2, x3), rows, 0)
+    near_got = swap_core(near_att)
+    far_att, ff = merge_blocks(at, (y0, y1, y2, y3, d0, d1, d2, d3), rows, 1, (ff,))
+    far_got = swap_core(far_att)
+    return ((near_att, far_att), ff), ((near_got, far_got), swap_core(after(ff, (near_got, far_got))))
 
 
 def add_low(*terms):
@@ -848,12 +851,16 @@
     return total.astype(BF)
 
 
-def reduce_windows(own, got, z, x, rows):
+def reduce_windows(own_att, got_att, own_ff, got_ff, z, x, rows):
     at = window_places(z, x)
-    a = split_windows(at, ("D3", "Y3", "D2", "D1"), own, got, rows)
+    far_got = swap_core(got_att[1])
+    near_got = swap_core(after(got_att[0], far_got))
+    far = (own_att[1], own_att[1], own_ff), (far_got, far_got, got_ff)
+    a = split_windows(at, ("D3", "Y3", "D2", "D1"), *far, rows)
     y1, z1, x1 = swap_y(a["D3"]), ring_back(a["Y3"]), swap_x(a["D2"])
+    both = (*own_att, own_ff), (near_got, far_got, got_ff)
     a |= split_windows(
-        at, ("X3", "Y2", "Y1", "R3", "X2", "R2", "X1", "R1", "D0", "X0", "Y0", "R0"), own, got, rows
+        at, ("X3", "Y2", "Y1", "R3", "X2", "R2", "X1", "R1", "D0", "X0", "Y0", "R0"), *both, rows
     )
     z2 = ring_back(after(a["D1"], x1))
     y3 = swap_y(after(a["Y1"], x1))
@@ -900,34 +907,30 @@
     at_wide, at_narrow = lax.axis_index("wide"), lax.axis_index("narrow")
     if fits:
         place = jnp.stack([at_wide, at_narrow // 2, at_narrow % 2]).astype(jnp.int32)
-        block = own_block(place, params, rows, spare, wide)
-        own_att, own_ff = gather_blocks(block, at_wide // 2, at_wide % 2, rows)
-        got_att = swap_core(own_att)
-        got_ff = swap_core(after(own_ff, got_att))
+        scalars = jnp.concatenate([pair_lengths[0], place])
+        block = own_block(scalars, params, rows, spare, wide)
+        (own_att, own_ff), (got_att, got_ff) = gather_blocks(block, at_wide // 2, at_wide % 2, rows)
     else:
-        place = jnp.zeros((3,), jnp.int32)
+        scalars = jnp.concatenate([pair_lengths[0], jnp.zeros((3,), jnp.int32)])
         (own_att, own_ff), (got_att, got_ff) = gather_plain(params)
-    scalars = jnp.concatenate([pair_lengths[0], place])
-    tails = jnp.concatenate([own_att[:, D:], got_att[:, D:]], axis=0)
-
-    qkv, wq, mixed, probs, xp, n1, r1 = attention_forward(scalars, hidden_in, own_att, got_att, tails)
+    atts = (own_att[0], own_att[1], got_att[0], got_att[1])
+
+    qkv, wq, mixed, probs, xp, n1, r1, tails = attention_forward(scalars, hidden_in, atts)
     block_out, own_ffg, got_ffg, grad_one, ga, vec_g, up_g = feed_forward(
-        place, n1, r1, out_grad, own_ff, got_ff, tails
-    )
-    own_attg, got_attg, in_grad = attention_backward(
-        place, ga, own_att, got_att, qkv, wq, mixed, probs, xp, vec_g, up_g, grad_one
-    )
+        scalars, n1, r1, out_grad, own_ff, got_ff, tails
+    )
+    *attg, in_grad = attention_backward(scalars, ga, atts, qkv, wq, mixed, probs, xp, vec_g, up_g, grad_one)
+    own_attg, got_attg = attg[:2], attg[2:]
 
     device_count = wide * ranks
     rate = 1.0 / (32.0 * math.sqrt(hidden_in.shape[0] * device_count))
     if fits:
-        got = swap_core(got_attg), swap_core(got_ffg)
-        parts = reduce_windows((own_attg, own_ffg), got, at_wide // 2, at_wide % 2, rows)
+        parts = reduce_windows(own_attg, got_attg, own_ffg, swap_core(got_ffg), at_wide // 2, at_wide % 2, rows)
         grads, new_params, new_momentum, new_average, low = update_shard(
-            place, parts, params, momentum, average, rate, rows, spare, wide
+            scalars, parts, params, momentum, average, rate, rows, spare, wide
         )
     else:
-        grads = scatter_plain(((own_attg, own_ffg), (got_attg, got_ffg)), shard, wide)
+        grads = scatter_plain(((jnp.stack(own_attg), own_ffg), (jnp.stack(got_attg), got_ffg)), shard, wide)
         new_momentum = 0.5 * momentum + rate * grads
         new_params = params - (rate * grads + 0.5 * new_momentum)
         new_average = 0.5 * average + 0.5 * new_params

time: 234 us -> 229 us (0.979)
  waiting for transfers between devices: 88.6 us -> 80.4 us
  Pallas kernels: 101 us -> 105 us
    ppermute x4 -> x6, waiting for transfers between devices: 9.52 us -> 5.76 us  [swap_core(): return lax.ppermute(a, 'narrow', CORE_SWAP)]
    pallas_call x8 -> x9, Pallas kernels: 101 us -> 105 us  [call(): pl.pallas_call(kernel, grid_spec=pltpu.PrefetchScalarGridSpec(num_scalar_...]
    ppermute x10, waiting for transfers between devices: 23.9 us -> 21.2 us  [swap_x(): return lax.ppermute(a, 'wide', X_SWAP)]
  transfers between devices with their start and end apart: 34 -> 36, of which waited for: 18 -> 17; matrix products, arithmetic and copies ran while one was open for 3% -> 1% of each run, Pallas kernels for 24% -> 31%
where the time goes in v5:
time: 229 us; the launch traced here: 228 us
  Pallas kernels  105 us (46%)
  waiting for transfers between devices  80.4 us (35%)
  starting transfers between devices  34.8 us (15%)
  local copies, waits for them, and re-layouts  3.87 us (2%)
  other arithmetic  3.63 us (2%)
    pallas_call x9, Pallas kernels, call(): pl.pallas_call(kernel, grid_spec=pltpu.PrefetchScalarGridSpec(num_scalar_...  105 us
    ppermute x5, waiting for transfers between devices, ring_z(): return lax.ppermute(a, 'wide', Z_RING)  31.3 us
    ppermute x10, waiting for transfers between devices, swap_x(): return lax.ppermute(a, 'wide', X_SWAP)  21.2 us
    ppermute x10, waiting for transfers between devices, swap_y(): return lax.ppermute(a, 'narrow', Y_SWAP)  21 us
    ppermute x10, starting transfers between devices, swap_y(): return lax.ppermute(a, 'narrow', Y_SWAP)  11.9 us
    ppermute x10, starting transfers between devices, swap_x(): return lax.ppermute(a, 'wide', X_SWAP)  11.7 us
    ppermute x5, starting transfers between devices, ring_back(): return lax.ppermute(a, 'wide', [(j, i) for i, j in Z_RING])  6.86 us
    ppermute x6, waiting for transfers between devices, swap_core(): return lax.ppermute(a, 'narrow', CORE_SWAP)  5.76 us
  transfers between devices with their start and end apart: 36, of which 17 were waited for; matrix products, arithmetic and copies ran while one was open for 1% of the time, Pallas kernels for 31%

profile of v5, /device:TPU:0, one launch (start us, length us, event | category | flops | bytes accessed | tf_op | source)
XLA Modules:
  0.0 228.4 jit_solution(10389733202163771583)
XLA Ops:
  3.3 3.1 %collective-permute-start = (bf16[296,768]{1,0:T(8,128)(2,1)S(1)}, bf16[296,768]{1,0:T(8,128)(2,1)S(1)}, u32[]{:S(2)}, u32[]{:S(2)}) collective-permute-start(bf16[296,768]{1,0:T(8,128)(2,1)S(1)} %own_block.1.refs_0_), channel_id=1, source_target_pairs={{0,8},{4,12},{8,16},{12,20},{16,24},{20,28},{24,0},{28,4},{1,9},{5... | collective-permute-start | bytes 1363976 | tf_op jit(solution)/shard_map/ppermute | solution.py:796
  9.4 9.4 %collective-permute-done.refs_1_ = bf16[296,768]{1,0:T(8,128)(2,1)S(1)} collective-permute-done((bf16[296,768]{1,0:T(8,128)(2,1)S(1)}, bf16[296,768]{1,0:T(8,128)(2,1)S(1)}, u32[]{:S(2)}, u32[]{:S(2)}) %collective-permute-start) | collective-permute-done | bytes 454688 | tf_op jit(solution)/shard_map/ppermute | solution.py:796
  21.9 10.3 %collective-permute-done.1.refs_2_ = bf16[296,768]{1,0:T(8,128)(2,1)S(1)} collective-permute-done((bf16[296,768]{1,0:T(8,128)(2,1)S(1)}, bf16[296,768]{1,0:T(8,128)(2,1)S(1)}, u32[]{:S(2)}, u32[]{:S(2)}) %collective-permute-start.1) | collective-permute-done | bytes 454688 | tf_op jit(solution)/shard_map/ppermute | solution.py:796
  35.5 9.2 %collective-permute-done.2.refs_3_ = bf16[296,768]{1,0:T(8,128)(2,1)S(1)} collective-permute-done((bf16[296,768]{1,0:T(8,128)(2,1)S(1)}, bf16[296,768]{1,0:T(8,128)(2,1)S(1)}, u32[]{:S(2)}, u32[]{:S(2)}) %collective-permute-start.2) | collective-permute-done | bytes 454688 | tf_op jit(solution)/shard_map/ppermute | solution.py:796
  45.8 7.0 %collective-permute-done.10.refs_2_ = bf16[296,768]{1,0:T(8,128)(2,1)} collective-permute-done((bf16[296,768]{1,0:T(8,128)(2,1)S(1)}, bf16[296,768]{1,0:T(8,128)(2,1)}, u32[]{:S(2)}, u32[]{:S(2)}) %collective-permute-start.10) | collective-permute-done | bytes 454688 | tf_op jit(solution)/shard_map/ppermute | solution.py:792
  53.9 2.4 %collective-permute-done.6.refs_7_ = bf16[296,768]{1,0:T(8,128)(2,1)} collective-permute-done((bf16[296,768]{1,0:T(8,128)(2,1)S(1)}, bf16[296,768]{1,0:T(8,128)(2,1)}, u32[]{:S(2)}, u32[]{:S(2)}) %collective-permute-start.6) | collective-permute-done | bytes 454688 | tf_op jit(solution)/shard_map/ppermute | solution.py:788
  57.7 4.7 %merge_weights.2 = (bf16[776,768]{1,0:T(8,128)(2,1)}, bf16[2,1536,768]{2,1,0:T(8,128)(2,1)}) custom-call(s32[8]{0:T(128)} %pad_add_fusion.1.at_ref, bf16[296,768]{1,0:T(8,128)(2,1)} %copy-done.2, bf16[296,768]{1,0:T(8,128)(2,1)} %copy-done.13, bf16[296,768]{1,0:T(8,128)(2,1)} %copy-done.16, bf16[296,768]{1,0:T(8,128)(2,1)} %copy-done.19, ...), custom_call_target="tpu_custom_call" | custom-call | tf_op jit(solution)/shard_map/merge_weights/pallas_call | solution.py:106
  62.6 1.9 collective-permute-done.13.refs_6_
  64.5 2.3 %collective-permute-done.11.refs_3_ = bf16[296,768]{1,0:T(8,128)(2,1)} collective-permute-done((bf16[296,768]{1,0:T(8,128)(2,1)}, bf16[296,768]{1,0:T(8,128)(2,1)}, u32[]{:S(2)}, u32[]{:S(2)}) %collective-permute-start.11) | collective-permute-done | bytes 454688 | tf_op jit(solution)/shard_map/ppermute | solution.py:796
  66.8 4.6 %merge_weights.3 = (bf16[776,768]{1,0:T(8,128)(2,1)}, bf16[2,1536,768]{2,1,0:T(8,128)(2,1)}) custom-call(s32[8]{0:T(128)} %pad_add_fusion.1.at_ref, bf16[296,768]{1,0:T(8,128)(2,1)} %copy-done.11, bf16[296,768]{1,0:T(8,128)(2,1)} %copy-done.15, bf16[296,768]{1,0:T(8,128)(2,1)} %collective-permute-done.10.refs_2_, ...), custom_call_target="tpu_custom_call", output_to_operand_aliasing={{1}: (9, {})} | custom-call | tf_op jit(solution)/shard_map/merge_weights/pallas_call | solution.py:106
  71.6 3.0 %collective-permute-done.16.att3_ref = bf16[776,768]{1,0:T(8,128)(2,1)S(1)} collective-permute-done((bf16[776,768]{1,0:T(8,128)(2,1)}, bf16[776,768]{1,0:T(8,128)(2,1)S(1)}, u32[]{:S(2)}, u32[]{:S(2)}) %collective-permute-start.16) | collective-permute-done | bytes 1191968 | tf_op jit(solution)/shard_map/ppermute | solution.py:804
  75.7 20.1 %attention_forward.1 = (bf16[4,512,576]{2,1,0:T(8,128)(2,1)}, bf16[4,768,576]{2,1,0:T(8,128)(2,1)}, bf16[4,512,192]{2,1,0:T(8,128)(2,1)}, bf16[4,3,512,512]{3,2,...) custom-call(s32[7]{0:T(128)} %copy-done.6, ...), custom_call_target="tpu_custom_call" | custom-call | flops 6000000000 | bytes 24000000 | tf_op jit(solution)/shard_map/attention_forward/pallas_call | solution.py:106
  95.7 29.5 %feed_forward.1 = (bf16[512,768]{1,0:T(8,128)(2,1)}, bf16[2,1536,768]{2,1,0:T(8,128)(2,1)}, bf16[2,1536,768]{2,1,0:T(8,128)(2,1)}, f32[512,768]{1,0:T(8,128)}, b...) custom-call(s32[7]{0:T(128)} %copy-done.6, f32[512,768]{1,0:T(8,128)} %get-tuple-element.82.n1_ref, ...), custom_call_target="tpu_custom_call" | custom-call | flops 14499999744 | bytes 36000000 | tf_op jit(solution)/shard_map/feed_forward/pallas_call | solution.py:106
  125.5 30.0 %attention_backward.1 = (bf16[776,768]{1,0:T(8,128)(2,1)}, bf16[776,768]{1,0:T(8,128)(2,1)}, bf16[776,768]{1,0:T(8,128)(2,1)}, bf16[776,768]{1,0:T(8,128)(2,1)}, f32[512,768]{1,0:T(8,128)}) custom-call(s32[7]{0:T(128)} %copy-done.6, bf16[512,768]{1,0:T(8,128)(2,1)} %get-tuple-element.88.ga_ref, bf16[776,768]{1,0:T(8,128)(2,1)} %get-tuple-element.72.att0_ref, ...), custom_call_target="tpu_custom_call" | custom-call | flops 12000000000 | bytes 30000000 | tf_op jit(solution)/shard_map/attention_backward/pallas_call | solution.py:106
  155.9 2.7 %collective-permute-done.18.refs_4_.refs_3_ = bf16[776,768]{1,0:T(8,128)(2,1)S(1)} collective-permute-done((bf16[776,768]{1,0:T(8,128)(2,1)}, bf16[776,768]{1,0:T(8,128)(2,1)S(1)}, u32[]{:S(2)}, u32[]{:S(2)}) %collective-permute-start.18) | collective-permute-done | bytes 1191968 | tf_op jit(solution)/shard_map/ppermute | solution.py:804
  159.6 4.0 %split_windows.3 = (bf16[296,768]{1,0:T(8,128)(2,1)}, bf16[296,768]{1,0:T(8,128)(2,1)}, bf16[296,768]{1,0:T(8,128)(2,1)}, bf16[296,768]{1,0:T(8,128)(2,1)}) custom-call(s32[8]{0:T(128)} %pad_add_fusion.1.at_ref, bf16[776,768]{1,0:T(8,128)(2,1)} %get-tuple-element.99.refs_1_.refs_0_, bf16[776,768]{1,0:T(8,128)(2,1)} %get-tuple-element.99.refs_1_.refs_0_, ...), custom_call_target="tpu_custom_call" | custom-call | tf_op jit(solution)/shard_map/split_windows/pallas_call | solution.py:106
  168.3 7.5 %split_windows.2 = (bf16[296,768]{1,0:T(8,128)(2,1)}, bf16[296,768]{1,0:T(8,128)(2,1)}, bf16[296,768]{1,0:T(8,128)(2,1)}, bf16[296,768]{1,0:T(8,128)(2,1)}, bf16...) custom-call(s32[8]{0:T(128)} %pad_add_fusion.1.at_ref, ...), custom_call_target="tpu_custom_call" | custom-call | tf_op jit(solution)/shard_map/split_windows/pallas_call | solution.py:106
  181.8 8.0 %collective-permute-done.26 = bf16[296,768]{1,0:T(8,128)(2,1)S(1)} collective-permute-done((bf16[296,768]{1,0:T(8,128)(2,1)S(1)}, bf16[296,768]{1,0:T(8,128)(2,1)S(1)}, u32[]{:S(2)}, u32[]{:S(2)}) %collective-permute-start.26) | collective-permute-done | bytes 454688 | tf_op jit(solution)/shard_map/ppermute | solution.py:788
  194.2 6.5 %collective-permute-done.28 = bf16[296,768]{1,0:T(8,128)(2,1)S(1)} collective-permute-done((bf16[296,768]{1,0:T(8,128)(2,1)S(1)}, bf16[296,768]{1,0:T(8,128)(2,1)S(1)}, u32[]{:S(2)}, u32[]{:S(2)}) %collective-permute-start.28) | collective-permute-done | bytes 454688 | tf_op jit(solution)/shard_map/ppermute | solution.py:788
  202.2 2.6 %collective-permute-start.29 = (bf16[296,768]{1,0:T(8,128)(2,1)S(1)}, bf16[296,768]{1,0:T(8,128)(2,1)S(1)}, u32[]{:S(2)}, u32[]{:S(2)}) collective-permute-start(bf16[296,768]{1,0:T(8,128)(2,1)S(1)} %add_convert_fusion.3), channel_id=1, source_target_pairs={{8,0},{12,4},{16,8},{20,12},{24,16},{28,20},{0,24},{4,28},{9,1},{1... | collective-permute-start | bytes 1363976 | tf_op jit(solution)/shard_map/ppermute | solution.py:800
  206.3 8.7 %collective-permute-done.33 = bf16[296,768]{1,0:T(8,128)(2,1)S(1)} collective-permute-done((bf16[296,768]{1,0:T(8,128)(2,1)S(1)}, bf16[296,768]{1,0:T(8,128)(2,1)S(1)}, u32[]{:S(2)}, u32[]{:S(2)}) %collective-permute-start.33) | collective-permute-done | bytes 454688 | tf_op jit(solution)/shard_map/ppermute | solution.py:792
  217.3 4.6 %collective-permute-done.35.ring_ref = bf16[296,768]{1,0:T(8,128)(2,1)S(1)} collective-permute-done((bf16[296,768]{1,0:T(8,128)(2,1)S(1)}, bf16[296,768]{1,0:T(8,128)(2,1)S(1)}, u32[]{:S(2)}, u32[]{:S(2)}) %collective-permute-start.35) | collective-permute-done | bytes 454688 | tf_op jit(solution)/shard_map/ppermute | solution.py:792
  221.9 1.8 collective-permute-done.34.second_ref
  224.8 3.6 %update_shard.1 = (f32[1,221568]{1,0:T(1,128)}, f32[1,221568]{1,0:T(1,128)}, f32[1,221568]{1,0:T(1,128)}, f32[1,221568]{1,0:T(1,128)}, bf16[1,221568]{1,0:T(2,128)(2,1)}) custom-call(s32[7]{0:T(128)S(1)} %copy-done.7, bf16[296,768]{1,0:T(8,128)(2,1)S(1)} %copy-done.5, bf16[296,768]{1,0:T(8,128)(2,1)S(1)} %collective-permute-done.31.near_ref, ...), custom_call_target="tpu_custom_call" | custom-call | tf_op jit(solution)/shard_map/update_shard/pallas_call | solution.py:106
  (131 shorter events, 39.9 us)
Async XLA Ops:
  3.3 15.6 %collective-permute-start = (bf16[296,768]{1,0:T(8,128)(2,1)S(1)}, bf16[296,768]{1,0:T(8,128)(2,1)S(1)}, u32[]{:S(2)}, u32[]{:S(2)}) collective-permute-start(bf16[296,768]{1,0:T(8,128)(2,1)S(1)} %own_block.1.refs_0_), channel_id=1, source_target_pairs={{0,8},{4,12},{8,16},{12,20},{16,24},{20,28},{24,0},{28,4},{1,9},{5... | collective-permute-start | bytes 1363976 | tf_op jit(solution)/shard_map/ppermute | solution.py:796
  6.4 12.5 %collective-permute-start.7 = (bf16[296,768]{1,0:T(8,128)(2,1)S(1)}, bf16[296,768]{1,0:T(8,128)(2,1)S(1)}, u32[]{:S(2)}, u32[]{:S(2)}) collective-permute-start(bf16[296,768]{1,0:T(8,128)(2,1)S(1)} %own_block.1.refs_0_), channel_id=1, source_target_pairs={{0,2},{1,3},{2,0},{3,1},{4,6},{5,7},{6,4},{7,5},{8,10},{9,11},{10,... | collective-permute-start | bytes 1363976 | tf_op jit(solution)/shard_map/ppermute | solution.py:792
  18.8 13.4 %collective-permute-start.1 = (bf16[296,768]{1,0:T(8,128)(2,1)S(1)}, bf16[296,768]{1,0:T(8,128)(2,1)S(1)}, u32[]{:S(2)}, u32[]{:S(2)}) collective-permute-start(bf16[296,768]{1,0:T(8,128)(2,1)S(1)} %collective-permute-done.refs_1_), channel_id=1, source_target_pairs={{0,8},{4,12},{8,16},{12,20},{16,24},{20,28},{24,0},{28,4},{1,9},{5... | collective-permute-start | bytes 1363976 | tf_op jit(solution)/shard_map/ppermute | solution.py:796
  19.5 14.0 %collective-permute-start.9 = (bf16[296,768]{1,0:T(8,128)(2,1)S(1)}, bf16[296,768]{1,0:T(8,128)(2,1)S(1)}, u32[]{:S(2)}, u32[]{:S(2)}) collective-permute-start(bf16[296,768]{1,0:T(8,128)(2,1)S(1)} %collective-permute-done.3.refs_4_), channel_id=1, source_target_pairs={{0,2},{1,3},{2,0},{3,1},{4,6},{5,7},{6,4},{7,5},{8,10},{9,11},{10,... | collective-permute-start | bytes 1363976 | tf_op jit(solution)/shard_map/ppermute | solution.py:792
  20.5 15.1 %collective-permute-start.4 = (bf16[296,768]{1,0:T(8,128)(2,1)S(1)}, bf16[296,768]{1,0:T(8,128)(2,1)S(1)}, u32[]{:S(2)}, u32[]{:S(2)}) collective-permute-start(bf16[296,768]{1,0:T(8,128)(2,1)S(1)} %collective-permute-done.refs_1_), channel_id=1, source_target_pairs={{0,4},{4,0},{8,12},{12,8},{16,20},{20,16},{24,28},{28,24},{1,5},{5... | collective-permute-start | bytes 1363976 | tf_op jit(solution)/shard_map/ppermute | solution.py:788
  32.2 12.5 %collective-permute-start.2 = (bf16[296,768]{1,0:T(8,128)(2,1)S(1)}, bf16[296,768]{1,0:T(8,128)(2,1)S(1)}, u32[]{:S(2)}, u32[]{:S(2)}) collective-permute-start(bf16[296,768]{1,0:T(8,128)(2,1)S(1)} %collective-permute-done.1.refs_2_), channel_id=1, source_target_pairs={{0,8},{4,12},{8,16},{12,20},{16,24},{20,28},{24,0},{28,4},{1,9},{5... | collective-permute-start | bytes 1363976 | tf_op jit(solution)/shard_map/ppermute | solution.py:796
  32.2 13.6 %collective-permute-start.8 = (bf16[296,768]{1,0:T(8,128)(2,1)S(1)}, bf16[296,768]{1,0:T(8,128)(2,1)S(1)}, u32[]{:S(2)}, u32[]{:S(2)}) collective-permute-start(bf16[296,768]{1,0:T(8,128)(2,1)S(1)} %collective-permute-done.refs_1_), channel_id=1, source_target_pairs={{0,2},{1,3},{2,0},{3,1},{4,6},{5,7},{6,4},{7,5},{8,10},{9,11},{10,... | collective-permute-start | bytes 1363976 | tf_op jit(solution)/shard_map/ppermute | solution.py:792
  33.5 12.3 %collective-permute-start.5 = (bf16[296,768]{1,0:T(8,128)(2,1)S(1)}, bf16[296,768]{1,0:T(8,128)(2,1)S(1)}, u32[]{:S(2)}, u32[]{:S(2)}) collective-permute-start(bf16[296,768]{1,0:T(8,128)(2,1)S(1)} %collective-permute-done.1.refs_2_), channel_id=1, source_target_pairs={{0,4},{4,0},{8,12},{12,8},{16,20},{20,16},{24,28},{28,24},{1,5},{5... | collective-permute-start | bytes 1363976 | tf_op jit(solution)/shard_map/ppermute | solution.py:788
  35.0 17.8 %collective-permute-start.10 = (bf16[296,768]{1,0:T(8,128)(2,1)S(1)}, bf16[296,768]{1,0:T(8,128)(2,1)}, u32[]{:S(2)}, u32[]{:S(2)}) collective-permute-start(bf16[296,768]{1,0:T(8,128)(2,1)S(1)} %collective-permute-done.1.refs_2_), channel_id=1, source_target_pairs={{0,2},{1,3},{2,0},{3,1},{4,6},{5,7},{6,4},{7,5},{8,10},{9,11},{10,... | collective-permute-start | bytes 1363976 | tf_op jit(solution)/shard_map/ppermute | solution.py:792
  45.8 16.7 %collective-permute-start.12 = (bf16[296,768]{1,0:T(8,128)(2,1)S(1)}, bf16[296,768]{1,0:T(8,128)(2,1)}, u32[]{:S(2)}, u32[]{:S(2)}) collective-permute-start(bf16[296,768]{1,0:T(8,128)(2,1)S(1)} %collective-permute-done.9.refs_4_), channel_id=1, source_target_pairs={{0,8},{4,12},{8,16},{12,20},{16,24},{20,28},{24,0},{28,4},{1,9},{5... | collective-permute-start | bytes 1363976 | tf_op jit(solution)/shard_map/ppermute | solution.py:796
  53.9 13.0 %collective-permute-start.11 = (bf16[296,768]{1,0:T(8,128)(2,1)}, bf16[296,768]{1,0:T(8,128)(2,1)}, u32[]{:S(2)}, u32[]{:S(2)}) collective-permute-start(bf16[296,768]{1,0:T(8,128)(2,1)} %collective-permute-done.10.refs_2_), channel_id=1, source_target_pairs={{0,8},{4,12},{8,16},{12,20},{16,24},{20,28},{24,0},{28,4},{1,9},{5... | collective-permute-start | bytes 1363976 | tf_op jit(solution)/shard_map/ppermute | solution.py:796
  74.6 21.1 %collective-permute-start.17 = (bf16[2,1536,768]{2,1,0:T(8,128)(2,1)}, bf16[2,1536,768]{2,1,0:T(8,128)(2,1)}, u32[]{:S(2)}, u32[]{:S(2)}) collective-permute-start(bf16[2,1536,768]{2,1,0:T(8,128)(2,1)} %get-tuple-element.85.up0_ref.down0_ref), channel_id=1, source_target_pairs={{0,1},{1,0},{2,3},{3,2},{4,5},{5,4},{6,7},{7,6},{8,9},{9,8},{10,11... | collective-permute-start | bytes 14155784 | tf_op jit(solution)/shard_map/ppermute | solution.py:804
  125.3 33.7 %collective-permute-start.20 = (bf16[2,1536,768]{2,1,0:T(8,128)(2,1)}, bf16[2,1536,768]{2,1,0:T(8,128)(2,1)}, u32[]{:S(2)}, u32[]{:S(2)}) collective-permute-start(bf16[2,1536,768]{2,1,0:T(8,128)(2,1)} %get-tuple-element.104), channel_id=1, source_target_pairs={{0,1},{1,0},{2,3},{3,2},{4,5},{5,4},{6,7},{7,6},{8,9},{9,8},{10,11... | collective-permute-start | bytes 14155784 | tf_op jit(solution)/shard_map/ppermute | solution.py:804
  163.6 13.0 %collective-permute-start.25 = (bf16[296,768]{1,0:T(8,128)(2,1)}, bf16[296,768]{1,0:T(8,128)(2,1)S(1)}, u32[]{:S(2)}, u32[]{:S(2)}) collective-permute-start(bf16[296,768]{1,0:T(8,128)(2,1)} %get-tuple-element.115), channel_id=1, source_target_pairs={{0,2},{1,3},{2,0},{3,1},{4,6},{5,7},{6,4},{7,5},{8,10},{9,11},{10,... | collective-permute-start | bytes 1363976 | tf_op jit(solution)/shard_map/ppermute | solution.py:792
  165.2 13.9 %collective-permute-start.21 = (bf16[296,768]{1,0:T(8,128)(2,1)}, bf16[296,768]{1,0:T(8,128)(2,1)S(1)}, u32[]{:S(2)}, u32[]{:S(2)}) collective-permute-start(bf16[296,768]{1,0:T(8,128)(2,1)} %get-tuple-element.108), channel_id=1, source_target_pairs={{0,4},{4,0},{8,12},{12,8},{16,20},{20,16},{24,28},{28,24},{1,5},{5... | collective-permute-start | bytes 1363976 | tf_op jit(solution)/shard_map/ppermute | solution.py:788
  165.7 14.2 %collective-permute-start.23 = (bf16[296,768]{1,0:T(8,128)(2,1)}, bf16[296,768]{1,0:T(8,128)(2,1)S(1)}, u32[]{:S(2)}, u32[]{:S(2)}) collective-permute-start(bf16[296,768]{1,0:T(8,128)(2,1)} %get-tuple-element.112), channel_id=1, source_target_pairs={{8,0},{12,4},{16,8},{20,12},{24,16},{28,20},{0,24},{4,28},{9,1},{1... | collective-permute-start | bytes 1363976 | tf_op jit(solution)/shard_map/ppermute | solution.py:800
  177.8 11.9 %collective-permute-start.26 = (bf16[296,768]{1,0:T(8,128)(2,1)S(1)}, bf16[296,768]{1,0:T(8,128)(2,1)S(1)}, u32[]{:S(2)}, u32[]{:S(2)}) collective-permute-start(bf16[296,768]{1,0:T(8,128)(2,1)S(1)} %add_convert_fusion.5), channel_id=1, source_target_pairs={{0,4},{4,0},{8,12},{12,8},{16,20},{20,16},{24,28},{28,24},{1,5},{5... | collective-permute-start | bytes 1363976 | tf_op jit(solution)/shard_map/ppermute | solution.py:788
  179.1 14.4 %collective-permute-start.32 = (bf16[296,768]{1,0:T(8,128)(2,1)S(1)}, bf16[296,768]{1,0:T(8,128)(2,1)S(1)}, u32[]{:S(2)}, u32[]{:S(2)}) collective-permute-start(bf16[296,768]{1,0:T(8,128)(2,1)S(1)} %copy-done.30), channel_id=1, source_target_pairs={{8,0},{12,4},{16,8},{20,12},{24,16},{28,20},{0,24},{4,28},{9,1},{1... | collective-permute-start | bytes 1363976 | tf_op jit(solution)/shard_map/ppermute | solution.py:800
  180.2 21.8 %collective-permute-start.24 = (bf16[296,768]{1,0:T(8,128)(2,1)S(1)}, bf16[296,768]{1,0:T(8,128)(2,1)S(1)}, u32[]{:S(2)}, u32[]{:S(2)}) collective-permute-start(bf16[296,768]{1,0:T(8,128)(2,1)S(1)} %add_convert_fusion.6), channel_id=1, source_target_pairs={{0,2},{1,3},{2,0},{3,1},{4,6},{5,7},{6,4},{7,5},{8,10},{9,11},{10,... | collective-permute-start | bytes 1363976 | tf_op jit(solution)/shard_map/ppermute | solution.py:792
  192.0 24.0 %collective-permute-start.22 = (bf16[296,768]{1,0:T(8,128)(2,1)S(1)}, bf16[296,768]{1,0:T(8,128)(2,1)S(1)}, u32[]{:S(2)}, u32[]{:S(2)}) collective-permute-start(bf16[296,768]{1,0:T(8,128)(2,1)S(1)} %copy-done.29), channel_id=1, source_target_pairs={{0,2},{1,3},{2,0},{3,1},{4,6},{5,7},{6,4},{7,5},{8,10},{9,11},{10,... | collective-permute-start | bytes 1363976 | tf_op jit(solution)/shard_map/ppermute | solution.py:792
  193.6 21.4 %collective-permute-start.33 = (bf16[296,768]{1,0:T(8,128)(2,1)S(1)}, bf16[296,768]{1,0:T(8,128)(2,1)S(1)}, u32[]{:S(2)}, u32[]{:S(2)}) collective-permute-start(bf16[296,768]{1,0:T(8,128)(2,1)S(1)} %add_convert_fusion.1), channel_id=1, source_target_pairs={{0,2},{1,3},{2,0},{3,1},{4,6},{5,7},{6,4},{7,5},{8,10},{9,11},{10,... | collective-permute-start | bytes 1363976 | tf_op jit(solution)/shard_map/ppermute | solution.py:792
  200.7 15.3 %collective-permute-start.30 = (bf16[296,768]{1,0:T(8,128)(2,1)S(1)}, bf16[296,768]{1,0:T(8,128)(2,1)S(1)}, u32[]{:S(2)}, u32[]{:S(2)}) collective-permute-start(bf16[296,768]{1,0:T(8,128)(2,1)S(1)} %copy-done.28), channel_id=1, source_target_pairs={{0,4},{4,0},{8,12},{12,8},{16,20},{20,16},{24,28},{28,24},{1,5},{5... | collective-permute-start | bytes 1363976 | tf_op jit(solution)/shard_map/ppermute | solution.py:788
  202.2 13.8 %collective-permute-start.29 = (bf16[296,768]{1,0:T(8,128)(2,1)S(1)}, bf16[296,768]{1,0:T(8,128)(2,1)S(1)}, u32[]{:S(2)}, u32[]{:S(2)}) collective-permute-start(bf16[296,768]{1,0:T(8,128)(2,1)S(1)} %add_convert_fusion.3), channel_id=1, source_target_pairs={{8,0},{12,4},{16,8},{20,12},{24,16},{28,20},{0,24},{4,28},{9,1},{1... | collective-permute-start | bytes 1363976 | tf_op jit(solution)/shard_map/ppermute | solution.py:800
  204.8 17.1 %collective-permute-start.35 = (bf16[296,768]{1,0:T(8,128)(2,1)S(1)}, bf16[296,768]{1,0:T(8,128)(2,1)S(1)}, u32[]{:S(2)}, u32[]{:S(2)}) collective-permute-start(bf16[296,768]{1,0:T(8,128)(2,1)S(1)} %copy-done.27), channel_id=1, source_target_pairs={{0,2},{1,3},{2,0},{3,1},{4,6},{5,7},{6,4},{7,5},{8,10},{9,11},{10,... | collective-permute-start | bytes 1363976 | tf_op jit(solution)/shard_map/ppermute | solution.py:792
  (44 other events, 664.6 us)

commit v6 on v5

--- a/solution.py
+++ b/solution.py
@@ -495,7 +495,7 @@
 def ffn_kernel(
     place_ref, n1_ref, r1_ref, og_ref, up0_ref, down0_ref, up1_ref, down1_ref, tails_ref,
     block_ref, grad0_ref, grad1_ref, grad_one_ref, ga_ref, vec_ref, bup_ref,
-    fn_s, fl_s, slope_s, act_s, down_s, gd_s, gf_s,
+    fn_s, fl_s, slope_s, act_s, down_s, gd_s, gf_s, og_s, og_sem,
 ):
     step = pl.program_id(0)
     inv_root2 = 1.0 / math.sqrt(2.0)
@@ -504,6 +504,7 @@
     def _():
         vec = vector_rows(tails_ref, PlaceView(place_ref))
         first = n1_ref[...] * vec[2] + vec[3]
+        pltpu.make_async_copy(og_ref, og_s, og_sem).start()
         fn_s[...] = first
         fl_s[...] = first.astype(BF)
         down_s[...] = jnp.zeros_like(down_s)
@@ -530,7 +531,8 @@
         vec = vector_rows(tails_ref, PlaceView(place_ref))
         normed, inv = normalize(fn_s[...] + down_s[...] + vec[1])
         block_ref[...] = (normed * vec[4] + vec[5]).astype(BF)
-        og = og_ref[...].astype(F32)
+        pltpu.make_async_copy(og_ref, og_s, og_sem).wait()
+        og = og_s[...].astype(F32)
         vec_ref[4:5, :] = col_sum(og * normed)
         vec_ref[5:6, :] = col_sum(og)
         grad_two = norm_backward(og * vec[4], normed, inv)
@@ -583,7 +585,7 @@
         ffn_kernel,
         "feed_forward", (2 * RANKS,),
         [
-            whole(L, D), whole(L, BLK), whole(L, D),
+            whole(L, D), whole(L, BLK), pl.BlockSpec(memory_space=pl.ANY),
             wt(own_at(0)), wt(own_at(1)), wt(got_at(0)), wt(got_at(1)),
             whole(RANKS, TILE_ROWS, D),
         ],
@@ -611,6 +613,8 @@
             pltpu.VMEM((L, D), F32),
             pltpu.VMEM((L, D), BF),
             pltpu.VMEM((L, D), F32),
+            pltpu.VMEM((L, D), BF),
+            pltpu.SemaphoreType.DMA,
         ],
         (place, n1, r1, out_grad, own_ff, own_ff, got_ff, got_ff, tails),
         flops=14_500_000_000, moved=36_000_000,
@@ -632,7 +636,7 @@
     place_ref, ga_ref, att0_ref, att1_ref, att2_ref, att3_ref,
     qkv_ref, probs_ref, mixed_ref, wq_ref, xp_ref, vec_ref, bup_ref, grad_one_ref,
     da0_ref, da1_ref, da2_ref, da3_ref, in_grad_ref,
-    ds_s, near_s, sums_s, dx_s, order_s, wo_s, das_s, sem, out_sem,
+    ds_s, near_s, sums_s, dx_s, order_s, wo_s, das_s, xp_s, one_s, sem, out_sem, late_sem,
 ):
     s = pl.program_id(0)
     slot = RANKS - 1 - s
@@ -652,6 +656,8 @@
     def _():
         for k, att in enumerate((att0_ref, att1_ref, att2_ref, att3_ref)):
             pltpu.make_async_copy(att.at[QKV_ROWS:D], wo_s.at[k], sem.at[k]).start()
+        pltpu.make_async_copy(xp_ref, xp_s, late_sem.at[0]).start()
+        pltpu.make_async_copy(grad_one_ref, one_s, late_sem.at[1]).start()
         order_s[...] = table_order()
         dx_s[...] = jnp.zeros_like(dx_s)
         sums_s[...] = jnp.zeros_like(sums_s)
@@ -729,7 +735,11 @@
     )
     da_s[D:ATT_ROWS, :] = tail.astype(BF)
 
-    dw = mm_tn(xp_ref[...], dqkv).astype(BF)
+    @pl.when(s == 0)
+    def _():
+        pltpu.make_async_copy(xp_ref, xp_s, late_sem.at[0]).wait()
+
+    dw = mm_tn(xp_s[...], dqkv).astype(BF)
     for src_row, src_col, dst_row, dst_col in qkv_pieces():
         da_s[src_row : src_row + 96, src_col : src_col + PART] = dw[
             dst_row : dst_row + 96, dst_col : dst_col + PART
@@ -744,7 +754,8 @@
 
     @pl.when(s == RANKS - 1)
     def _():
-        in_grad_ref[...] = grad_one_ref[...] + mm_nt(dx_s[...].astype(BF), column_order())
+        pltpu.make_async_copy(grad_one_ref, one_s, late_sem.at[1]).wait()
+        in_grad_ref[...] = one_s[...] + mm_nt(dx_s[...].astype(BF), column_order())
         for k in range(2):
             leave(k).wait()
 
@@ -758,7 +769,7 @@
         + [pl.BlockSpec(memory_space=pl.ANY)] * RANKS
         + [
             per(L, QKV_ROWS), per(HPR, L, L), per(L, PART), per(D, QKV_ROWS),
-            whole(L, D), whole(8, D), per(8, D), whole(L, D),
+            pl.BlockSpec(memory_space=pl.ANY), whole(8, D), per(8, D), pl.BlockSpec(memory_space=pl.ANY),
         ],
         [pl.BlockSpec(memory_space=pl.ANY)] * RANKS + [whole(L, D)],
         [shaped(BF, ATT_ROWS, D)] * RANKS + [shaped(F32, L, D)],
@@ -770,8 +781,11 @@
             pltpu.VMEM((D, D), BF),
             pltpu.VMEM((RANKS, PART, D), BF),
             pltpu.VMEM((2, ATT_ROWS, D), BF),
+            pltpu.VMEM((L, D), BF),
+            pltpu.VMEM((L, D), F32),
             pltpu.SemaphoreType.DMA((RANKS,)),
             pltpu.SemaphoreType.DMA((RANKS,)),
+            pltpu.SemaphoreType.DMA((2,)),
         ],
         (scalars, ga, *atts, qkv, probs, mixed, wq, xp, vec_g, up_g, grad_one),
         flops=12_000_000_000, moved=30_000_000,
@@ -856,11 +870,11 @@
     far_got = swap_core(got_att[1])
     near_got = swap_core(after(got_att[0], far_got))
     far = (own_att[1], own_att[1], own_ff), (far_got, far_got, got_ff)
-    a = split_windows(at, ("D3", "Y3", "D2", "D1"), *far, rows)
+    a = split_windows(at, ("D3", "Y3", "D2"), *far, rows)
     y1, z1, x1 = swap_y(a["D3"]), ring_back(a["Y3"]), swap_x(a["D2"])
     both = (*own_att, own_ff), (near_got, far_got, got_ff)
     a |= split_windows(
-        at, ("X3", "Y2", "Y1", "R3", "X2", "R2", "X1", "R1", "D0", "X0", "Y0", "R0"), *both, rows
+        at, ("X3", "Y2", "Y1", "D1", "R3", "X2", "R2", "X1", "R1", "D0", "X0", "Y0", "R0"), *both, rows
     )
     z2 = ring_back(after(a["D1"], x1))
     y3 = swap_y(after(a["Y1"], x1))

time: 229 us -> 228 us (level)
  no operation moved by 1% of the time
where the time goes in v6:
time: 228 us
  Pallas kernels  104 us (46%)
  waiting for transfers between devices  80.2 us (35%)
  starting transfers between devices  34.7 us (15%)
  local copies, waits for them, and re-layouts  3.86 us (2%)
  other arithmetic  3.6 us (2%)
    pallas_call x9, Pallas kernels, call(): pl.pallas_call(kernel, grid_spec=pltpu.PrefetchScalarGridSpec(num_scalar_...  104 us
    ppermute x5, waiting for transfers between devices, ring_z(): return lax.ppermute(a, 'wide', Z_RING)  31.3 us
    ppermute x10, waiting for transfers between devices, swap_x(): return lax.ppermute(a, 'wide', X_SWAP)  21.3 us
    ppermute x10, waiting for transfers between devices, swap_y(): return lax.ppermute(a, 'narrow', Y_SWAP)  20.8 us
    ppermute x10, starting transfers between devices, swap_y(): return lax.ppermute(a, 'narrow', Y_SWAP)  11.9 us
    ppermute x10, starting transfers between devices, swap_x(): return lax.ppermute(a, 'wide', X_SWAP)  11.6 us
    ppermute x5, starting transfers between devices, ring_back(): return lax.ppermute(a, 'wide', [(j, i) for i, j in Z_RING])  6.78 us
    ppermute x6, waiting for transfers between devices, swap_core(): return lax.ppermute(a, 'narrow', CORE_SWAP)  5.75 us
  transfers between devices with their start and end apart: 36, of which 17 were waited for; matrix products, arithmetic and copies ran while one was open for 1% of the time, Pallas kernels for 31%

profile of v6, /device:TPU:0, one launch (start us, length us, event | category | flops | bytes accessed | tf_op | source)
XLA Modules:
  0.0 227.7 jit_solution(17796190458561373651)
XLA Ops:
  3.3 3.1 %collective-permute-start = (bf16[296,768]{1,0:T(8,128)(2,1)S(1)}, bf16[296,768]{1,0:T(8,128)(2,1)S(1)}, u32[]{:S(2)}, u32[]{:S(2)}) collective-permute-start(bf16[296,768]{1,0:T(8,128)(2,1)S(1)} %own_block.1.refs_0_), channel_id=1, source_target_pairs={{0,8},{4,12},{8,16},{12,20},{16,24},{20,28},{24,0},{28,4},{1,9},{5... | collective-permute-start | bytes 1363976 | tf_op jit(solution)/shard_map/ppermute | solution.py:810
  9.4 9.4 %collective-permute-done.refs_1_ = bf16[296,768]{1,0:T(8,128)(2,1)S(1)} collective-permute-done((bf16[296,768]{1,0:T(8,128)(2,1)S(1)}, bf16[296,768]{1,0:T(8,128)(2,1)S(1)}, u32[]{:S(2)}, u32[]{:S(2)}) %collective-permute-start) | collective-permute-done | bytes 454688 | tf_op jit(solution)/shard_map/ppermute | solution.py:810
  21.9 10.3 %collective-permute-done.1.refs_2_ = bf16[296,768]{1,0:T(8,128)(2,1)S(1)} collective-permute-done((bf16[296,768]{1,0:T(8,128)(2,1)S(1)}, bf16[296,768]{1,0:T(8,128)(2,1)S(1)}, u32[]{:S(2)}, u32[]{:S(2)}) %collective-permute-start.1) | collective-permute-done | bytes 454688 | tf_op jit(solution)/shard_map/ppermute | solution.py:810
  35.5 9.2 %collective-permute-done.2.refs_3_ = bf16[296,768]{1,0:T(8,128)(2,1)S(1)} collective-permute-done((bf16[296,768]{1,0:T(8,128)(2,1)S(1)}, bf16[296,768]{1,0:T(8,128)(2,1)S(1)}, u32[]{:S(2)}, u32[]{:S(2)}) %collective-permute-start.2) | collective-permute-done | bytes 454688 | tf_op jit(solution)/shard_map/ppermute | solution.py:810
  45.8 7.0 %collective-permute-done.10.refs_2_ = bf16[296,768]{1,0:T(8,128)(2,1)} collective-permute-done((bf16[296,768]{1,0:T(8,128)(2,1)S(1)}, bf16[296,768]{1,0:T(8,128)(2,1)}, u32[]{:S(2)}, u32[]{:S(2)}) %collective-permute-start.10) | collective-permute-done | bytes 454688 | tf_op jit(solution)/shard_map/ppermute | solution.py:806
  53.9 2.4 %collective-permute-done.6.refs_7_ = bf16[296,768]{1,0:T(8,128)(2,1)} collective-permute-done((bf16[296,768]{1,0:T(8,128)(2,1)S(1)}, bf16[296,768]{1,0:T(8,128)(2,1)}, u32[]{:S(2)}, u32[]{:S(2)}) %collective-permute-start.6) | collective-permute-done | bytes 454688 | tf_op jit(solution)/shard_map/ppermute | solution.py:802
  57.7 4.7 %merge_weights.2 = (bf16[776,768]{1,0:T(8,128)(2,1)}, bf16[2,1536,768]{2,1,0:T(8,128)(2,1)}) custom-call(s32[8]{0:T(128)} %pad_add_fusion.1.at_ref, bf16[296,768]{1,0:T(8,128)(2,1)} %copy-done.2, bf16[296,768]{1,0:T(8,128)(2,1)} %copy-done.13, bf16[296,768]{1,0:T(8,128)(2,1)} %copy-done.16, bf16[296,768]{1,0:T(8,128)(2,1)} %copy-done.19, ...), custom_call_target="tpu_custom_call" | custom-call | tf_op jit(solution)/shard_map/merge_weights/pallas_call | solution.py:106
  62.5 2.0 collective-permute-done.13.refs_6_
  64.5 2.3 %collective-permute-done.11.refs_3_ = bf16[296,768]{1,0:T(8,128)(2,1)} collective-permute-done((bf16[296,768]{1,0:T(8,128)(2,1)}, bf16[296,768]{1,0:T(8,128)(2,1)}, u32[]{:S(2)}, u32[]{:S(2)}) %collective-permute-start.11) | collective-permute-done | bytes 454688 | tf_op jit(solution)/shard_map/ppermute | solution.py:810
  66.8 4.6 %merge_weights.3 = (bf16[776,768]{1,0:T(8,128)(2,1)}, bf16[2,1536,768]{2,1,0:T(8,128)(2,1)}) custom-call(s32[8]{0:T(128)} %pad_add_fusion.1.at_ref, bf16[296,768]{1,0:T(8,128)(2,1)} %copy-done.11, bf16[296,768]{1,0:T(8,128)(2,1)} %copy-done.15, bf16[296,768]{1,0:T(8,128)(2,1)} %collective-permute-done.10.refs_2_, ...), custom_call_target="tpu_custom_call", output_to_operand_aliasing={{1}: (9, {})} | custom-call | tf_op jit(solution)/shard_map/merge_weights/pallas_call | solution.py:106
  71.6 3.0 %collective-permute-done.16.att3_ref = bf16[776,768]{1,0:T(8,128)(2,1)S(1)} collective-permute-done((bf16[776,768]{1,0:T(8,128)(2,1)}, bf16[776,768]{1,0:T(8,128)(2,1)S(1)}, u32[]{:S(2)}, u32[]{:S(2)}) %collective-permute-start.16) | collective-permute-done | bytes 1191968 | tf_op jit(solution)/shard_map/ppermute | solution.py:818
  75.7 20.1 %attention_forward.1 = (bf16[4,512,576]{2,1,0:T(8,128)(2,1)}, bf16[4,768,576]{2,1,0:T(8,128)(2,1)}, bf16[4,512,192]{2,1,0:T(8,128)(2,1)}, bf16[4,3,512,512]{3,2,...) custom-call(s32[7]{0:T(128)} %copy-done.6, ...), custom_call_target="tpu_custom_call" | custom-call | flops 6000000000 | bytes 24000000 | tf_op jit(solution)/shard_map/attention_forward/pallas_call | solution.py:106
  95.7 29.4 %feed_forward.1 = (bf16[512,768]{1,0:T(8,128)(2,1)}, bf16[2,1536,768]{2,1,0:T(8,128)(2,1)}, bf16[2,1536,768]{2,1,0:T(8,128)(2,1)}, f32[512,768]{1,0:T(8,128)}, b...) custom-call(s32[7]{0:T(128)} %copy-done.6, f32[512,768]{1,0:T(8,128)} %get-tuple-element.82.n1_ref, ...), custom_call_target="tpu_custom_call" | custom-call | flops 14499999744 | bytes 36000000 | tf_op jit(solution)/shard_map/feed_forward/pallas_call | solution.py:106
  125.3 29.8 %attention_backward.1 = (bf16[776,768]{1,0:T(8,128)(2,1)}, bf16[776,768]{1,0:T(8,128)(2,1)}, bf16[776,768]{1,0:T(8,128)(2,1)}, bf16[776,768]{1,0:T(8,128)(2,1)}, f32[512,768]{1,0:T(8,128)}) custom-call(s32[7]{0:T(128)} %copy-done.6, bf16[512,768]{1,0:T(8,128)(2,1)} %get-tuple-element.88.ga_ref, bf16[776,768]{1,0:T(8,128)(2,1)} %get-tuple-element.72.att0_ref, ...), custom_call_target="tpu_custom_call" | custom-call | flops 12000000000 | bytes 30000000 | tf_op jit(solution)/shard_map/attention_backward/pallas_call | solution.py:106
  155.6 2.7 %collective-permute-done.18.refs_4_.refs_3_ = bf16[776,768]{1,0:T(8,128)(2,1)S(1)} collective-permute-done((bf16[776,768]{1,0:T(8,128)(2,1)}, bf16[776,768]{1,0:T(8,128)(2,1)S(1)}, u32[]{:S(2)}, u32[]{:S(2)}) %collective-permute-start.18) | collective-permute-done | bytes 1191968 | tf_op jit(solution)/shard_map/ppermute | solution.py:818
  159.3 3.5 %split_windows.3 = (bf16[296,768]{1,0:T(8,128)(2,1)}, bf16[296,768]{1,0:T(8,128)(2,1)}, bf16[296,768]{1,0:T(8,128)(2,1)}) custom-call(s32[8]{0:T(128)} %pad_add_fusion.1.at_ref, bf16[776,768]{1,0:T(8,128)(2,1)} %get-tuple-element.99.refs_1_.refs_0_, bf16[776,768]{1,0:T(8,128)(2,1)} %get-tuple-element.99.refs_1_.refs_0_, ...), custom_call_target="tpu_custom_call" | custom-call | tf_op jit(solution)/shard_map/split_windows/pallas_call | solution.py:106
  167.5 7.8 %split_windows.2 = (bf16[296,768]{1,0:T(8,128)(2,1)}, bf16[296,768]{1,0:T(8,128)(2,1)}, bf16[296,768]{1,0:T(8,128)(2,1)}, bf16[296,768]{1,0:T(8,128)(2,1)}, bf16...) custom-call(s32[8]{0:T(128)} %pad_add_fusion.1.at_ref, ...), custom_call_target="tpu_custom_call" | custom-call | tf_op jit(solution)/shard_map/split_windows/pallas_call | solution.py:106
  181.0 8.0 %collective-permute-done.26 = bf16[296,768]{1,0:T(8,128)(2,1)S(1)} collective-permute-done((bf16[296,768]{1,0:T(8,128)(2,1)S(1)}, bf16[296,768]{1,0:T(8,128)(2,1)S(1)}, u32[]{:S(2)}, u32[]{:S(2)}) %collective-permute-start.26) | collective-permute-done | bytes 454688 | tf_op jit(solution)/shard_map/ppermute | solution.py:802
  193.5 6.6 %collective-permute-done.28 = bf16[296,768]{1,0:T(8,128)(2,1)S(1)} collective-permute-done((bf16[296,768]{1,0:T(8,128)(2,1)S(1)}, bf16[296,768]{1,0:T(8,128)(2,1)S(1)}, u32[]{:S(2)}, u32[]{:S(2)}) %collective-permute-start.28) | collective-permute-done | bytes 454688 | tf_op jit(solution)/shard_map/ppermute | solution.py:802
  201.5 2.5 %collective-permute-start.29 = (bf16[296,768]{1,0:T(8,128)(2,1)S(1)}, bf16[296,768]{1,0:T(8,128)(2,1)S(1)}, u32[]{:S(2)}, u32[]{:S(2)}) collective-permute-start(bf16[296,768]{1,0:T(8,128)(2,1)S(1)} %add_convert_fusion.3), channel_id=1, source_target_pairs={{8,0},{12,4},{16,8},{20,12},{24,16},{28,20},{0,24},{4,28},{9,1},{1... | collective-permute-start | bytes 1363976 | tf_op jit(solution)/shard_map/ppermute | solution.py:814
  205.6 8.7 %collective-permute-done.33 = bf16[296,768]{1,0:T(8,128)(2,1)S(1)} collective-permute-done((bf16[296,768]{1,0:T(8,128)(2,1)S(1)}, bf16[296,768]{1,0:T(8,128)(2,1)S(1)}, u32[]{:S(2)}, u32[]{:S(2)}) %collective-permute-start.33) | collective-permute-done | bytes 454688 | tf_op jit(solution)/shard_map/ppermute | solution.py:806
  216.6 4.6 %collective-permute-done.35.ring_ref = bf16[296,768]{1,0:T(8,128)(2,1)S(1)} collective-permute-done((bf16[296,768]{1,0:T(8,128)(2,1)S(1)}, bf16[296,768]{1,0:T(8,128)(2,1)S(1)}, u32[]{:S(2)}, u32[]{:S(2)}) %collective-permute-start.35) | collective-permute-done | bytes 454688 | tf_op jit(solution)/shard_map/ppermute | solution.py:806
  221.1 1.8 collective-permute-done.34.second_ref
  224.1 3.6 %update_shard.1 = (f32[1,221568]{1,0:T(1,128)}, f32[1,221568]{1,0:T(1,128)}, f32[1,221568]{1,0:T(1,128)}, f32[1,221568]{1,0:T(1,128)}, bf16[1,221568]{1,0:T(2,128)(2,1)}) custom-call(s32[7]{0:T(128)S(1)} %copy-done.7, bf16[296,768]{1,0:T(8,128)(2,1)S(1)} %copy-done.5, bf16[296,768]{1,0:T(8,128)(2,1)S(1)} %collective-permute-done.31.near_ref, ...), custom_call_target="tpu_custom_call" | custom-call | tf_op jit(solution)/shard_map/update_shard/pallas_call | solution.py:106
  (129 shorter events, 39.5 us)
Async XLA Ops:
  3.3 15.6 %collective-permute-start = (bf16[296,768]{1,0:T(8,128)(2,1)S(1)}, bf16[296,768]{1,0:T(8,128)(2,1)S(1)}, u32[]{:S(2)}, u32[]{:S(2)}) collective-permute-start(bf16[296,768]{1,0:T(8,128)(2,1)S(1)} %own_block.1.refs_0_), channel_id=1, source_target_pairs={{0,8},{4,12},{8,16},{12,20},{16,24},{20,28},{24,0},{28,4},{1,9},{5... | collective-permute-start | bytes 1363976 | tf_op jit(solution)/shard_map/ppermute | solution.py:810
  6.4 12.5 %collective-permute-start.7 = (bf16[296,768]{1,0:T(8,128)(2,1)S(1)}, bf16[296,768]{1,0:T(8,128)(2,1)S(1)}, u32[]{:S(2)}, u32[]{:S(2)}) collective-permute-start(bf16[296,768]{1,0:T(8,128)(2,1)S(1)} %own_block.1.refs_0_), channel_id=1, source_target_pairs={{0,2},{1,3},{2,0},{3,1},{4,6},{5,7},{6,4},{7,5},{8,10},{9,11},{10,... | collective-permute-start | bytes 1363976 | tf_op jit(solution)/shard_map/ppermute | solution.py:806
  18.8 13.4 %collective-permute-start.1 = (bf16[296,768]{1,0:T(8,128)(2,1)S(1)}, bf16[296,768]{1,0:T(8,128)(2,1)S(1)}, u32[]{:S(2)}, u32[]{:S(2)}) collective-permute-start(bf16[296,768]{1,0:T(8,128)(2,1)S(1)} %collective-permute-done.refs_1_), channel_id=1, source_target_pairs={{0,8},{4,12},{8,16},{12,20},{16,24},{20,28},{24,0},{28,4},{1,9},{5... | collective-permute-start | bytes 1363976 | tf_op jit(solution)/shard_map/ppermute | solution.py:810
  19.5 14.0 %collective-permute-start.9 = (bf16[296,768]{1,0:T(8,128)(2,1)S(1)}, bf16[296,768]{1,0:T(8,128)(2,1)S(1)}, u32[]{:S(2)}, u32[]{:S(2)}) collective-permute-start(bf16[296,768]{1,0:T(8,128)(2,1)S(1)} %collective-permute-done.3.refs_4_), channel_id=1, source_target_pairs={{0,2},{1,3},{2,0},{3,1},{4,6},{5,7},{6,4},{7,5},{8,10},{9,11},{10,... | collective-permute-start | bytes 1363976 | tf_op jit(solution)/shard_map/ppermute | solution.py:806
  20.5 15.1 %collective-permute-start.4 = (bf16[296,768]{1,0:T(8,128)(2,1)S(1)}, bf16[296,768]{1,0:T(8,128)(2,1)S(1)}, u32[]{:S(2)}, u32[]{:S(2)}) collective-permute-start(bf16[296,768]{1,0:T(8,128)(2,1)S(1)} %collective-permute-done.refs_1_), channel_id=1, source_target_pairs={{0,4},{4,0},{8,12},{12,8},{16,20},{20,16},{24,28},{28,24},{1,5},{5... | collective-permute-start | bytes 1363976 | tf_op jit(solution)/shard_map/ppermute | solution.py:802
  32.2 12.5 %collective-permute-start.2 = (bf16[296,768]{1,0:T(8,128)(2,1)S(1)}, bf16[296,768]{1,0:T(8,128)(2,1)S(1)}, u32[]{:S(2)}, u32[]{:S(2)}) collective-permute-start(bf16[296,768]{1,0:T(8,128)(2,1)S(1)} %collective-permute-done.1.refs_2_), channel_id=1, source_target_pairs={{0,8},{4,12},{8,16},{12,20},{16,24},{20,28},{24,0},{28,4},{1,9},{5... | collective-permute-start | bytes 1363976 | tf_op jit(solution)/shard_map/ppermute | solution.py:810
  32.2 13.6 %collective-permute-start.8 = (bf16[296,768]{1,0:T(8,128)(2,1)S(1)}, bf16[296,768]{1,0:T(8,128)(2,1)S(1)}, u32[]{:S(2)}, u32[]{:S(2)}) collective-permute-start(bf16[296,768]{1,0:T(8,128)(2,1)S(1)} %collective-permute-done.refs_1_), channel_id=1, source_target_pairs={{0,2},{1,3},{2,0},{3,1},{4,6},{5,7},{6,4},{7,5},{8,10},{9,11},{10,... | collective-permute-start | bytes 1363976 | tf_op jit(solution)/shard_map/ppermute | solution.py:806
  33.5 12.3 %collective-permute-start.5 = (bf16[296,768]{1,0:T(8,128)(2,1)S(1)}, bf16[296,768]{1,0:T(8,128)(2,1)S(1)}, u32[]{:S(2)}, u32[]{:S(2)}) collective-permute-start(bf16[296,768]{1,0:T(8,128)(2,1)S(1)} %collective-permute-done.1.refs_2_), channel_id=1, source_target_pairs={{0,4},{4,0},{8,12},{12,8},{16,20},{20,16},{24,28},{28,24},{1,5},{5... | collective-permute-start | bytes 1363976 | tf_op jit(solution)/shard_map/ppermute | solution.py:802
  35.0 17.8 %collective-permute-start.10 = (bf16[296,768]{1,0:T(8,128)(2,1)S(1)}, bf16[296,768]{1,0:T(8,128)(2,1)}, u32[]{:S(2)}, u32[]{:S(2)}) collective-permute-start(bf16[296,768]{1,0:T(8,128)(2,1)S(1)} %collective-permute-done.1.refs_2_), channel_id=1, source_target_pairs={{0,2},{1,3},{2,0},{3,1},{4,6},{5,7},{6,4},{7,5},{8,10},{9,11},{10,... | collective-permute-start | bytes 1363976 | tf_op jit(solution)/shard_map/ppermute | solution.py:806
  45.8 16.7 %collective-permute-start.12 = (bf16[296,768]{1,0:T(8,128)(2,1)S(1)}, bf16[296,768]{1,0:T(8,128)(2,1)}, u32[]{:S(2)}, u32[]{:S(2)}) collective-permute-start(bf16[296,768]{1,0:T(8,128)(2,1)S(1)} %collective-permute-done.9.refs_4_), channel_id=1, source_target_pairs={{0,8},{4,12},{8,16},{12,20},{16,24},{20,28},{24,0},{28,4},{1,9},{5... | collective-permute-start | bytes 1363976 | tf_op jit(solution)/shard_map/ppermute | solution.py:810
  53.9 13.0 %collective-permute-start.11 = (bf16[296,768]{1,0:T(8,128)(2,1)}, bf16[296,768]{1,0:T(8,128)(2,1)}, u32[]{:S(2)}, u32[]{:S(2)}) collective-permute-start(bf16[296,768]{1,0:T(8,128)(2,1)} %collective-permute-done.10.refs_2_), channel_id=1, source_target_pairs={{0,8},{4,12},{8,16},{12,20},{16,24},{20,28},{24,0},{28,4},{1,9},{5... | collective-permute-start | bytes 1363976 | tf_op jit(solution)/shard_map/ppermute | solution.py:810
  74.6 21.1 %collective-permute-start.17 = (bf16[2,1536,768]{2,1,0:T(8,128)(2,1)}, bf16[2,1536,768]{2,1,0:T(8,128)(2,1)}, u32[]{:S(2)}, u32[]{:S(2)}) collective-permute-start(bf16[2,1536,768]{2,1,0:T(8,128)(2,1)} %get-tuple-element.85.up0_ref.down0_ref), channel_id=1, source_target_pairs={{0,1},{1,0},{2,3},{3,2},{4,5},{5,4},{6,7},{7,6},{8,9},{9,8},{10,11... | collective-permute-start | bytes 14155784 | tf_op jit(solution)/shard_map/ppermute | solution.py:818
  125.1 33.5 %collective-permute-start.20 = (bf16[2,1536,768]{2,1,0:T(8,128)(2,1)}, bf16[2,1536,768]{2,1,0:T(8,128)(2,1)}, u32[]{:S(2)}, u32[]{:S(2)}) collective-permute-start(bf16[2,1536,768]{2,1,0:T(8,128)(2,1)} %get-tuple-element.104), channel_id=1, source_target_pairs={{0,1},{1,0},{2,3},{3,2},{4,5},{5,4},{6,7},{7,6},{8,9},{9,8},{10,11... | collective-permute-start | bytes 14155784 | tf_op jit(solution)/shard_map/ppermute | solution.py:818
  162.9 13.0 %collective-permute-start.25 = (bf16[296,768]{1,0:T(8,128)(2,1)}, bf16[296,768]{1,0:T(8,128)(2,1)S(1)}, u32[]{:S(2)}, u32[]{:S(2)}) collective-permute-start(bf16[296,768]{1,0:T(8,128)(2,1)} %get-tuple-element.115), channel_id=1, source_target_pairs={{0,2},{1,3},{2,0},{3,1},{4,6},{5,7},{6,4},{7,5},{8,10},{9,11},{10,... | collective-permute-start | bytes 1363976 | tf_op jit(solution)/shard_map/ppermute | solution.py:806
  164.5 13.9 %collective-permute-start.21 = (bf16[296,768]{1,0:T(8,128)(2,1)}, bf16[296,768]{1,0:T(8,128)(2,1)S(1)}, u32[]{:S(2)}, u32[]{:S(2)}) collective-permute-start(bf16[296,768]{1,0:T(8,128)(2,1)} %get-tuple-element.108), channel_id=1, source_target_pairs={{0,4},{4,0},{8,12},{12,8},{16,20},{20,16},{24,28},{28,24},{1,5},{5... | collective-permute-start | bytes 1363976 | tf_op jit(solution)/shard_map/ppermute | solution.py:802
  165.0 14.2 %collective-permute-start.23 = (bf16[296,768]{1,0:T(8,128)(2,1)}, bf16[296,768]{1,0:T(8,128)(2,1)S(1)}, u32[]{:S(2)}, u32[]{:S(2)}) collective-permute-start(bf16[296,768]{1,0:T(8,128)(2,1)} %get-tuple-element.112), channel_id=1, source_target_pairs={{8,0},{12,4},{16,8},{20,12},{24,16},{28,20},{0,24},{4,28},{9,1},{1... | collective-permute-start | bytes 1363976 | tf_op jit(solution)/shard_map/ppermute | solution.py:814
  177.1 11.9 %collective-permute-start.26 = (bf16[296,768]{1,0:T(8,128)(2,1)S(1)}, bf16[296,768]{1,0:T(8,128)(2,1)S(1)}, u32[]{:S(2)}, u32[]{:S(2)}) collective-permute-start(bf16[296,768]{1,0:T(8,128)(2,1)S(1)} %add_convert_fusion.5), channel_id=1, source_target_pairs={{0,4},{4,0},{8,12},{12,8},{16,20},{20,16},{24,28},{28,24},{1,5},{5... | collective-permute-start | bytes 1363976 | tf_op jit(solution)/shard_map/ppermute | solution.py:802
  178.4 14.4 %collective-permute-start.32 = (bf16[296,768]{1,0:T(8,128)(2,1)}, bf16[296,768]{1,0:T(8,128)(2,1)S(1)}, u32[]{:S(2)}, u32[]{:S(2)}) collective-permute-start(bf16[296,768]{1,0:T(8,128)(2,1)} %get-tuple-element.123), channel_id=1, source_target_pairs={{8,0},{12,4},{16,8},{20,12},{24,16},{28,20},{0,24},{4,28},{9,1},{1... | collective-permute-start | bytes 1363976 | tf_op jit(solution)/shard_map/ppermute | solution.py:814
  179.4 21.8 %collective-permute-start.24 = (bf16[296,768]{1,0:T(8,128)(2,1)S(1)}, bf16[296,768]{1,0:T(8,128)(2,1)S(1)}, u32[]{:S(2)}, u32[]{:S(2)}) collective-permute-start(bf16[296,768]{1,0:T(8,128)(2,1)S(1)} %add_convert_fusion.6), channel_id=1, source_target_pairs={{0,2},{1,3},{2,0},{3,1},{4,6},{5,7},{6,4},{7,5},{8,10},{9,11},{10,... | collective-permute-start | bytes 1363976 | tf_op jit(solution)/shard_map/ppermute | solution.py:806
  191.2 24.1 %collective-permute-start.22 = (bf16[296,768]{1,0:T(8,128)(2,1)S(1)}, bf16[296,768]{1,0:T(8,128)(2,1)S(1)}, u32[]{:S(2)}, u32[]{:S(2)}) collective-permute-start(bf16[296,768]{1,0:T(8,128)(2,1)S(1)} %copy-done.29), channel_id=1, source_target_pairs={{0,2},{1,3},{2,0},{3,1},{4,6},{5,7},{6,4},{7,5},{8,10},{9,11},{10,... | collective-permute-start | bytes 1363976 | tf_op jit(solution)/shard_map/ppermute | solution.py:806
  192.9 21.4 %collective-permute-start.33 = (bf16[296,768]{1,0:T(8,128)(2,1)S(1)}, bf16[296,768]{1,0:T(8,128)(2,1)S(1)}, u32[]{:S(2)}, u32[]{:S(2)}) collective-permute-start(bf16[296,768]{1,0:T(8,128)(2,1)S(1)} %add_convert_fusion.1), channel_id=1, source_target_pairs={{0,2},{1,3},{2,0},{3,1},{4,6},{5,7},{6,4},{7,5},{8,10},{9,11},{10,... | collective-permute-start | bytes 1363976 | tf_op jit(solution)/shard_map/ppermute | solution.py:806
  200.0 15.3 %collective-permute-start.30 = (bf16[296,768]{1,0:T(8,128)(2,1)S(1)}, bf16[296,768]{1,0:T(8,128)(2,1)S(1)}, u32[]{:S(2)}, u32[]{:S(2)}) collective-permute-start(bf16[296,768]{1,0:T(8,128)(2,1)S(1)} %copy-done.28), channel_id=1, source_target_pairs={{0,4},{4,0},{8,12},{12,8},{16,20},{20,16},{24,28},{28,24},{1,5},{5... | collective-permute-start | bytes 1363976 | tf_op jit(solution)/shard_map/ppermute | solution.py:802
  201.5 13.8 %collective-permute-start.29 = (bf16[296,768]{1,0:T(8,128)(2,1)S(1)}, bf16[296,768]{1,0:T(8,128)(2,1)S(1)}, u32[]{:S(2)}, u32[]{:S(2)}) collective-permute-start(bf16[296,768]{1,0:T(8,128)(2,1)S(1)} %add_convert_fusion.3), channel_id=1, source_target_pairs={{8,0},{12,4},{16,8},{20,12},{24,16},{28,20},{0,24},{4,28},{9,1},{1... | collective-permute-start | bytes 1363976 | tf_op jit(solution)/shard_map/ppermute | solution.py:814
  204.1 17.1 %collective-permute-start.35 = (bf16[296,768]{1,0:T(8,128)(2,1)S(1)}, bf16[296,768]{1,0:T(8,128)(2,1)S(1)}, u32[]{:S(2)}, u32[]{:S(2)}) collective-permute-start(bf16[296,768]{1,0:T(8,128)(2,1)S(1)} %copy-done.27), channel_id=1, source_target_pairs={{0,2},{1,3},{2,0},{3,1},{4,6},{5,7},{6,4},{7,5},{8,10},{9,11},{10,... | collective-permute-start | bytes 1363976 | tf_op jit(solution)/shard_map/ppermute | solution.py:806
  (43 other events, 653.1 us)

commit v7 on v6

--- a/solution.py
+++ b/solution.py
@@ -883,7 +883,7 @@
     y2 = swap_y(add_low(a["Y2"], z1, x1))
     x3 = swap_x(after(a["X2"], x2))
     z3 = ring_back(add_low(a["R3"], x2))
-    x4 = swap_x(after(a["X1"], x3))
+    x4 = swap_x(after(a["X1"], x2))
     y4 = swap_y(add_low(a["D0"], z2))
     z4 = ring_back(add_low(a["R2"], y2, z3, x3))
     y5 = swap_y(after(a["Y0"], y2))

time: 228 us -> 228 us (level)
  no operation moved by 1% of the time
where the time goes in v7:
time: 228 us
  Pallas kernels  104 us (46%)
  waiting for transfers between devices  81.8 us (36%)
  starting transfers between devices  33.2 us (15%)
  local copies, waits for them, and re-layouts  3.86 us (2%)
  other arithmetic  3.6 us (2%)
    pallas_call x9, Pallas kernels, call(): pl.pallas_call(kernel, grid_spec=pltpu.PrefetchScalarGridSpec(num_scalar_...  104 us
    ppermute x5, waiting for transfers between devices, ring_z(): return lax.ppermute(a, 'wide', Z_RING)  31.3 us
    ppermute x10, waiting for transfers between devices, swap_x(): return lax.ppermute(a, 'wide', X_SWAP)  22.8 us
    ppermute x10, waiting for transfers between devices, swap_y(): return lax.ppermute(a, 'narrow', Y_SWAP)  20.8 us
    ppermute x10, starting transfers between devices, swap_y(): return lax.ppermute(a, 'narrow', Y_SWAP)  11.9 us
    ppermute x10, starting transfers between devices, swap_x(): return lax.ppermute(a, 'wide', X_SWAP)  11.2 us
    ppermute x6, waiting for transfers between devices, swap_core(): return lax.ppermute(a, 'narrow', CORE_SWAP)  5.75 us
    ppermute x5, starting transfers between devices, ring_back(): return lax.ppermute(a, 'wide', [(j, i) for i, j in Z_RING])  5.7 us
  transfers between devices with their start and end apart: 36, of which 17 were waited for; matrix products, arithmetic and copies ran while one was open for 1% of the time, Pallas kernels for 31%

profile of v7, /device:TPU:0, one launch (start us, length us, event | category | flops | bytes accessed | tf_op | source)
XLA Modules:
  0.0 227.7 jit_solution(14643143293662859341)
XLA Ops:
  3.3 3.1 %collective-permute-start = (bf16[296,768]{1,0:T(8,128)(2,1)S(1)}, bf16[296,768]{1,0:T(8,128)(2,1)S(1)}, u32[]{:S(2)}, u32[]{:S(2)}) collective-permute-start(bf16[296,768]{1,0:T(8,128)(2,1)S(1)} %own_block.1.refs_0_), channel_id=1, source_target_pairs={{0,8},{4,12},{8,16},{12,20},{16,24},{20,28},{24,0},{28,4},{1,9},{5... | collective-permute-start | bytes 1363976 | tf_op jit(solution)/shard_map/ppermute | solution.py:810
  9.4 9.4 %collective-permute-done.refs_1_ = bf16[296,768]{1,0:T(8,128)(2,1)S(1)} collective-permute-done((bf16[296,768]{1,0:T(8,128)(2,1)S(1)}, bf16[296,768]{1,0:T(8,128)(2,1)S(1)}, u32[]{:S(2)}, u32[]{:S(2)}) %collective-permute-start) | collective-permute-done | bytes 454688 | tf_op jit(solution)/shard_map/ppermute | solution.py:810
  21.9 10.3 %collective-permute-done.1.refs_2_ = bf16[296,768]{1,0:T(8,128)(2,1)S(1)} collective-permute-done((bf16[296,768]{1,0:T(8,128)(2,1)S(1)}, bf16[296,768]{1,0:T(8,128)(2,1)S(1)}, u32[]{:S(2)}, u32[]{:S(2)}) %collective-permute-start.1) | collective-permute-done | bytes 454688 | tf_op jit(solution)/shard_map/ppermute | solution.py:810
  35.5 9.2 %collective-permute-done.2.refs_3_ = bf16[296,768]{1,0:T(8,128)(2,1)S(1)} collective-permute-done((bf16[296,768]{1,0:T(8,128)(2,1)S(1)}, bf16[296,768]{1,0:T(8,128)(2,1)S(1)}, u32[]{:S(2)}, u32[]{:S(2)}) %collective-permute-start.2) | collective-permute-done | bytes 454688 | tf_op jit(solution)/shard_map/ppermute | solution.py:810
  45.8 7.0 %collective-permute-done.10.refs_2_ = bf16[296,768]{1,0:T(8,128)(2,1)} collective-permute-done((bf16[296,768]{1,0:T(8,128)(2,1)S(1)}, bf16[296,768]{1,0:T(8,128)(2,1)}, u32[]{:S(2)}, u32[]{:S(2)}) %collective-permute-start.10) | collective-permute-done | bytes 454688 | tf_op jit(solution)/shard_map/ppermute | solution.py:806
  53.9 2.4 %collective-permute-done.6.refs_7_ = bf16[296,768]{1,0:T(8,128)(2,1)} collective-permute-done((bf16[296,768]{1,0:T(8,128)(2,1)S(1)}, bf16[296,768]{1,0:T(8,128)(2,1)}, u32[]{:S(2)}, u32[]{:S(2)}) %collective-permute-start.6) | collective-permute-done | bytes 454688 | tf_op jit(solution)/shard_map/ppermute | solution.py:802
  57.7 4.7 %merge_weights.2 = (bf16[776,768]{1,0:T(8,128)(2,1)}, bf16[2,1536,768]{2,1,0:T(8,128)(2,1)}) custom-call(s32[8]{0:T(128)} %pad_add_fusion.1.at_ref, bf16[296,768]{1,0:T(8,128)(2,1)} %copy-done.2, bf16[296,768]{1,0:T(8,128)(2,1)} %copy-done.13, bf16[296,768]{1,0:T(8,128)(2,1)} %copy-done.16, bf16[296,768]{1,0:T(8,128)(2,1)} %copy-done.19, ...), custom_call_target="tpu_custom_call" | custom-call | tf_op jit(solution)/shard_map/merge_weights/pallas_call | solution.py:106
  62.5 2.0 collective-permute-done.13.refs_6_
  64.5 2.3 %collective-permute-done.11.refs_3_ = bf16[296,768]{1,0:T(8,128)(2,1)} collective-permute-done((bf16[296,768]{1,0:T(8,128)(2,1)}, bf16[296,768]{1,0:T(8,128)(2,1)}, u32[]{:S(2)}, u32[]{:S(2)}) %collective-permute-start.11) | collective-permute-done | bytes 454688 | tf_op jit(solution)/shard_map/ppermute | solution.py:810
  66.8 4.6 %merge_weights.3 = (bf16[776,768]{1,0:T(8,128)(2,1)}, bf16[2,1536,768]{2,1,0:T(8,128)(2,1)}) custom-call(s32[8]{0:T(128)} %pad_add_fusion.1.at_ref, bf16[296,768]{1,0:T(8,128)(2,1)} %copy-done.11, bf16[296,768]{1,0:T(8,128)(2,1)} %copy-done.15, bf16[296,768]{1,0:T(8,128)(2,1)} %collective-permute-done.10.refs_2_, ...), custom_call_target="tpu_custom_call", output_to_operand_aliasing={{1}: (9, {})} | custom-call | tf_op jit(solution)/shard_map/merge_weights/pallas_call | solution.py:106
  71.6 3.0 %collective-permute-done.16.att3_ref = bf16[776,768]{1,0:T(8,128)(2,1)S(1)} collective-permute-done((bf16[776,768]{1,0:T(8,128)(2,1)}, bf16[776,768]{1,0:T(8,128)(2,1)S(1)}, u32[]{:S(2)}, u32[]{:S(2)}) %collective-permute-start.16) | collective-permute-done | bytes 1191968 | tf_op jit(solution)/shard_map/ppermute | solution.py:818
  75.7 20.1 %attention_forward.1 = (bf16[4,512,576]{2,1,0:T(8,128)(2,1)}, bf16[4,768,576]{2,1,0:T(8,128)(2,1)}, bf16[4,512,192]{2,1,0:T(8,128)(2,1)}, bf16[4,3,512,512]{3,2,...) custom-call(s32[7]{0:T(128)} %copy-done.6, ...), custom_call_target="tpu_custom_call" | custom-call | flops 6000000000 | bytes 24000000 | tf_op jit(solution)/shard_map/attention_forward/pallas_call | solution.py:106
  95.7 29.4 %feed_forward.1 = (bf16[512,768]{1,0:T(8,128)(2,1)}, bf16[2,1536,768]{2,1,0:T(8,128)(2,1)}, bf16[2,1536,768]{2,1,0:T(8,128)(2,1)}, f32[512,768]{1,0:T(8,128)}, b...) custom-call(s32[7]{0:T(128)} %copy-done.6, f32[512,768]{1,0:T(8,128)} %get-tuple-element.82.n1_ref, ...), custom_call_target="tpu_custom_call" | custom-call | flops 14499999744 | bytes 36000000 | tf_op jit(solution)/shard_map/feed_forward/pallas_call | solution.py:106
  125.3 29.8 %attention_backward.1 = (bf16[776,768]{1,0:T(8,128)(2,1)}, bf16[776,768]{1,0:T(8,128)(2,1)}, bf16[776,768]{1,0:T(8,128)(2,1)}, bf16[776,768]{1,0:T(8,128)(2,1)}, f32[512,768]{1,0:T(8,128)}) custom-call(s32[7]{0:T(128)} %copy-done.6, bf16[512,768]{1,0:T(8,128)(2,1)} %get-tuple-element.88.ga_ref, bf16[776,768]{1,0:T(8,128)(2,1)} %get-tuple-element.72.att0_ref, ...), custom_call_target="tpu_custom_call" | custom-call | flops 12000000000 | bytes 30000000 | tf_op jit(solution)/shard_map/attention_backward/pallas_call | solution.py:106
  155.6 2.7 %collective-permute-done.18.refs_4_.refs_3_ = bf16[776,768]{1,0:T(8,128)(2,1)S(1)} collective-permute-done((bf16[776,768]{1,0:T(8,128)(2,1)}, bf16[776,768]{1,0:T(8,128)(2,1)S(1)}, u32[]{:S(2)}, u32[]{:S(2)}) %collective-permute-start.18) | collective-permute-done | bytes 1191968 | tf_op jit(solution)/shard_map/ppermute | solution.py:818
  159.3 3.5 %split_windows.3 = (bf16[296,768]{1,0:T(8,128)(2,1)}, bf16[296,768]{1,0:T(8,128)(2,1)}, bf16[296,768]{1,0:T(8,128)(2,1)}) custom-call(s32[8]{0:T(128)} %pad_add_fusion.1.at_ref, bf16[776,768]{1,0:T(8,128)(2,1)} %get-tuple-element.99.refs_1_.refs_0_, bf16[776,768]{1,0:T(8,128)(2,1)} %get-tuple-element.99.refs_1_.refs_0_, ...), custom_call_target="tpu_custom_call" | custom-call | tf_op jit(solution)/shard_map/split_windows/pallas_call | solution.py:106
  167.5 7.8 %split_windows.2 = (bf16[296,768]{1,0:T(8,128)(2,1)}, bf16[296,768]{1,0:T(8,128)(2,1)}, bf16[296,768]{1,0:T(8,128)(2,1)}, bf16[296,768]{1,0:T(8,128)(2,1)}, bf16...) custom-call(s32[8]{0:T(128)} %pad_add_fusion.1.at_ref, ...), custom_call_target="tpu_custom_call" | custom-call | tf_op jit(solution)/shard_map/split_windows/pallas_call | solution.py:106
  179.4 1.6 collective-permute-start.24
  181.0 8.0 %collective-permute-done.26 = bf16[296,768]{1,0:T(8,128)(2,1)S(1)} collective-permute-done((bf16[296,768]{1,0:T(8,128)(2,1)S(1)}, bf16[296,768]{1,0:T(8,128)(2,1)S(1)}, u32[]{:S(2)}, u32[]{:S(2)}) %collective-permute-start.26) | collective-permute-done | bytes 454688 | tf_op jit(solution)/shard_map/ppermute | solution.py:802
  194.2 8.1 %collective-permute-done.28 = bf16[296,768]{1,0:T(8,128)(2,1)S(1)} collective-permute-done((bf16[296,768]{1,0:T(8,128)(2,1)S(1)}, bf16[296,768]{1,0:T(8,128)(2,1)S(1)}, u32[]{:S(2)}, u32[]{:S(2)}) %collective-permute-start.28) | collective-permute-done | bytes 454688 | tf_op jit(solution)/shard_map/ppermute | solution.py:802
  205.6 8.7 %collective-permute-done.33 = bf16[296,768]{1,0:T(8,128)(2,1)S(1)} collective-permute-done((bf16[296,768]{1,0:T(8,128)(2,1)S(1)}, bf16[296,768]{1,0:T(8,128)(2,1)S(1)}, u32[]{:S(2)}, u32[]{:S(2)}) %collective-permute-start.33) | collective-permute-done | bytes 454688 | tf_op jit(solution)/shard_map/ppermute | solution.py:806
  216.6 4.6 %collective-permute-done.35.ring_ref = bf16[296,768]{1,0:T(8,128)(2,1)S(1)} collective-permute-done((bf16[296,768]{1,0:T(8,128)(2,1)S(1)}, bf16[296,768]{1,0:T(8,128)(2,1)S(1)}, u32[]{:S(2)}, u32[]{:S(2)}) %collective-permute-start.35) | collective-permute-done | bytes 454688 | tf_op jit(solution)/shard_map/ppermute | solution.py:806
  221.1 1.8 collective-permute-done.34.second_ref
  224.1 3.6 %update_shard.1 = (f32[1,221568]{1,0:T(1,128)}, f32[1,221568]{1,0:T(1,128)}, f32[1,221568]{1,0:T(1,128)}, f32[1,221568]{1,0:T(1,128)}, bf16[1,221568]{1,0:T(2,128)(2,1)}) custom-call(s32[7]{0:T(128)S(1)} %copy-done.7, bf16[296,768]{1,0:T(8,128)(2,1)S(1)} %copy-done.5, bf16[296,768]{1,0:T(8,128)(2,1)S(1)} %collective-permute-done.31.near_ref, ...), custom_call_target="tpu_custom_call" | custom-call | tf_op jit(solution)/shard_map/update_shard/pallas_call | solution.py:106
  (129 shorter events, 39.0 us)
Async XLA Ops:
  3.3 15.6 %collective-permute-start = (bf16[296,768]{1,0:T(8,128)(2,1)S(1)}, bf16[296,768]{1,0:T(8,128)(2,1)S(1)}, u32[]{:S(2)}, u32[]{:S(2)}) collective-permute-start(bf16[296,768]{1,0:T(8,128)(2,1)S(1)} %own_block.1.refs_0_), channel_id=1, source_target_pairs={{0,8},{4,12},{8,16},{12,20},{16,24},{20,28},{24,0},{28,4},{1,9},{5... | collective-permute-start | bytes 1363976 | tf_op jit(solution)/shard_map/ppermute | solution.py:810
  6.4 12.5 %collective-permute-start.7 = (bf16[296,768]{1,0:T(8,128)(2,1)S(1)}, bf16[296,768]{1,0:T(8,128)(2,1)S(1)}, u32[]{:S(2)}, u32[]{:S(2)}) collective-permute-start(bf16[296,768]{1,0:T(8,128)(2,1)S(1)} %own_block.1.refs_0_), channel_id=1, source_target_pairs={{0,2},{1,3},{2,0},{3,1},{4,6},{5,7},{6,4},{7,5},{8,10},{9,11},{10,... | collective-permute-start | bytes 1363976 | tf_op jit(solution)/shard_map/ppermute | solution.py:806
  18.8 13.4 %collective-permute-start.1 = (bf16[296,768]{1,0:T(8,128)(2,1)S(1)}, bf16[296,768]{1,0:T(8,128)(2,1)S(1)}, u32[]{:S(2)}, u32[]{:S(2)}) collective-permute-start(bf16[296,768]{1,0:T(8,128)(2,1)S(1)} %collective-permute-done.refs_1_), channel_id=1, source_target_pairs={{0,8},{4,12},{8,16},{12,20},{16,24},{20,28},{24,0},{28,4},{1,9},{5... | collective-permute-start | bytes 1363976 | tf_op jit(solution)/shard_map/ppermute | solution.py:810
  19.5 14.0 %collective-permute-start.9 = (bf16[296,768]{1,0:T(8,128)(2,1)S(1)}, bf16[296,768]{1,0:T(8,128)(2,1)S(1)}, u32[]{:S(2)}, u32[]{:S(2)}) collective-permute-start(bf16[296,768]{1,0:T(8,128)(2,1)S(1)} %collective-permute-done.3.refs_4_), channel_id=1, source_target_pairs={{0,2},{1,3},{2,0},{3,1},{4,6},{5,7},{6,4},{7,5},{8,10},{9,11},{10,... | collective-permute-start | bytes 1363976 | tf_op jit(solution)/shard_map/ppermute | solution.py:806
  20.5 15.1 %collective-permute-start.4 = (bf16[296,768]{1,0:T(8,128)(2,1)S(1)}, bf16[296,768]{1,0:T(8,128)(2,1)S(1)}, u32[]{:S(2)}, u32[]{:S(2)}) collective-permute-start(bf16[296,768]{1,0:T(8,128)(2,1)S(1)} %collective-permute-done.refs_1_), channel_id=1, source_target_pairs={{0,4},{4,0},{8,12},{12,8},{16,20},{20,16},{24,28},{28,24},{1,5},{5... | collective-permute-start | bytes 1363976 | tf_op jit(solution)/shard_map/ppermute | solution.py:802
  32.2 12.5 %collective-permute-start.2 = (bf16[296,768]{1,0:T(8,128)(2,1)S(1)}, bf16[296,768]{1,0:T(8,128)(2,1)S(1)}, u32[]{:S(2)}, u32[]{:S(2)}) collective-permute-start(bf16[296,768]{1,0:T(8,128)(2,1)S(1)} %collective-permute-done.1.refs_2_), channel_id=1, source_target_pairs={{0,8},{4,12},{8,16},{12,20},{16,24},{20,28},{24,0},{28,4},{1,9},{5... | collective-permute-start | bytes 1363976 | tf_op jit(solution)/shard_map/ppermute | solution.py:810
  32.2 13.6 %collective-permute-start.8 = (bf16[296,768]{1,0:T(8,128)(2,1)S(1)}, bf16[296,768]{1,0:T(8,128)(2,1)S(1)}, u32[]{:S(2)}, u32[]{:S(2)}) collective-permute-start(bf16[296,768]{1,0:T(8,128)(2,1)S(1)} %collective-permute-done.refs_1_), channel_id=1, source_target_pairs={{0,2},{1,3},{2,0},{3,1},{4,6},{5,7},{6,4},{7,5},{8,10},{9,11},{10,... | collective-permute-start | bytes 1363976 | tf_op jit(solution)/shard_map/ppermute | solution.py:806
  33.5 12.3 %collective-permute-start.5 = (bf16[296,768]{1,0:T(8,128)(2,1)S(1)}, bf16[296,768]{1,0:T(8,128)(2,1)S(1)}, u32[]{:S(2)}, u32[]{:S(2)}) collective-permute-start(bf16[296,768]{1,0:T(8,128)(2,1)S(1)} %collective-permute-done.1.refs_2_), channel_id=1, source_target_pairs={{0,4},{4,0},{8,12},{12,8},{16,20},{20,16},{24,28},{28,24},{1,5},{5... | collective-permute-start | bytes 1363976 | tf_op jit(solution)/shard_map/ppermute | solution.py:802
  35.0 17.8 %collective-permute-start.10 = (bf16[296,768]{1,0:T(8,128)(2,1)S(1)}, bf16[296,768]{1,0:T(8,128)(2,1)}, u32[]{:S(2)}, u32[]{:S(2)}) collective-permute-start(bf16[296,768]{1,0:T(8,128)(2,1)S(1)} %collective-permute-done.1.refs_2_), channel_id=1, source_target_pairs={{0,2},{1,3},{2,0},{3,1},{4,6},{5,7},{6,4},{7,5},{8,10},{9,11},{10,... | collective-permute-start | bytes 1363976 | tf_op jit(solution)/shard_map/ppermute | solution.py:806
  45.8 16.7 %collective-permute-start.12 = (bf16[296,768]{1,0:T(8,128)(2,1)S(1)}, bf16[296,768]{1,0:T(8,128)(2,1)}, u32[]{:S(2)}, u32[]{:S(2)}) collective-permute-start(bf16[296,768]{1,0:T(8,128)(2,1)S(1)} %collective-permute-done.9.refs_4_), channel_id=1, source_target_pairs={{0,8},{4,12},{8,16},{12,20},{16,24},{20,28},{24,0},{28,4},{1,9},{5... | collective-permute-start | bytes 1363976 | tf_op jit(solution)/shard_map/ppermute | solution.py:810
  53.9 13.0 %collective-permute-start.11 = (bf16[296,768]{1,0:T(8,128)(2,1)}, bf16[296,768]{1,0:T(8,128)(2,1)}, u32[]{:S(2)}, u32[]{:S(2)}) collective-permute-start(bf16[296,768]{1,0:T(8,128)(2,1)} %collective-permute-done.10.refs_2_), channel_id=1, source_target_pairs={{0,8},{4,12},{8,16},{12,20},{16,24},{20,28},{24,0},{28,4},{1,9},{5... | collective-permute-start | bytes 1363976 | tf_op jit(solution)/shard_map/ppermute | solution.py:810
  74.6 21.1 %collective-permute-start.17 = (bf16[2,1536,768]{2,1,0:T(8,128)(2,1)}, bf16[2,1536,768]{2,1,0:T(8,128)(2,1)}, u32[]{:S(2)}, u32[]{:S(2)}) collective-permute-start(bf16[2,1536,768]{2,1,0:T(8,128)(2,1)} %get-tuple-element.85.up0_ref.down0_ref), channel_id=1, source_target_pairs={{0,1},{1,0},{2,3},{3,2},{4,5},{5,4},{6,7},{7,6},{8,9},{9,8},{10,11... | collective-permute-start | bytes 14155784 | tf_op jit(solution)/shard_map/ppermute | solution.py:818
  125.1 33.5 %collective-permute-start.20 = (bf16[2,1536,768]{2,1,0:T(8,128)(2,1)}, bf16[2,1536,768]{2,1,0:T(8,128)(2,1)}, u32[]{:S(2)}, u32[]{:S(2)}) collective-permute-start(bf16[2,1536,768]{2,1,0:T(8,128)(2,1)} %get-tuple-element.104), channel_id=1, source_target_pairs={{0,1},{1,0},{2,3},{3,2},{4,5},{5,4},{6,7},{7,6},{8,9},{9,8},{10,11... | collective-permute-start | bytes 14155784 | tf_op jit(solution)/shard_map/ppermute | solution.py:818
  162.9 13.0 %collective-permute-start.25 = (bf16[296,768]{1,0:T(8,128)(2,1)}, bf16[296,768]{1,0:T(8,128)(2,1)S(1)}, u32[]{:S(2)}, u32[]{:S(2)}) collective-permute-start(bf16[296,768]{1,0:T(8,128)(2,1)} %get-tuple-element.115), channel_id=1, source_target_pairs={{0,2},{1,3},{2,0},{3,1},{4,6},{5,7},{6,4},{7,5},{8,10},{9,11},{10,... | collective-permute-start | bytes 1363976 | tf_op jit(solution)/shard_map/ppermute | solution.py:806
  164.5 13.9 %collective-permute-start.21 = (bf16[296,768]{1,0:T(8,128)(2,1)}, bf16[296,768]{1,0:T(8,128)(2,1)S(1)}, u32[]{:S(2)}, u32[]{:S(2)}) collective-permute-start(bf16[296,768]{1,0:T(8,128)(2,1)} %get-tuple-element.108), channel_id=1, source_target_pairs={{0,4},{4,0},{8,12},{12,8},{16,20},{20,16},{24,28},{28,24},{1,5},{5... | collective-permute-start | bytes 1363976 | tf_op jit(solution)/shard_map/ppermute | solution.py:802
  165.0 14.2 %collective-permute-start.23 = (bf16[296,768]{1,0:T(8,128)(2,1)}, bf16[296,768]{1,0:T(8,128)(2,1)S(1)}, u32[]{:S(2)}, u32[]{:S(2)}) collective-permute-start(bf16[296,768]{1,0:T(8,128)(2,1)} %get-tuple-element.112), channel_id=1, source_target_pairs={{8,0},{12,4},{16,8},{20,12},{24,16},{28,20},{0,24},{4,28},{9,1},{1... | collective-permute-start | bytes 1363976 | tf_op jit(solution)/shard_map/ppermute | solution.py:814
  178.4 14.4 %collective-permute-start.32 = (bf16[296,768]{1,0:T(8,128)(2,1)}, bf16[296,768]{1,0:T(8,128)(2,1)S(1)}, u32[]{:S(2)}, u32[]{:S(2)}) collective-permute-start(bf16[296,768]{1,0:T(8,128)(2,1)} %get-tuple-element.123), channel_id=1, source_target_pairs={{8,0},{12,4},{16,8},{20,12},{24,16},{28,20},{0,24},{4,28},{9,1},{1... | collective-permute-start | bytes 1363976 | tf_op jit(solution)/shard_map/ppermute | solution.py:814
  179.4 14.0 %collective-permute-start.24 = (bf16[296,768]{1,0:T(8,128)(2,1)S(1)}, bf16[296,768]{1,0:T(8,128)(2,1)S(1)}, u32[]{:S(2)}, u32[]{:S(2)}) collective-permute-start(bf16[296,768]{1,0:T(8,128)(2,1)S(1)} %add_convert_fusion.6), channel_id=1, source_target_pairs={{0,2},{1,3},{2,0},{3,1},{4,6},{5,7},{6,4},{7,5},{8,10},{9,11},{10,... | collective-permute-start | bytes 1363976 | tf_op jit(solution)/shard_map/ppermute | solution.py:806
  189.0 13.3 %collective-permute-start.28 = (bf16[296,768]{1,0:T(8,128)(2,1)S(1)}, bf16[296,768]{1,0:T(8,128)(2,1)S(1)}, u32[]{:S(2)}, u32[]{:S(2)}) collective-permute-start(bf16[296,768]{1,0:T(8,128)(2,1)S(1)} %copy-done.30), channel_id=1, source_target_pairs={{0,4},{4,0},{8,12},{12,8},{16,20},{20,16},{24,28},{28,24},{1,5},{5... | collective-permute-start | bytes 1363976 | tf_op jit(solution)/shard_map/ppermute | solution.py:802
  191.2 24.1 %collective-permute-start.22 = (bf16[296,768]{1,0:T(8,128)(2,1)S(1)}, bf16[296,768]{1,0:T(8,128)(2,1)S(1)}, u32[]{:S(2)}, u32[]{:S(2)}) collective-permute-start(bf16[296,768]{1,0:T(8,128)(2,1)S(1)} %copy-done.29), channel_id=1, source_target_pairs={{0,2},{1,3},{2,0},{3,1},{4,6},{5,7},{6,4},{7,5},{8,10},{9,11},{10,... | collective-permute-start | bytes 1363976 | tf_op jit(solution)/shard_map/ppermute | solution.py:806
  192.9 21.4 %collective-permute-start.33 = (bf16[296,768]{1,0:T(8,128)(2,1)S(1)}, bf16[296,768]{1,0:T(8,128)(2,1)S(1)}, u32[]{:S(2)}, u32[]{:S(2)}) collective-permute-start(bf16[296,768]{1,0:T(8,128)(2,1)S(1)} %add_convert_fusion.1), channel_id=1, source_target_pairs={{0,2},{1,3},{2,0},{3,1},{4,6},{5,7},{6,4},{7,5},{8,10},{9,11},{10,... | collective-permute-start | bytes 1363976 | tf_op jit(solution)/shard_map/ppermute | solution.py:806
  193.5 21.8 %collective-permute-start.30 = (bf16[296,768]{1,0:T(8,128)(2,1)S(1)}, bf16[296,768]{1,0:T(8,128)(2,1)S(1)}, u32[]{:S(2)}, u32[]{:S(2)}) collective-permute-start(bf16[296,768]{1,0:T(8,128)(2,1)S(1)} %copy-done.28), channel_id=1, source_target_pairs={{0,4},{4,0},{8,12},{12,8},{16,20},{20,16},{24,28},{28,24},{1,5},{5... | collective-permute-start | bytes 1363976 | tf_op jit(solution)/shard_map/ppermute | solution.py:802
  202.6 12.7 %collective-permute-start.29 = (bf16[296,768]{1,0:T(8,128)(2,1)S(1)}, bf16[296,768]{1,0:T(8,128)(2,1)S(1)}, u32[]{:S(2)}, u32[]{:S(2)}) collective-permute-start(bf16[296,768]{1,0:T(8,128)(2,1)S(1)} %add_convert_fusion.3), channel_id=1, source_target_pairs={{8,0},{12,4},{16,8},{20,12},{24,16},{28,20},{0,24},{4,28},{9,1},{1... | collective-permute-start | bytes 1363976 | tf_op jit(solution)/shard_map/ppermute | solution.py:814
  204.1 17.1 %collective-permute-start.35 = (bf16[296,768]{1,0:T(8,128)(2,1)S(1)}, bf16[296,768]{1,0:T(8,128)(2,1)S(1)}, u32[]{:S(2)}, u32[]{:S(2)}) collective-permute-start(bf16[296,768]{1,0:T(8,128)(2,1)S(1)} %copy-done.27), channel_id=1, source_target_pairs={{0,2},{1,3},{2,0},{3,1},{4,6},{5,7},{6,4},{7,5},{8,10},{9,11},{10,... | collective-permute-start | bytes 1363976 | tf_op jit(solution)/shard_map/ppermute | solution.py:806
  (43 other events, 648.6 us)
